TPU v7x, 256 devices: a whole 4x4x8 slice. The times are simulated.
256 devices in a mesh: expert: 64 (over z, x, core), dp: 4 (over y).
Axes of the slice: x: 4, y: 4, z: 8, core: 2. Of those that a mesh axis runs over, the one named last changes fastest.
Arguments:
- tokens: bfloat16 [32768, 2048], P(('expert', 'dp')), may hold values from -6 to 6
- cotangent: bfloat16 [32768, 2048], P(('expert', 'dp')), may hold values from -6 to 6
- expert_ids: int32 [32768, 4], P(('expert', 'dp')), may hold values from 0 to 63, all different within a row; in each aligned block of 128 rows (0 to 127, 128 to 255, ...) at most 9 rows name the same one
- gate_probs: float32 [32768, 4], P(('expert', 'dp')), may hold values from 0.05 to 1
- w_gate: bfloat16 [64, 2048, 768], P('expert', 'dp'), may hold values from -0.125 to 0.125
- w_up: bfloat16 [64, 2048, 768], P('expert', 'dp'), may hold values from -0.125 to 0.125
- w_down: bfloat16 [64, 768, 2048], P('expert', 'dp'), may hold values from -0.21875 to 0.21875
Outputs:
- grad_tokens: bfloat16 [32768, 2048], P(('expert', 'dp'))
- grad_gate: bfloat16 [64, 2048, 768], P('expert', 'dp')
- grad_up: bfloat16 [64, 2048, 768], P('expert', 'dp')
- grad_down: bfloat16 [64, 768, 2048], P('expert', 'dp')
Inputs may be any that keep to these rules, and one draw needn't show every extreme that they name: `expert_ids`: the 4 experts of a token differ. Among the rows of one device no expert is named more than 9 times, a bound that some block reaches.
All inputs are finite; a program needn't handle non-finite values.
Results may differ from a plain program's by a relative error of at most 0.0064.
Values may be sent and summed in bfloat16 or wider, within the bound.
A program may use at most 128 MiB of HBM per device.

v0:
```python
import jax
import jax.numpy as jnp
from jax import lax
from jax.sharding import PartitionSpec as P


def silu_parts(pre_gate):
    sigma = jax.nn.sigmoid(pre_gate)
    return (pre_gate * sigma, sigma * (1.0 + pre_gate * (1.0 - sigma)))


def shards(tokens, cotangent, expert_ids, gate_probs, w_gate, w_up, w_down):
    tok_rows, top_count = expert_ids.shape
    width = tokens.shape[1]
    owners = lax.axis_size("expert")
    slot_cap = (tok_rows * top_count * 9 + 8 * owners - 1) // (8 * owners)
    entries = tok_rows * top_count
    flat_ids = expert_ids.reshape(-1)
    one_hot = (flat_ids[:, None] == jnp.arange(owners, dtype=jnp.int32)[None, :]).astype(jnp.int32)
    ranks = jnp.sum((jnp.cumsum(one_hot, axis=0) - 1) * one_hot, axis=1)
    slots = flat_ids * slot_cap + ranks
    source = (
        jnp.zeros((owners * slot_cap,), jnp.int32)
        .at[slots]
        .set(jnp.arange(entries, dtype=jnp.int32) // top_count)
    )
    filled = jnp.zeros((owners * slot_cap,), jnp.bool_).at[slots].set(True)
    slot_probs = jnp.zeros((owners * slot_cap,), jnp.float32).at[slots].set(gate_probs.reshape(-1))
    send_rows = jnp.where(filled[:, None], tokens[source], jnp.zeros((), jnp.bfloat16)).reshape(
        owners, slot_cap, width
    )
    send_cot = (
        (slot_probs[:, None] * cotangent[source].astype(jnp.float32))
        .astype(jnp.bfloat16)
        .reshape(owners, slot_cap, width)
    )
    full_gate, full_up, full_down = (
        lax.all_gather(w_gate, "dp", axis=1, tiled=True),
        lax.all_gather(w_up, "dp", axis=1, tiled=True),
        lax.all_gather(w_down, "dp", axis=1, tiled=True),
    )
    gate_full = full_gate[0]
    up_full = full_up[0]
    down_full = full_down[0]
    got_rows, got_cot = (
        lax.all_to_all(send_rows, "expert", split_axis=0, concat_axis=0, tiled=True),
        lax.all_to_all(send_cot, "expert", split_axis=0, concat_axis=0, tiled=True),
    )
    rows = got_rows.reshape(-1, width)
    pre_gate = jnp.dot(rows, gate_full, preferred_element_type=jnp.float32)
    pre_up = jnp.dot(rows, up_full, preferred_element_type=jnp.float32)
    pre_gate, pre_up = (pre_gate, pre_up)
    scaled = got_cot.reshape(-1, width)
    act_value, act_slope = silu_parts(pre_gate)
    activ = (act_value * pre_up).astype(jnp.bfloat16)
    grad_act = jnp.dot(scaled, down_full.T, preferred_element_type=jnp.float32)
    grad_pre_gate = (grad_act * pre_up * act_slope).astype(jnp.bfloat16)
    grad_pre_up = (grad_act * act_value).astype(jnp.bfloat16)
    slot_grad = jnp.dot(grad_pre_gate, gate_full.T, preferred_element_type=jnp.float32)
    slot_grad = (
        slot_grad + jnp.dot(grad_pre_up, up_full.T, preferred_element_type=jnp.float32)
    ).astype(jnp.bfloat16)
    returned = lax.all_to_all(
        slot_grad.reshape(owners, slot_cap, width),
        "expert",
        split_axis=0,
        concat_axis=0,
        tiled=True,
    ).reshape(-1, width)
    per_entry = returned[slots].astype(jnp.float32).reshape(tok_rows, top_count, width)
    grad_tokens = jnp.sum(per_entry, axis=1).astype(jnp.bfloat16)
    part_gate = jnp.dot(rows.T, grad_pre_gate, preferred_element_type=jnp.float32)
    part_up = jnp.dot(rows.T, grad_pre_up, preferred_element_type=jnp.float32)
    part_down = jnp.dot(activ.T, scaled, preferred_element_type=jnp.float32)
    sum_gate, sum_up, sum_down = (
        lax.psum_scatter(part_gate, "dp", scatter_dimension=0, tiled=True),
        lax.psum_scatter(part_up, "dp", scatter_dimension=0, tiled=True),
        lax.psum_scatter(part_down, "dp", scatter_dimension=0, tiled=True),
    )
    return (
        grad_tokens,
        sum_gate.astype(jnp.bfloat16)[None],
        sum_up.astype(jnp.bfloat16)[None],
        sum_down.astype(jnp.bfloat16)[None],
    )


def solution(mesh):
    placed = (
        P(("expert", "dp"), None),
        P(("expert", "dp"), None),
        P(("expert", "dp"), None),
        P(("expert", "dp"), None),
        P("expert", "dp", None),
        P("expert", "dp", None),
        P("expert", "dp", None),
    )
    return jax.shard_map(
        shards,
        mesh=mesh,
        in_specs=placed,
        out_specs=(
            P(("expert", "dp"), None),
            P("expert", "dp", None),
            P("expert", "dp", None),
            P("expert", "dp", None),
        ),
        check_vma=False,
    )
```

profile of v0, /device:TPU:1, one launch (start us, length us, event | category | flops | bytes accessed | tf_op | source)
XLA Modules:
  0.0 475.4 jit_solution(7728522558410782737)
XLA Ops:
  7.2 0.7 all-gather.8.cloned.1.call-update
  7.9 0.8 copy.12
  8.9 1.2 reduce-window.6
  10.1 0.2 slice_reduce_fusion
  10.4 0.7 broadcast_multiply_fusion
  11.5 2.4 scatter_custom_fusion.1
  14.0 3.4 gather_fusion.1
  17.4 2.8 gather.15
  20.2 2.4 scatter_custom_fusion.2
  22.6 0.1 broadcast_in_dim.47
  22.8 4.5 broadcast_select_fusion
  27.3 13.5 %all-to-all-start.1 = ((bf16[64,9,2048]{2,1,0:T(8,128)(2,1)}), bf16[64,9,2048]{2,1,0:T(8,128)(2,1)}, u32[]{:S(2)}, u32[]{:S(2)}) async-start(bf16[64,9,2048]{2,1,0:T(8,128)(2,1)} %broadcast_select_fusion), calls=%async_computation.1 | async-start | bytes 8388608 | tf_op jit(solution)/shard_map/all_to_all | solution.py:46
  40.8 0.7 all-gather.6.cloned.1.call-update
  41.5 0.3 copy-done.2
  41.8 3.4 gather_fusion
  45.2 3.7 reshape.97
  49.1 2.4 scatter_custom_fusion
  51.6 0.1 mul.55
  51.7 5.8 %multiply_convert_fusion = bf16[64,9,2048]{2,1,0:T(8,128)(2,1)} fusion(f32[64,9,2048]{2,1,0:T(8,128)} %reshape.97, f32[64,9]{1,0:T(8,128)S(1)} %mul.55), kind=kLoop, calls=%fused_computation.6 | loop fusion | flops 2359296 | bytes 7080192 | tf_op jit(solution)/shard_map/convert_element_type | solution.py:34
  57.5 77.6 %all-to-all-done.1 = bf16[64,9,2048]{2,1,0:T(8,128)(2,1)} async-done(((bf16[64,9,2048]{2,1,0:T(8,128)(2,1)}), bf16[64,9,2048]{2,1,0:T(8,128)(2,1)}, u32[]{:S(2)}, u32[]{:S(2)}) %all-to-all-start.1) | async-done | bytes 2359328 | tf_op jit(solution)/shard_map/all_to_all | solution.py:46
  135.2 7.4 %all-to-all-start = ((bf16[64,9,2048]{2,1,0:T(8,128)(2,1)}), bf16[64,9,2048]{2,1,0:T(8,128)(2,1)}, u32[]{:S(2)}, u32[]{:S(2)}) async-start(bf16[64,9,2048]{2,1,0:T(8,128)(2,1)} %multiply_convert_fusion), calls=%async_computation | async-start | bytes 8388608 | tf_op jit(solution)/shard_map/all_to_all | solution.py:47
  142.6 0.7 all-gather.4.cloned.1.call-update
  143.3 0.2 reduce-scatter.6.cloned.1.call-start
  143.5 4.7 reshape.94
  148.2 89.0 %all-to-all-done = bf16[64,9,2048]{2,1,0:T(8,128)(2,1)} async-done(((bf16[64,9,2048]{2,1,0:T(8,128)(2,1)}), bf16[64,9,2048]{2,1,0:T(8,128)(2,1)}, u32[]{:S(2)}, u32[]{:S(2)}) %all-to-all-start) | async-done | bytes 2359328 | tf_op jit(solution)/shard_map/all_to_all | solution.py:47
  237.2 3.4 reshape.93
  240.6 5.8 %fusion.2 = f32[576,768]{1,0:T(8,128)} fusion(bf16[576,2048]{1,0:T(8,128)(2,1)} %reshape.94, bf16[1,2048,768]{2,1,0:T(8,128)(2,1)} %all-gather.8.cloned.1.call-done), kind=kOutput, calls=%fused_computation.11 | convolution fusion | flops 1811939328 | bytes 7274496 | tf_op jit(solution)/shard_map/dot_general | solution.py:50
  246.4 5.8 %fusion.6 = f32[576,768]{1,0:T(8,128)} fusion(bf16[576,2048]{1,0:T(8,128)(2,1)} %reshape.94, bf16[1,2048,768]{2,1,0:T(8,128)(2,1)} %all-gather.6.cloned.1.call-done), kind=kOutput, calls=%fused_computation.15 | convolution fusion | flops 1811939328 | bytes 7274496 | tf_op jit(solution)/shard_map/dot_general | solution.py:51
  252.2 6.6 %multiply_convert_fusion.2 = (bf16[576,768]{1,0:T(8,128)(2,1)S(1)}, bf16[576,768]{1,0:T(8,128)(2,1)}) fusion(f32[576,768]{1,0:T(8,128)} %fusion.2, f32[576,768]{1,0:T(8,128)} %fusion.6, bf16[576,2048]{1,0:T(8,128)(2,1)S(1)} %reshape.93, bf16[1,768,2048]{2,1,0:T(8,128)(2,1)} %all-gather.4.cloned.1.call-done), kind=kOutput, calls=%fused_computation.20 | convolution fusion | flops 1817690112 | bytes 10813440 | tf_op jit(solution)/shard_map/dot_general | solution.py:56
  258.8 0.9 copy-done.6
  259.7 4.5 fusion.29
  264.3 7.2 %fusion.28 = f32[2048,768]{1,0:T(8,128)} fusion(bf16[576,2048]{1,0:T(8,128)(2,1)} %reshape.94, bf16[576,768]{1,0:T(8,128)(2,1)} %get-tuple-element.5), kind=kOutput, calls=%fused_computation.55 | convolution fusion | flops 1811939328 | bytes 9535488 | tf_op jit(solution)/shard_map/dot_general | solution.py:72
  271.5 0.3 reduce-scatter.8.cloned.1.call-start
  271.8 6.8 %fusion.13 = f32[768,2048]{1,0:T(8,128)} fusion(bf16[576,2048]{1,0:T(8,128)(2,1)S(1)} %reshape.93, f32[576,768]{1,0:T(8,128)} %fusion.6, f32[576,768]{1,0:T(8,128)} %fusion.2), kind=kOutput, calls=%fused_computation.24 | convolution fusion | flops 1814593536 | bytes 12189696 | tf_op jit(solution)/shard_map/dot_general | solution.py:74
  278.7 1.1 copy-done.8
  279.8 4.1 fusion
  283.9 2.0 add_convert_fusion
  285.9 2.8 reshape.95
  288.8 8.0 %all-to-all-start.2 = ((bf16[64,9,2048]{2,1,0:T(8,128)(2,1)}), bf16[64,9,2048]{2,1,0:T(8,128)(2,1)}, u32[]{:S(2)}, u32[]{:S(2)}) async-start(bf16[64,9,2048]{2,1,0:T(8,128)(2,1)} %reshape.95), calls=%async_computation.2 | async-start | bytes 8388608 | tf_op jit(solution)/shard_map/all_to_all | solution.py:63
  296.8 94.6 %all-to-all-done.2 = bf16[64,9,2048]{2,1,0:T(8,128)(2,1)} async-done(((bf16[64,9,2048]{2,1,0:T(8,128)(2,1)}), bf16[64,9,2048]{2,1,0:T(8,128)(2,1)}, u32[]{:S(2)}, u32[]{:S(2)}) %all-to-all-start.2) | async-done | bytes 2359328 | tf_op jit(solution)/shard_map/all_to_all | solution.py:63
  391.4 3.4 reshape.96
  394.8 3.3 gather_fusion.2
  398.1 2.7 gather.17
  400.9 3.9 reduce_sum.25
  404.7 2.4 convert_bitcast_fusion.1
  407.2 2.4 convert_bitcast_fusion.2
  409.5 56.7 %reduce-scatter.8.cloned.1.call-done = f32[192,2048]{1,0:T(8,128)} async-done(((f32[768,2048]{1,0:T(8,128)}), f32[192,2048]{1,0:T(8,128)}) %reduce-scatter.8.cloned.1.call-update) | async-done | bytes 1572880 | tf_op jit(solution)/shard_map/reduce_scatter | solution.py:78
  466.2 2.4 convert_bitcast_fusion
  (43 shorter events, 1.1 us)
Async XLA Ops:
  7.2 6.8 %copy-start = (bf16[128,2048]{1,0:T(8,128)(2,1)S(1)}, bf16[128,2048]{1,0:T(8,128)(2,1)}, u32[]{:S(2)}) copy-start(bf16[128,2048]{1,0:T(8,128)(2,1)} %param.7) | copy-start | bytes 1572868
  7.2 233.4 %all-gather.8.cloned.1.call-start = ((), (), s32[]{:S(2)}) async-start(), calls=%async_computation.8 | async-start | bytes 3932160 | tf_op jit(solution)/shard_map/all_gather | solution.py:38
  27.3 107.9 %all-to-all-start.1 = ((bf16[64,9,2048]{2,1,0:T(8,128)(2,1)}), bf16[64,9,2048]{2,1,0:T(8,128)(2,1)}, u32[]{:S(2)}, u32[]{:S(2)}) async-start(bf16[64,9,2048]{2,1,0:T(8,128)(2,1)} %broadcast_select_fusion), calls=%async_computation.1 | async-start | bytes 8388608 | tf_op jit(solution)/shard_map/all_to_all | solution.py:46
  40.8 1.0 copy-start.2
  40.8 205.6 %all-gather.6.cloned.1.call-start = ((), (), s32[]{:S(2)}) async-start(), calls=%async_computation.7 | async-start | bytes 3932160 | tf_op jit(solution)/shard_map/all_gather | solution.py:39
  45.2 3.7 copy-start.4
  135.2 102.0 %all-to-all-start = ((bf16[64,9,2048]{2,1,0:T(8,128)(2,1)}), bf16[64,9,2048]{2,1,0:T(8,128)(2,1)}, u32[]{:S(2)}, u32[]{:S(2)}) async-start(bf16[64,9,2048]{2,1,0:T(8,128)(2,1)} %multiply_convert_fusion), calls=%async_computation | async-start | bytes 8388608 | tf_op jit(solution)/shard_map/all_to_all | solution.py:47
  142.5 109.7 %all-gather.4.cloned.1.call-start = ((), (), s32[]{:S(2)}) async-start(), calls=%async_computation.6 | async-start | bytes 3932160 | tf_op jit(solution)/shard_map/all_gather | solution.py:40
  143.3 261.4 %reduce-scatter.6.cloned.1.call-start = ((), (), s32[]{:S(2)}) async-start(), calls=%async_computation.10 | async-start | bytes 7864320 | tf_op jit(solution)/shard_map/reduce_scatter | solution.py:77
  252.2 7.5 %copy-start.3 = (bf16[576,2048]{1,0:T(8,128)(2,1)S(1)}, bf16[576,2048]{1,0:T(8,128)(2,1)}, u32[]{:S(2)}) copy-start(bf16[576,2048]{1,0:T(8,128)(2,1)} %reshape.94) | copy-start | bytes 7077892
  258.8 0.9 copy-start.6
  264.3 142.9 %reduce-scatter.4.cloned.1.call-start = ((), (), s32[]{:S(2)}) async-start(), calls=%async_computation.9 | async-start | bytes 7864320 | tf_op jit(solution)/shard_map/reduce_scatter | solution.py:76
  271.5 194.7 %reduce-scatter.8.cloned.1.call-start = ((), (), s32[]{:S(2)}) async-start(), calls=%async_computation.11 | async-start | bytes 7864320 | tf_op jit(solution)/shard_map/reduce_scatter | solution.py:78
  278.6 1.2 copy-start.8
  279.8 4.1 copy-start.5
  279.8 4.1 copy-start.7
  288.8 102.7 %all-to-all-start.2 = ((bf16[64,9,2048]{2,1,0:T(8,128)(2,1)}), bf16[64,9,2048]{2,1,0:T(8,128)(2,1)}, u32[]{:S(2)}, u32[]{:S(2)}) async-start(bf16[64,9,2048]{2,1,0:T(8,128)(2,1)} %reshape.95), calls=%async_computation.2 | async-start | bytes 8388608 | tf_op jit(solution)/shard_map/all_to_all | solution.py:63
  404.7 63.9 %copy-start.1 = (bf16[128,2048]{1,0:T(8,128)(2,1)S(1)}, bf16[128,2048]{1,0:T(8,128)(2,1)}, u32[]{:S(2)}) copy-start(bf16[128,2048]{1,0:T(8,128)(2,1)} %param.7) | copy-start | bytes 1572868
Sparse Core Ops, SparseCore 0:
  9.8 45.9 all-gather.7
  57.6 42.3 all-gather.5
  145.2 43.3 all-gather.3
  264.4 64.3 reduce-scatter.5
  331.2 66.2 reduce-scatter.3
  399.9 66.2 reduce-scatter.7
where the time goes:
time: 476 us; the launch traced here: 475 us
  waiting for transfers between devices  320 us (67%)
  local copies, waits for them, and re-layouts  45.3 us (10%)
  matrix products  42.8 us (9%)
  starting transfers between devices  29.5 us (6%)
  other arithmetic  23.5 us (5%)
  between operations  14.3 us (3%)
    all_to_all x1, waiting for transfers between devices, shards(): lax.all_to_all(slot_grad.reshape(owners, slot_cap, width), 'expert', spli...  94.6 us
    all_to_all x1, waiting for transfers between devices, shards(): lax.all_to_all(send_cot, 'expert', split_axis=0, concat_axis=0, tiled=True)  89 us
    all_to_all x1, waiting for transfers between devices, shards(): lax.all_to_all(send_rows, 'expert', split_axis=0, concat_axis=0, tiled=True)  77.6 us
    reduce_scatter x1, waiting for transfers between devices, shards(): lax.psum_scatter(part_down, 'dp', scatter_dimension=0, tiled=True)  56.7 us
    all_to_all x1, starting transfers between devices, shards(): lax.all_to_all(send_rows, 'expert', split_axis=0, concat_axis=0, tiled=True)  13.5 us
  transfers between devices with their start and end apart: 9, of which 4 were waited for; matrix products, arithmetic and copies ran while one was open for 20% of the time, Pallas kernels for 0%

commit v1 on v0

--- a/solution.py
+++ b/solution.py
@@ -26,14 +26,9 @@
     )
     filled = jnp.zeros((owners * slot_cap,), jnp.bool_).at[slots].set(True)
     slot_probs = jnp.zeros((owners * slot_cap,), jnp.float32).at[slots].set(gate_probs.reshape(-1))
-    send_rows = jnp.where(filled[:, None], tokens[source], jnp.zeros((), jnp.bfloat16)).reshape(
-        owners, slot_cap, width
-    )
-    send_cot = (
-        (slot_probs[:, None] * cotangent[source].astype(jnp.float32))
-        .astype(jnp.bfloat16)
-        .reshape(owners, slot_cap, width)
-    )
+    send_rows = jnp.where(filled[:, None], tokens[source], jnp.zeros((), jnp.bfloat16))
+    send_cot = (slot_probs[:, None] * cotangent[source].astype(jnp.float32)).astype(jnp.bfloat16)
+    send_both = jnp.concatenate([send_rows, send_cot], axis=1).reshape(owners, slot_cap, 2 * width)
     full_gate, full_up, full_down = (
         lax.all_gather(w_gate, "dp", axis=1, tiled=True),
         lax.all_gather(w_up, "dp", axis=1, tiled=True),
@@ -42,20 +37,25 @@
     gate_full = full_gate[0]
     up_full = full_up[0]
     down_full = full_down[0]
-    got_rows, got_cot = (
-        lax.all_to_all(send_rows, "expert", split_axis=0, concat_axis=0, tiled=True),
-        lax.all_to_all(send_cot, "expert", split_axis=0, concat_axis=0, tiled=True),
-    )
-    rows = got_rows.reshape(-1, width)
+    got_both = lax.all_to_all(send_both, "expert", split_axis=0, concat_axis=0, tiled=True)
+    got_both = got_both.reshape(-1, 2 * width)
+    rows = got_both[:, :width]
+    scaled = got_both[:, width:]
     pre_gate = jnp.dot(rows, gate_full, preferred_element_type=jnp.float32)
     pre_up = jnp.dot(rows, up_full, preferred_element_type=jnp.float32)
-    pre_gate, pre_up = (pre_gate, pre_up)
-    scaled = got_cot.reshape(-1, width)
     act_value, act_slope = silu_parts(pre_gate)
     activ = (act_value * pre_up).astype(jnp.bfloat16)
     grad_act = jnp.dot(scaled, down_full.T, preferred_element_type=jnp.float32)
     grad_pre_gate = (grad_act * pre_up * act_slope).astype(jnp.bfloat16)
     grad_pre_up = (grad_act * act_value).astype(jnp.bfloat16)
+    part_gate = jnp.dot(rows.T, grad_pre_gate, preferred_element_type=jnp.float32)
+    part_up = jnp.dot(rows.T, grad_pre_up, preferred_element_type=jnp.float32)
+    part_down = jnp.dot(activ.T, scaled, preferred_element_type=jnp.float32)
+    sum_gate, sum_up, sum_down = (
+        lax.psum_scatter(part_gate.astype(jnp.bfloat16), "dp", scatter_dimension=0, tiled=True),
+        lax.psum_scatter(part_up.astype(jnp.bfloat16), "dp", scatter_dimension=0, tiled=True),
+        lax.psum_scatter(part_down.astype(jnp.bfloat16), "dp", scatter_dimension=0, tiled=True),
+    )
     slot_grad = jnp.dot(grad_pre_gate, gate_full.T, preferred_element_type=jnp.float32)
     slot_grad = (
         slot_grad + jnp.dot(grad_pre_up, up_full.T, preferred_element_type=jnp.float32)
@@ -69,19 +69,11 @@
     ).reshape(-1, width)
     per_entry = returned[slots].astype(jnp.float32).reshape(tok_rows, top_count, width)
     grad_tokens = jnp.sum(per_entry, axis=1).astype(jnp.bfloat16)
-    part_gate = jnp.dot(rows.T, grad_pre_gate, preferred_element_type=jnp.float32)
-    part_up = jnp.dot(rows.T, grad_pre_up, preferred_element_type=jnp.float32)
-    part_down = jnp.dot(activ.T, scaled, preferred_element_type=jnp.float32)
-    sum_gate, sum_up, sum_down = (
-        lax.psum_scatter(part_gate, "dp", scatter_dimension=0, tiled=True),
-        lax.psum_scatter(part_up, "dp", scatter_dimension=0, tiled=True),
-        lax.psum_scatter(part_down, "dp", scatter_dimension=0, tiled=True),
-    )
     return (
         grad_tokens,
-        sum_gate.astype(jnp.bfloat16)[None],
-        sum_up.astype(jnp.bfloat16)[None],
-        sum_down.astype(jnp.bfloat16)[None],
+        sum_gate[None],
+        sum_up[None],
+        sum_down[None],
     )
 
 

time: 476 us -> 424 us (0.89)
  waiting for transfers between devices: 320 us -> 277 us
  starting transfers between devices: 29.5 us -> 24.1 us
    reduce_scatter x3, waiting for transfers between devices: 56.7 us -> 0.01 us  [the longest x1 0.01 us: shards(): lax.psum_scatter(part_down.astype(jnp.bfloat16), 'dp', scatter_dimension=...]
    all_to_all x2 -> x1, waiting for transfers between devices: 167 us -> 181 us  [shards(): lax.all_to_all(send_both, 'expert', split_axis=0, concat_axis=0, tiled=True)]
    concatenate x0 -> x1, other arithmetic: none -> 8.72 us  [shards(): jnp.concatenate([send_rows, send_cot], axis=1)]
    all_to_all x2 -> x1, starting transfers between devices: 20.8 us -> 13.2 us  [shards(): lax.all_to_all(send_both, 'expert', split_axis=0, concat_axis=0, tiled=True)]
    broadcast_in_dim x3 -> x0, other arithmetic: 7.18 us -> none  [the longest x1 2.42 us: shards(): sum_up.astype(jnp.bfloat16)[None]]
  transfers between devices with their start and end apart: 9 -> 8, of which waited for: 4 -> 2; matrix products, arithmetic and copies ran while one was open for 20% -> 25% of each run, Pallas kernels for 0% -> 0%
where the time goes in v1:
time: 424 us; the launch traced here: 422 us
  waiting for transfers between devices  277 us (65%)
  local copies, waits for them, and re-layouts  46 us (11%)
  matrix products  38.6 us (9%)
  starting transfers between devices  24.1 us (6%)
  other arithmetic  22 us (5%)
  between operations  14.4 us (3%)
    all_to_all x1, waiting for transfers between devices, shards(): lax.all_to_all(send_both, 'expert', split_axis=0, concat_axis=0, tiled=True)  181 us
    all_to_all x1, waiting for transfers between devices, shards(): lax.all_to_all(slot_grad.reshape(owners, slot_cap, width), 'expert', spli...  94.4 us
    all_to_all x1, starting transfers between devices, shards(): lax.all_to_all(send_both, 'expert', split_axis=0, concat_axis=0, tiled=True)  13.2 us
    all_to_all x1, starting transfers between devices, shards(): lax.all_to_all(slot_grad.reshape(owners, slot_cap, width), 'expert', spli...  10.3 us
    concatenate x1, other arithmetic, shards(): jnp.concatenate([send_rows, send_cot], axis=1)  8.72 us
    reshape x1, local copies, waits for them, and re-layouts, shards(): got_both = got_both.reshape(-1, 2 * width)  8.51 us
  transfers between devices with their start and end apart: 8, of which 2 were waited for; matrix products, arithmetic and copies ran while one was open for 25% of the time, Pallas kernels for 0%

profile of v1, /device:TPU:1, one launch (start us, length us, event | category | flops | bytes accessed | tf_op | source)
XLA Modules:
  0.0 422.4 jit_solution(6748770560743274585)
XLA Ops:
  7.2 0.7 all-gather.6.cloned.1.call-update
  7.9 0.8 copy.12
  8.7 0.1 eq.29
  8.8 0.1 eq.25
  8.9 1.2 reduce-window.6
  10.1 0.2 slice_reduce_fusion
  10.4 0.7 broadcast_multiply_fusion
  11.1 0.1 copy.11
  11.2 0.1 mul.53
  11.3 0.1 fusion.21
  11.5 2.4 scatter_custom_fusion.1
  14.0 3.4 gather_fusion.1
  17.4 3.7 reshape.94
  21.1 0.1 copy.15
  21.2 0.1 reshape.139
  21.3 2.4 scatter_custom_fusion.2
  23.7 0.1 mul.55
  23.9 3.4 gather_fusion
  27.3 2.8 gather.14
  30.1 2.4 scatter_custom_fusion
  32.6 0.1 broadcast_in_dim.45
  32.7 4.9 %broadcast_select_fusion = bf16[64,9,2048]{2,1,0:T(8,128)(2,1)} fusion(bf16[64,9,2048]{2,1,0:T(8,128)(2,1)} %gather.14, pred[64,9]{1,0:T(8,128)(4,1)S(1)} %broadcast_in_dim.45), kind=kLoop, calls=%fused_computation.9 | loop fusion | flops 1179648 | bytes 4719168 | tf_op jit(solution)/shard_map/jit(_where)/select_n | solution.py:29
  37.6 1.4 copy-done.3
  39.0 2.5 multiply_convert_fusion
  41.5 8.7 %pad_maximum_fusion = bf16[64,9,4096]{2,1,0:T(8,128)(2,1)} fusion(bf16[64,9,2048]{2,1,0:T(8,128)(2,1)} %multiply_convert_fusion, bf16[64,9,2048]{2,1,0:T(8,128)(2,1)} %broadcast_select_fusion), kind=kLoop, calls=%fused_computation.6 | loop fusion | flops 9437184 | bytes 9437184 | tf_op jit(solution)/shard_map/concatenate | solution.py:31
  50.2 13.2 %all-to-all-start = ((bf16[64,9,4096]{2,1,0:T(8,128)(2,1)}), bf16[64,9,4096]{2,1,0:T(8,128)(2,1)}, u32[]{:S(2)}, u32[]{:S(2)}) async-start(bf16[64,9,4096]{2,1,0:T(8,128)(2,1)} %pad_maximum_fusion), calls=%async_computation | async-start | bytes 16777216 | tf_op jit(solution)/shard_map/all_to_all | solution.py:40
  63.4 0.7 all-gather.8.cloned.1.call-update
  64.2 0.7 all-gather.4.cloned.1.call-update
  64.9 0.2 reduce-scatter.8.cloned.1.call-start
  65.1 180.7 %all-to-all-done = bf16[64,9,4096]{2,1,0:T(8,128)(2,1)} async-done(((bf16[64,9,4096]{2,1,0:T(8,128)(2,1)}), bf16[64,9,4096]{2,1,0:T(8,128)(2,1)}, u32[]{:S(2)}, u32[]{:S(2)}) %all-to-all-start) | async-done | bytes 4718624 | tf_op jit(solution)/shard_map/all_to_all | solution.py:40
  245.8 8.5 %reshape.91 = bf16[576,4096]{1,0:T(8,128)(2,1)} reshape(bf16[64,9,4096]{2,1,0:T(8,128)(2,1)} %all-to-all-done) | data formatting | bytes 9437184 | tf_op jit(solution)/shard_map/reshape | solution.py:41
  254.3 4.6 %fusion.6 = f32[576,768]{1,0:T(8,128)S(1)} fusion(bf16[1,2048,768]{2,1,0:T(8,128)(2,1)} %all-gather.6.cloned.1.call-done, bf16[576,4096]{1,0:T(8,128)(2,1)} %reshape.91), kind=kOutput, calls=%fused_computation.19 | convolution fusion | flops 1811939328 | bytes 7274496 | tf_op jit(solution)/shard_map/dot_general | solution.py:45
  258.9 5.2 %fusion.2 = f32[576,768]{1,0:T(8,128)S(1)} fusion(bf16[1,2048,768]{2,1,0:T(8,128)(2,1)} %all-gather.8.cloned.1.call-done, bf16[576,4096]{1,0:T(8,128)(2,1)} %reshape.91), kind=kOutput, calls=%fused_computation.15 | convolution fusion | flops 1811939328 | bytes 7274496 | tf_op jit(solution)/shard_map/dot_general | solution.py:44
  264.2 1.2 copy-done.8
  265.4 4.1 convolution_convert_fusion
  269.7 6.1 %multiply_convert_fusion.2 = (bf16[576,768]{1,0:T(8,128)(2,1)S(1)}, bf16[576,768]{1,0:T(8,128)(2,1)S(1)}) fusion(f32[576,768]{1,0:T(8,128)} %copy-done.8, f32[576,768]{1,0:T(8,128)} %copy-done.7, bf16[1,768,2048]{2,1,0:T(8,128)(2,1)} %all-gather.4.cloned.1.call-done, bf16[576,4096]{1,0:T(8,128)(2,1)} %reshape.91), kind=kOutput, calls=%fused_computation.26 | convolution fusion | flops 1817690112 | bytes 10813440 | tf_op jit(solution)/shard_map/dot_general | solution.py:48
  275.8 6.3 %convolution_convert_fusion.1 = bf16[2048,768]{1,0:T(8,128)(2,1)} fusion(bf16[576,768]{1,0:T(8,128)(2,1)S(1)} %get-tuple-element.4, bf16[576,4096]{1,0:T(8,128)(2,1)} %reshape.91), kind=kOutput, calls=%fused_computation.11 | convolution fusion | flops 1813512192 | bytes 6389760 | tf_op jit(solution)/shard_map/dot_general | solution.py:52
  282.2 0.3 reduce-scatter.4.cloned.1.call-start
  282.4 6.1 %convolution_convert_fusion.2 = bf16[2048,768]{1,0:T(8,128)(2,1)} fusion(bf16[576,768]{1,0:T(8,128)(2,1)S(1)} %get-tuple-element.5, bf16[576,4096]{1,0:T(8,128)(2,1)} %reshape.91), kind=kOutput, calls=%fused_computation.12 | convolution fusion | flops 1813512192 | bytes 6389760 | tf_op jit(solution)/shard_map/dot_general | solution.py:51
  288.6 4.1 fusion
  292.7 2.0 add_convert_fusion
  294.7 2.8 reshape.92
  297.5 10.3 %all-to-all-start.1 = ((bf16[64,9,2048]{2,1,0:T(8,128)(2,1)}), bf16[64,9,2048]{2,1,0:T(8,128)(2,1)}, u32[]{:S(2)}, u32[]{:S(2)}) async-start(bf16[64,9,2048]{2,1,0:T(8,128)(2,1)} %reshape.92), calls=%async_computation.1 | async-start | bytes 8388608 | tf_op jit(solution)/shard_map/all_to_all | solution.py:63
  307.8 94.4 %all-to-all-done.1 = bf16[64,9,2048]{2,1,0:T(8,128)(2,1)} async-done(((bf16[64,9,2048]{2,1,0:T(8,128)(2,1)}), bf16[64,9,2048]{2,1,0:T(8,128)(2,1)}, u32[]{:S(2)}, u32[]{:S(2)}) %all-to-all-start.1) | async-done | bytes 2359328 | tf_op jit(solution)/shard_map/all_to_all | solution.py:63
  402.2 3.4 reshape.93
  405.6 3.3 gather_fusion.2
  408.9 2.7 gather.17
  411.7 3.9 reduce_sum.25
  (42 shorter events, 0.4 us)
Async XLA Ops:
  7.2 6.8 %copy-start = (bf16[128,2048]{1,0:T(8,128)(2,1)S(1)}, bf16[128,2048]{1,0:T(8,128)(2,1)}, u32[]{:S(2)}) copy-start(bf16[128,2048]{1,0:T(8,128)(2,1)} %param.8) | copy-start | bytes 1572868
  7.2 247.1 %all-gather.6.cloned.1.call-start = ((), (), s32[]{:S(2)}) async-start(), calls=%async_computation.6 | async-start | bytes 3932160 | tf_op jit(solution)/shard_map/all_gather | solution.py:34
  17.4 3.7 copy-start.5
  17.4 6.5 %copy-start.2 = (bf16[128,2048]{1,0:T(8,128)(2,1)S(1)}, bf16[128,2048]{1,0:T(8,128)(2,1)}, u32[]{:S(2)}) copy-start(bf16[128,2048]{1,0:T(8,128)(2,1)} %param.7) | copy-start | bytes 1572868
  32.7 6.3 %copy-start.3 = (f32[64,9,2048]{2,1,0:T(8,128)S(1)}, f32[64,9,2048]{2,1,0:T(8,128)}, u32[]{:S(2)}) copy-start(f32[64,9,2048]{2,1,0:T(8,128)} %reshape.94) | copy-start | bytes 14155780
  50.2 195.6 %all-to-all-start = ((bf16[64,9,4096]{2,1,0:T(8,128)(2,1)}), bf16[64,9,4096]{2,1,0:T(8,128)(2,1)}, u32[]{:S(2)}, u32[]{:S(2)}) async-start(bf16[64,9,4096]{2,1,0:T(8,128)(2,1)} %pad_maximum_fusion), calls=%async_computation | async-start | bytes 16777216 | tf_op jit(solution)/shard_map/all_to_all | solution.py:40
  63.4 195.5 %all-gather.8.cloned.1.call-start = ((), (), s32[]{:S(2)}) async-start(), calls=%async_computation.7 | async-start | bytes 3932160 | tf_op jit(solution)/shard_map/all_gather | solution.py:33
  64.2 205.5 %all-gather.4.cloned.1.call-start = ((), (), s32[]{:S(2)}) async-start(), calls=%async_computation.5 | async-start | bytes 3932160 | tf_op jit(solution)/shard_map/all_gather | solution.py:35
  64.9 350.7 %reduce-scatter.8.cloned.1.call-start = ((), (), s32[]{:S(2)}) async-start(), calls=%async_computation.10 | async-start | bytes 3932160 | tf_op jit(solution)/shard_map/reduce_scatter | solution.py:57
  258.9 5.3 %copy-start.7 = (f32[576,768]{1,0:T(8,128)}, f32[576,768]{1,0:T(8,128)S(1)}, u32[]{:S(2)}) copy-start(f32[576,768]{1,0:T(8,128)S(1)} %fusion.6) | copy-start | bytes 5308420
  258.9 6.5 %copy-start.4 = (bf16[576,4096]{1,0:T(8,128)(2,1)S(1)}, bf16[576,4096]{1,0:T(8,128)(2,1)}, u32[]{:S(2)}) copy-start(bf16[576,4096]{1,0:T(8,128)(2,1)} %reshape.91) | copy-start | bytes 14155780
  264.2 1.3 copy-start.8
  269.6 146.0 %reduce-scatter.6.cloned.1.call-start = ((), (), s32[]{:S(2)}) async-start(), calls=%async_computation.9 | async-start | bytes 3932160 | tf_op jit(solution)/shard_map/reduce_scatter | solution.py:56
  275.8 6.4 %copy-start.9 = (bf16[576,768]{1,0:T(8,128)(2,1)}, bf16[576,768]{1,0:T(8,128)(2,1)S(1)}, u32[]{:S(2)}) copy-start(bf16[576,768]{1,0:T(8,128)(2,1)S(1)} %get-tuple-element.4) | copy-start | bytes 2654212
  282.2 133.4 %reduce-scatter.4.cloned.1.call-start = ((), (), s32[]{:S(2)}) async-start(), calls=%async_computation.8 | async-start | bytes 3932160 | tf_op jit(solution)/shard_map/reduce_scatter | solution.py:55
  288.6 4.1 copy-start.6
  288.6 4.1 copy-start.10
  297.5 104.7 %all-to-all-start.1 = ((bf16[64,9,2048]{2,1,0:T(8,128)(2,1)}), bf16[64,9,2048]{2,1,0:T(8,128)(2,1)}, u32[]{:S(2)}, u32[]{:S(2)}) async-start(bf16[64,9,2048]{2,1,0:T(8,128)(2,1)} %reshape.92), calls=%async_computation.1 | async-start | bytes 8388608 | tf_op jit(solution)/shard_map/all_to_all | solution.py:63
  405.6 9.9 %copy-start.1 = (bf16[128,2048]{1,0:T(8,128)(2,1)S(1)}, bf16[128,2048]{1,0:T(8,128)(2,1)}, u32[]{:S(2)}) copy-start(bf16[128,2048]{1,0:T(8,128)(2,1)} %param.8) | copy-start | bytes 1572868
Sparse Core Ops, SparseCore 0:
  9.8 45.9 all-gather.5
  66.1 43.1 all-gather.7
  111.1 42.3 all-gather.3
  269.7 41.7 reduce-scatter.7
  314.4 40.5 reduce-scatter.5
  358.0 40.5 reduce-scatter.3

commit v2 on v1

--- a/solution.py
+++ b/solution.py
@@ -28,7 +28,10 @@
     slot_probs = jnp.zeros((owners * slot_cap,), jnp.float32).at[slots].set(gate_probs.reshape(-1))
     send_rows = jnp.where(filled[:, None], tokens[source], jnp.zeros((), jnp.bfloat16))
     send_cot = (slot_probs[:, None] * cotangent[source].astype(jnp.float32)).astype(jnp.bfloat16)
-    send_both = jnp.concatenate([send_rows, send_cot], axis=1).reshape(owners, slot_cap, 2 * width)
+    lanes = 128
+    send_both = jnp.concatenate([send_rows, send_cot], axis=1).reshape(
+        owners, slot_cap * 2 * width // lanes, lanes
+    )
     full_gate, full_up, full_down = (
         lax.all_gather(w_gate, "dp", axis=1, tiled=True),
         lax.all_gather(w_up, "dp", axis=1, tiled=True),
@@ -61,7 +64,7 @@
         slot_grad + jnp.dot(grad_pre_up, up_full.T, preferred_element_type=jnp.float32)
     ).astype(jnp.bfloat16)
     returned = lax.all_to_all(
-        slot_grad.reshape(owners, slot_cap, width),
+        slot_grad.reshape(owners, slot_cap * width // lanes, lanes),
         "expert",
         split_axis=0,
         concat_axis=0,

time: 424 us -> 316 us (0.75)
  waiting for transfers between devices: 277 us -> 182 us
  other arithmetic: 22 us -> 9.37 us
    all_to_all x1, waiting for transfers between devices: 181 us -> 104 us  [shards(): lax.all_to_all(send_both, 'expert', split_axis=0, concat_axis=0, tiled=True)]
    all_to_all x1, waiting for transfers between devices: 94.4 us -> 55.1 us  [shards(): lax.all_to_all(slot_grad.reshape(owners, slot_cap * width // lanes, lanes...]
    reduce_scatter x1, waiting for transfers between devices: 0.01 us -> 21.2 us  [shards(): lax.psum_scatter(part_up.astype(jnp.bfloat16), 'dp', scatter_dimension=0,...]
    reshape x2 -> x3, local copies, waits for them, and re-layouts: 6.18 us -> 14.4 us  [the longest x1 8.3 us: shards(): jnp.concatenate([send_rows, send_cot], axis=1)]
    concatenate x1, other arithmetic: 8.72 us -> 2.75 us  [shards(): jnp.concatenate([send_rows, send_cot], axis=1)]
    select_n x1, other arithmetic: 4.89 us -> 0.23 us  [shards(): jnp.where(filled[:, None], tokens[source], jnp.zeros((), jnp.bfloat16))]
  transfers between devices with their start and end apart: 8 -> 8, of which waited for: 2 -> 3; matrix products, arithmetic and copies ran while one was open for 25% -> 30% of each run, Pallas kernels for 0% -> 0%
where the time goes in v2:
time: 316 us; the launch traced here: 315 us
  waiting for transfers between devices  182 us (58%)
  local copies, waits for them, and re-layouts  49.6 us (16%)
  matrix products  38.2 us (12%)
  starting transfers between devices  21.7 us (7%)
  between operations  14.4 us (5%)
  other arithmetic  9.37 us (3%)
    all_to_all x1, waiting for transfers between devices, shards(): lax.all_to_all(send_both, 'expert', split_axis=0, concat_axis=0, tiled=True)  104 us
    all_to_all x1, waiting for transfers between devices, shards(): lax.all_to_all(slot_grad.reshape(owners, slot_cap * width // lanes, lanes...  55.1 us
    reduce_scatter x1, waiting for transfers between devices, shards(): lax.psum_scatter(part_up.astype(jnp.bfloat16), 'dp', scatter_dimension=0,...  21.2 us
    all_to_all x1, starting transfers between devices, shards(): lax.all_to_all(send_both, 'expert', split_axis=0, concat_axis=0, tiled=True)  12.9 us
    reshape x1, local copies, waits for them, and re-layouts, shards(): jnp.concatenate([send_rows, send_cot], axis=1)  8.3 us
    reshape x1, local copies, waits for them, and re-layouts, shards(): got_both = got_both.reshape(-1, 2 * width)  8.17 us
    all_to_all x1, starting transfers between devices, shards(): lax.all_to_all(slot_grad.reshape(owners, slot_cap * width // lanes, lanes...  8.08 us
    dot_general x1, matrix products, shards(): grad_act = jnp.dot(scaled, down_full.T, preferred_element_type=jnp.float32)  6.63 us
  transfers between devices with their start and end apart: 8, of which 3 were waited for; matrix products, arithmetic and copies ran while one was open for 30% of the time, Pallas kernels for 0%

profile of v2, /device:TPU:1, one launch (start us, length us, event | category | flops | bytes accessed | tf_op | source)
XLA Modules:
  0.0 315.2 jit_solution(300265263122107244)
XLA Ops:
  7.2 0.7 all-gather.8.cloned.1.call-update
  7.9 0.8 copy.12
  8.7 0.1 eq.29
  8.8 0.1 eq.25
  8.9 0.7 broadcast_multiply_fusion
  9.6 0.1 copy.11
  9.7 0.1 mul.50
  9.8 0.8 copy.15
  10.6 0.1 reshape.125
  10.7 1.2 reduce-window.6
  12.0 0.2 slice_reduce_fusion
  12.2 0.1 fusion.21
  12.4 2.4 scatter_custom_fusion.1
  14.9 4.0 %gather_fusion.1 = bf16[576,2048]{1,0:T(8,128)(2,1)} fusion(bf16[128,2048]{1,0:T(8,128)(2,1)S(1)} %copy-done, s32[1024]{0:T(1024)S(1)} %pad_clamp_fusion.1), kind=kCustom, calls=%fused_computation.1 | custom fusion | bytes 4720896 | tf_op jit(solution)/shard_map/gather | solution.py:30
  18.9 3.4 %gather_fusion = bf16[576,2048]{1,0:T(8,128)(2,1)S(1)} fusion(bf16[128,2048]{1,0:T(8,128)(2,1)S(1)} %copy-done.2, s32[1024]{0:T(1024)S(1)} %pad_clamp_fusion.1), kind=kCustom, calls=%fused_computation | custom fusion | bytes 4720896 | tf_op jit(solution)/shard_map/gather | solution.py:29
  22.3 2.4 scatter_custom_fusion
  24.7 2.4 scatter_custom_fusion.2
  27.2 0.2 broadcast_select_fusion
  27.4 1.6 copy-done.3
  29.1 0.4 multiply_convert_fusion
  29.5 2.7 pad_maximum_fusion
  32.3 8.3 %reshape.77 = bf16[64,288,128]{2,1,0:T(8,128)(2,1)} reshape(bf16[576,4096]{1,0:T(8,128)(2,1)} %pad_maximum_fusion) | data formatting | bytes 9437184 | tf_op jit(solution)/shard_map/reshape | solution.py:32
  40.6 12.9 %all-to-all-start = ((bf16[64,288,128]{2,1,0:T(8,128)(2,1)}), bf16[64,288,128]{2,1,0:T(8,128)(2,1)}, u32[]{:S(2)}, u32[]{:S(2)}) async-start(bf16[64,288,128]{2,1,0:T(8,128)(2,1)} %reshape.77), calls=%async_computation | async-start | bytes 9437184 | tf_op jit(solution)/shard_map/all_to_all | solution.py:43
  53.6 0.7 all-gather.6.cloned.1.call-update
  54.3 0.7 all-gather.4.cloned.1.call-update
  55.0 0.2 reduce-scatter.8.cloned.1.call-start
  55.2 103.5 %all-to-all-done = bf16[64,288,128]{2,1,0:T(8,128)(2,1)} async-done(((bf16[64,288,128]{2,1,0:T(8,128)(2,1)}), bf16[64,288,128]{2,1,0:T(8,128)(2,1)}, u32[]{:S(2)}, u32[]{:S(2)}) %all-to-all-start) | async-done | bytes 4718624 | tf_op jit(solution)/shard_map/all_to_all | solution.py:43
  158.8 8.2 %reshape.78 = bf16[576,4096]{1,0:T(8,128)(2,1)} reshape(bf16[64,288,128]{2,1,0:T(8,128)(2,1)} %all-to-all-done) | data formatting | bytes 9437184 | tf_op jit(solution)/shard_map/reshape | solution.py:44
  166.9 4.6 %fusion.2 = f32[576,768]{1,0:T(8,128)S(1)} fusion(bf16[1,2048,768]{2,1,0:T(8,128)(2,1)} %all-gather.8.cloned.1.call-done, bf16[576,4096]{1,0:T(8,128)(2,1)} %reshape.78), kind=kOutput, calls=%fused_computation.14 | convolution fusion | flops 1811939328 | bytes 7274496 | tf_op jit(solution)/shard_map/dot_general | solution.py:47
  171.6 4.7 %fusion.6 = f32[576,768]{1,0:T(8,128)S(1)} fusion(bf16[1,2048,768]{2,1,0:T(8,128)(2,1)} %all-gather.6.cloned.1.call-done, bf16[576,4096]{1,0:T(8,128)(2,1)} %reshape.78), kind=kOutput, calls=%fused_computation.18 | convolution fusion | flops 1811939328 | bytes 7274496 | tf_op jit(solution)/shard_map/dot_general | solution.py:48
  176.3 1.2 copy-done.6
  177.5 4.1 %convolution_convert_fusion = bf16[768,2048]{1,0:T(8,128)(2,1)} fusion(bf16[576,4096]{1,0:T(8,128)(2,1)S(1)} %copy-done.4, f32[576,768]{1,0:T(8,128)S(1)} %fusion.6, f32[576,768]{1,0:T(8,128)S(1)} %fusion.2), kind=kOutput, calls=%fused_computation.9 | convolution fusion | flops 1816166400 | bytes 9043968 | tf_op jit(solution)/shard_map/dot_general | solution.py:56
  181.7 0.0 reduce-scatter.4.cloned.1.call-start
  181.8 6.6 %multiply_convert_fusion.2 = (bf16[576,768]{1,0:T(8,128)(2,1)}, bf16[576,768]{1,0:T(8,128)(2,1)S(1)}) fusion(f32[576,768]{1,0:T(8,128)S(1)} %fusion.2, f32[576,768]{1,0:T(8,128)} %copy-done.6, bf16[1,768,2048]{2,1,0:T(8,128)(2,1)} %all-gather.4.cloned.1.call-done, bf16[576,4096]{1,0:T(8,128)(2,1)} %reshape.78), kind=kOutput, calls=%fused_computation.26 | convolution fusion | flops 1817690112 | bytes 10813440 | tf_op jit(solution)/shard_map/dot_general | solution.py:51
  188.4 6.0 %convolution_convert_fusion.2 = bf16[2048,768]{1,0:T(8,128)(2,1)} fusion(bf16[576,768]{1,0:T(8,128)(2,1)S(1)} %get-tuple-element.5, bf16[576,4096]{1,0:T(8,128)(2,1)} %reshape.78), kind=kOutput, calls=%fused_computation.11 | convolution fusion | flops 1813512192 | bytes 6389760 | tf_op jit(solution)/shard_map/dot_general | solution.py:54
  194.4 0.3 reduce-scatter.6.cloned.1.call-start
  194.7 0.9 copy-done.7
  195.6 6.0 %convolution_convert_fusion.1 = bf16[2048,768]{1,0:T(8,128)(2,1)} fusion(bf16[576,768]{1,0:T(8,128)(2,1)S(1)} %copy-done.7, bf16[576,4096]{1,0:T(8,128)(2,1)} %reshape.78), kind=kOutput, calls=%fused_computation.10 | convolution fusion | flops 1813512192 | bytes 6389760 | tf_op jit(solution)/shard_map/dot_general | solution.py:55
  201.6 4.1 %fusion = f32[576,2048]{1,0:T(8,128)S(1)} fusion(bf16[576,768]{1,0:T(8,128)(2,1)S(1)} %get-tuple-element.5, bf16[1,2048,768]{2,1,0:T(8,128)(2,1)} %all-gather.8.cloned.1.call-done), kind=kOutput, calls=%fused_computation.12 | convolution fusion | flops 1811939328 | bytes 8749056 | tf_op jit(solution)/shard_map/dot_general | solution.py:62
  205.7 2.0 add_convert_fusion
  207.8 2.5 reshape.79
  210.3 8.1 %all-to-all-start.1 = ((bf16[64,144,128]{2,1,0:T(8,128)(2,1)}), bf16[64,144,128]{2,1,0:T(8,128)(2,1)}, u32[]{:S(2)}, u32[]{:S(2)}) async-start(bf16[64,144,128]{2,1,0:T(8,128)(2,1)} %reshape.79), calls=%async_computation.1 | async-start | bytes 4718592 | tf_op jit(solution)/shard_map/all_to_all | solution.py:66
  218.4 55.1 %all-to-all-done.1 = bf16[64,144,128]{2,1,0:T(8,128)(2,1)} async-done(((bf16[64,144,128]{2,1,0:T(8,128)(2,1)}), bf16[64,144,128]{2,1,0:T(8,128)(2,1)}, u32[]{:S(2)}, u32[]{:S(2)}) %all-to-all-start.1) | async-done | bytes 2359328 | tf_op jit(solution)/shard_map/all_to_all | solution.py:66
  273.5 3.6 %reshape.80 = bf16[576,2048]{1,0:T(8,128)(2,1)S(1)} reshape(bf16[64,144,128]{2,1,0:T(8,128)(2,1)} %all-to-all-done.1) | data formatting | bytes 4718592 | tf_op jit(solution)/shard_map/reshape | solution.py:72
  277.1 3.3 %gather_fusion.2 = bf16[512,2048]{1,0:T(8,128)(2,1)} fusion(bf16[576,2048]{1,0:T(8,128)(2,1)S(1)} %reshape.80, s32[1024]{0:T(1024)S(1)} %pad_clamp_fusion), kind=kCustom, calls=%fused_computation.2 | custom fusion | bytes 4196352 | tf_op jit(solution)/shard_map/gather | solution.py:73
  280.4 2.8 gather.14
  283.2 3.9 %reduce_sum.25 = bf16[128,2048]{1,0:T(8,128)(2,1)} reduce(bf16[128,4,2048]{2,1,0:T(4,128)(2,1)S(1)} %gather.14, bf16[]{:T(256)} %constant.42.clone.1), dimensions={1}, to_apply=%region_6.7 | reduce | flops 786432 | bytes 2621442 | tf_op jit(solution)/shard_map/reduce_sum | solution.py:74
  287.1 21.2 %reduce-scatter.6.cloned.1.call-done = bf16[512,768]{1,0:T(8,128)(2,1)} async-done(((bf16[2048,768]{1,0:T(8,128)(2,1)}), bf16[512,768]{1,0:T(8,128)(2,1)}) %reduce-scatter.6.cloned.1.call-update) | async-done | bytes 786448 | tf_op jit(solution)/shard_map/reduce_scatter | solution.py:59
  (35 shorter events, 0.3 us)
Async XLA Ops:
  7.2 7.7 %copy-start = (bf16[128,2048]{1,0:T(8,128)(2,1)S(1)}, bf16[128,2048]{1,0:T(8,128)(2,1)}, u32[]{:S(2)}) copy-start(bf16[128,2048]{1,0:T(8,128)(2,1)} %param.8) | copy-start | bytes 1572868
  7.2 159.8 %all-gather.8.cloned.1.call-start = ((), (), s32[]{:S(2)}) async-start(), calls=%async_computation.7 | async-start | bytes 3932160 | tf_op jit(solution)/shard_map/all_gather | solution.py:36
  14.9 4.0 %copy-start.2 = (bf16[128,2048]{1,0:T(8,128)(2,1)S(1)}, bf16[128,2048]{1,0:T(8,128)(2,1)}, u32[]{:S(2)}) copy-start(bf16[128,2048]{1,0:T(8,128)(2,1)} %param.7) | copy-start | bytes 1572868
  27.2 1.9 copy-start.3
  40.6 118.2 %all-to-all-start = ((bf16[64,288,128]{2,1,0:T(8,128)(2,1)}), bf16[64,288,128]{2,1,0:T(8,128)(2,1)}, u32[]{:S(2)}, u32[]{:S(2)}) async-start(bf16[64,288,128]{2,1,0:T(8,128)(2,1)} %reshape.77), calls=%async_computation | async-start | bytes 9437184 | tf_op jit(solution)/shard_map/all_to_all | solution.py:43
  53.5 118.0 %all-gather.6.cloned.1.call-start = ((), (), s32[]{:S(2)}) async-start(), calls=%async_computation.6 | async-start | bytes 3932160 | tf_op jit(solution)/shard_map/all_gather | solution.py:37
  54.3 127.5 %all-gather.4.cloned.1.call-start = ((), (), s32[]{:S(2)}) async-start(), calls=%async_computation.5 | async-start | bytes 3932160 | tf_op jit(solution)/shard_map/all_gather | solution.py:38
  55.0 232.1 %reduce-scatter.8.cloned.1.call-start = ((), (), s32[]{:S(2)}) async-start(), calls=%async_computation.10 | async-start | bytes 3932160 | tf_op jit(solution)/shard_map/reduce_scatter | solution.py:60
  171.6 6.0 %copy-start.4 = (bf16[576,4096]{1,0:T(8,128)(2,1)S(1)}, bf16[576,4096]{1,0:T(8,128)(2,1)}, u32[]{:S(2)}) copy-start(bf16[576,4096]{1,0:T(8,128)(2,1)} %reshape.78) | copy-start | bytes 14155780
  176.3 1.2 copy-start.6
  181.7 105.4 %reduce-scatter.4.cloned.1.call-start = ((), (), s32[]{:S(2)}) async-start(), calls=%async_computation.8 | async-start | bytes 3932160 | tf_op jit(solution)/shard_map/reduce_scatter | solution.py:58
  194.4 1.2 copy-start.7
  194.4 113.9 %reduce-scatter.6.cloned.1.call-start = ((), (), s32[]{:S(2)}) async-start(), calls=%async_computation.9 | async-start | bytes 3932160 | tf_op jit(solution)/shard_map/reduce_scatter | solution.py:59
  201.6 4.1 %copy-start.5 = (bf16[1,2048,768]{2,1,0:T(8,128)(2,1)S(1)}, bf16[1,2048,768]{2,1,0:T(8,128)(2,1)}, u32[]{:S(2)}) copy-start(bf16[1,2048,768]{2,1,0:T(8,128)(2,1)} %all-gather.6.cloned.1.call-done) | copy-start | bytes 9437188
  201.6 4.1 %copy-start.8 = (bf16[576,768]{1,0:T(8,128)(2,1)S(1)}, bf16[576,768]{1,0:T(8,128)(2,1)}, u32[]{:S(2)}) copy-start(bf16[576,768]{1,0:T(8,128)(2,1)} %get-tuple-element.4) | copy-start | bytes 2654212
  210.3 63.2 %all-to-all-start.1 = ((bf16[64,144,128]{2,1,0:T(8,128)(2,1)}), bf16[64,144,128]{2,1,0:T(8,128)(2,1)}, u32[]{:S(2)}, u32[]{:S(2)}) async-start(bf16[64,144,128]{2,1,0:T(8,128)(2,1)} %reshape.79), calls=%async_computation.1 | async-start | bytes 4718592 | tf_op jit(solution)/shard_map/all_to_all | solution.py:66
  280.4 27.9 %copy-start.1 = (bf16[128,2048]{1,0:T(8,128)(2,1)S(1)}, bf16[128,2048]{1,0:T(8,128)(2,1)}, u32[]{:S(2)}) copy-start(bf16[128,2048]{1,0:T(8,128)(2,1)} %param.8) | copy-start | bytes 1572868
Sparse Core Ops, SparseCore 0:
  9.8 45.9 all-gather.7
  57.6 42.3 all-gather.5
  101.8 42.3 all-gather.3
  181.8 39.2 reduce-scatter.7
  224.1 40.5 reduce-scatter.3
  267.7 40.5 reduce-scatter.5

commit v3 on v2

--- a/solution.py
+++ b/solution.py
@@ -1,7 +1,58 @@
 import jax
 import jax.numpy as jnp
 from jax import lax
+from jax.experimental import pallas as pl
+from jax.experimental.pallas import tpu as pltpu
 from jax.sharding import PartitionSpec as P
+
+
+def _exchange_kernel(send_ref, recv_ref, send_sems, recv_sems, local_sem):
+    n = send_ref.shape[0]
+    me = lax.axis_index("expert")
+    group = lax.axis_index("dp")
+    local = pltpu.make_async_copy(send_ref.at[me], recv_ref.at[me], local_sem.at[0])
+    local.start()
+
+    def remote(peer, slot):
+        return pltpu.make_async_remote_copy(
+            src_ref=send_ref.at[peer],
+            dst_ref=recv_ref.at[slot],
+            send_sem=send_sems.at[peer],
+            recv_sem=recv_sems.at[slot],
+            device_id=(peer, group),
+            device_id_type=pl.DeviceIdType.MESH,
+        )
+
+    def start(i, carry):
+        remote(lax.rem(me + i, n), me).start()
+        return carry
+
+    lax.fori_loop(1, n, start, 0)
+
+    def wait(i, carry):
+        remote(lax.rem(me + i, n), me).wait_send()
+        src = lax.rem(me - i + n, n)
+        remote(src, src).wait_recv()
+        return carry
+
+    lax.fori_loop(1, n, wait, 0)
+    local.wait()
+
+
+def exchange(x):
+    n = x.shape[0]
+    return pl.pallas_call(
+        _exchange_kernel,
+        out_shape=jax.ShapeDtypeStruct(x.shape, x.dtype),
+        in_specs=[pl.BlockSpec(memory_space=pl.ANY)],
+        out_specs=pl.BlockSpec(memory_space=pl.ANY),
+        scratch_shapes=[
+            pltpu.SemaphoreType.DMA((n,)),
+            pltpu.SemaphoreType.DMA((n,)),
+            pltpu.SemaphoreType.DMA((1,)),
+        ],
+        compiler_params=pltpu.CompilerParams(has_side_effects=True),
+    )(x)
 
 
 def silu_parts(pre_gate):
@@ -40,7 +91,7 @@
     gate_full = full_gate[0]
     up_full = full_up[0]
     down_full = full_down[0]
-    got_both = lax.all_to_all(send_both, "expert", split_axis=0, concat_axis=0, tiled=True)
+    got_both = exchange(send_both)
     got_both = got_both.reshape(-1, 2 * width)
     rows = got_both[:, :width]
     scaled = got_both[:, width:]
@@ -63,13 +114,7 @@
     slot_grad = (
         slot_grad + jnp.dot(grad_pre_up, up_full.T, preferred_element_type=jnp.float32)
     ).astype(jnp.bfloat16)
-    returned = lax.all_to_all(
-        slot_grad.reshape(owners, slot_cap * width // lanes, lanes),
-        "expert",
-        split_axis=0,
-        concat_axis=0,
-        tiled=True,
-    ).reshape(-1, width)
+    returned = exchange(slot_grad.reshape(owners, slot_cap * width // lanes, lanes)).reshape(-1, width)
     per_entry = returned[slots].astype(jnp.float32).reshape(tok_rows, top_count, width)
     grad_tokens = jnp.sum(per_entry, axis=1).astype(jnp.bfloat16)
     return (

time: 316 us -> 332 us (1.051)
  Pallas kernels: 0 us -> 200 us
  waiting for transfers between devices: 182 us -> 21.5 us
  starting transfers between devices: 21.7 us -> 0.46 us
    pallas_call x0 -> x2, Pallas kernels: none -> 200 us  [exchange(): pl.pallas_call(_exchange_kernel, out_shape=jax.ShapeDtypeStruct(x.shape,...]
    all_to_all x2 -> x0, waiting for transfers between devices: 159 us -> none  [the longest x1 104 us: shards(): lax.all_to_all(send_both, 'expert', split_axis=0, concat_axis=0, tiled=True)]
    all_to_all x2 -> x0, starting transfers between devices: 21 us -> none  [the longest x1 12.9 us: shards(): lax.all_to_all(send_both, 'expert', split_axis=0, concat_axis=0, tiled=True)]
  transfers between devices with their start and end apart: 8 -> 6, of which waited for: 3 -> 1; matrix products, arithmetic and copies ran while one was open for 30% -> 28% of each run, Pallas kernels for 0% -> 60%
where the time goes in v3:
time: 332 us; the launch traced here: 331 us
  Pallas kernels  200 us (60%)
  local copies, waits for them, and re-layouts  48.3 us (15%)
  matrix products  38.2 us (12%)
  waiting for transfers between devices  21.5 us (6%)
  between operations  14.4 us (4%)
  other arithmetic  8.68 us (3%)
    pallas_call x2, Pallas kernels, exchange(): pl.pallas_call(_exchange_kernel, out_shape=jax.ShapeDtypeStruct(x.shape,...  200 us
    reduce_scatter x1, waiting for transfers between devices, shards(): lax.psum_scatter(part_up.astype(jnp.bfloat16), 'dp', scatter_dimension=0,...  19.3 us
    reshape x1, local copies, waits for them, and re-layouts, shards(): jnp.concatenate([send_rows, send_cot], axis=1)  8.3 us
    reshape x1, local copies, waits for them, and re-layouts, shards(): got_both = got_both.reshape(-1, 2 * width)  8.17 us
  transfers between devices with their start and end apart: 6, of which 1 were waited for; matrix products, arithmetic and copies ran while one was open for 28% of the time, Pallas kernels for 60%

profile of v3, /device:TPU:1, one launch (start us, length us, event | category | flops | bytes accessed | tf_op | source)
XLA Modules:
  0.0 331.3 jit_solution(4307350132483367728)
XLA Ops:
  7.2 0.0 all-gather.8.cloned.1.call-start
  7.2 0.7 all-gather.8.cloned.1.call-update
  7.9 0.0 all-gather.6.cloned.1.call-start
  8.0 0.7 all-gather.6.cloned.1.call-update
  8.7 0.0 all-gather.4.cloned.1.call-start
  8.7 0.7 all-gather.4.cloned.1.call-update
  9.4 0.0 reduce-scatter.8.cloned.1.call-start
  9.5 0.1 copy.12
  9.6 0.1 eq.29
  9.7 0.1 eq.25
  9.8 0.1 copy.11
  9.9 0.1 mul.50
  10.1 0.1 copy.15
  10.2 0.1 reshape.125
  10.3 1.2 reduce-window.6
  11.5 0.2 slice_reduce_fusion
  11.8 0.1 fusion.21
  11.9 2.4 scatter_custom_fusion.1
  14.4 4.0 %gather_fusion.1 = bf16[576,2048]{1,0:T(8,128)(2,1)} fusion(bf16[128,2048]{1,0:T(8,128)(2,1)S(1)} %copy-done, s32[1024]{0:T(1024)S(1)} %pad_clamp_fusion.1), kind=kCustom, calls=%fused_computation.1 | custom fusion | bytes 4720896 | tf_op jit(solution)/shard_map/gather | solution.py:81
  18.4 3.4 %gather_fusion = bf16[576,2048]{1,0:T(8,128)(2,1)S(1)} fusion(bf16[128,2048]{1,0:T(8,128)(2,1)S(1)} %copy-done.2, s32[1024]{0:T(1024)S(1)} %pad_clamp_fusion.1), kind=kCustom, calls=%fused_computation | custom fusion | bytes 4720896 | tf_op jit(solution)/shard_map/gather | solution.py:80
  21.9 2.4 scatter_custom_fusion
  24.3 2.4 scatter_custom_fusion.2
  26.8 0.2 broadcast_select_fusion
  27.0 1.6 copy-done.3
  28.6 0.4 multiply_convert_fusion
  29.0 2.7 pad_maximum_fusion
  31.8 8.3 %reshape.77.send_ref = bf16[64,288,128]{2,1,0:T(8,128)(2,1)} reshape(bf16[576,4096]{1,0:T(8,128)(2,1)} %pad_maximum_fusion) | data formatting | bytes 9437184 | tf_op jit(solution)/shard_map/reshape | solution.py:83
  40.1 127.4 %shard_map.102 = bf16[64,288,128]{2,1,0:T(8,128)(2,1)} custom-call(bf16[64,288,128]{2,1,0:T(8,128)(2,1)} %reshape.77.send_ref), custom_call_target="tpu_custom_call" | custom-call | tf_op jit(solution)/shard_map/pallas_call | solution.py:44
  167.5 8.2 %reshape.78 = bf16[576,4096]{1,0:T(8,128)(2,1)} reshape(bf16[64,288,128]{2,1,0:T(8,128)(2,1)} %shard_map.102) | data formatting | bytes 9437184 | tf_op jit(solution)/shard_map/reshape | solution.py:95
  175.7 4.6 %fusion.2 = f32[576,768]{1,0:T(8,128)S(1)} fusion(bf16[1,2048,768]{2,1,0:T(8,128)(2,1)} %all-gather.8.cloned.1.call-done, bf16[576,4096]{1,0:T(8,128)(2,1)} %reshape.78), kind=kOutput, calls=%fused_computation.14 | convolution fusion | flops 1811939328 | bytes 7274496 | tf_op jit(solution)/shard_map/dot_general | solution.py:98
  180.3 4.7 %fusion.6 = f32[576,768]{1,0:T(8,128)S(1)} fusion(bf16[1,2048,768]{2,1,0:T(8,128)(2,1)} %all-gather.6.cloned.1.call-done, bf16[576,4096]{1,0:T(8,128)(2,1)} %reshape.78), kind=kOutput, calls=%fused_computation.18 | convolution fusion | flops 1811939328 | bytes 7274496 | tf_op jit(solution)/shard_map/dot_general | solution.py:99
  185.1 1.2 copy-done.8
  186.3 4.1 %convolution_convert_fusion = bf16[768,2048]{1,0:T(8,128)(2,1)} fusion(bf16[576,4096]{1,0:T(8,128)(2,1)S(1)} %copy-done.4, f32[576,768]{1,0:T(8,128)S(1)} %fusion.6, f32[576,768]{1,0:T(8,128)S(1)} %fusion.2), kind=kOutput, calls=%fused_computation.9 | convolution fusion | flops 1816166400 | bytes 9043968 | tf_op jit(solution)/shard_map/dot_general | solution.py:107
  190.5 0.0 reduce-scatter.4.cloned.1.call-start
  190.5 6.6 %multiply_convert_fusion.2 = (bf16[576,768]{1,0:T(8,128)(2,1)}, bf16[576,768]{1,0:T(8,128)(2,1)S(1)}) fusion(f32[576,768]{1,0:T(8,128)S(1)} %fusion.2, f32[576,768]{1,0:T(8,128)} %copy-done.8, bf16[1,768,2048]{2,1,0:T(8,128)(2,1)} %all-gather.4.cloned.1.call-done, bf16[576,4096]{1,0:T(8,128)(2,1)} %reshape.78), kind=kOutput, calls=%fused_computation.26 | convolution fusion | flops 1817690112 | bytes 10813440 | tf_op jit(solution)/shard_map/dot_general | solution.py:102
  197.2 6.0 %convolution_convert_fusion.2 = bf16[2048,768]{1,0:T(8,128)(2,1)} fusion(bf16[576,768]{1,0:T(8,128)(2,1)S(1)} %get-tuple-element.5, bf16[576,4096]{1,0:T(8,128)(2,1)} %reshape.78), kind=kOutput, calls=%fused_computation.11 | convolution fusion | flops 1813512192 | bytes 6389760 | tf_op jit(solution)/shard_map/dot_general | solution.py:105
  203.2 0.3 reduce-scatter.6.cloned.1.call-start
  203.5 0.9 copy-done.9
  204.3 6.0 %convolution_convert_fusion.1 = bf16[2048,768]{1,0:T(8,128)(2,1)} fusion(bf16[576,768]{1,0:T(8,128)(2,1)S(1)} %copy-done.9, bf16[576,4096]{1,0:T(8,128)(2,1)} %reshape.78), kind=kOutput, calls=%fused_computation.10 | convolution fusion | flops 1813512192 | bytes 6389760 | tf_op jit(solution)/shard_map/dot_general | solution.py:106
  210.4 4.1 %fusion = f32[576,2048]{1,0:T(8,128)S(1)} fusion(bf16[576,768]{1,0:T(8,128)(2,1)S(1)} %get-tuple-element.5, bf16[1,2048,768]{2,1,0:T(8,128)(2,1)} %all-gather.8.cloned.1.call-done), kind=kOutput, calls=%fused_computation.12 | convolution fusion | flops 1811939328 | bytes 8749056 | tf_op jit(solution)/shard_map/dot_general | solution.py:113
  214.5 2.0 add_convert_fusion
  216.5 2.5 reshape.79.send_ref
  219.0 72.4 %shard_map.103 = bf16[64,144,128]{2,1,0:T(8,128)(2,1)} custom-call(bf16[64,144,128]{2,1,0:T(8,128)(2,1)} %reshape.79.send_ref), custom_call_target="tpu_custom_call" | custom-call | tf_op jit(solution)/shard_map/pallas_call | solution.py:44
  291.5 3.7 %reshape.80 = bf16[576,2048]{1,0:T(8,128)(2,1)S(1)} reshape(bf16[64,144,128]{2,1,0:T(8,128)(2,1)} %shard_map.103) | data formatting | bytes 4718592 | tf_op jit(solution)/shard_map/reshape | solution.py:117
  295.2 3.3 %gather_fusion.2 = bf16[512,2048]{1,0:T(8,128)(2,1)} fusion(bf16[576,2048]{1,0:T(8,128)(2,1)S(1)} %reshape.80, s32[1024]{0:T(1024)S(1)} %pad_clamp_fusion), kind=kCustom, calls=%fused_computation.2 | custom fusion | bytes 4196352 | tf_op jit(solution)/shard_map/gather | solution.py:118
  298.5 2.8 gather.14
  301.3 3.9 %reduce_sum.25 = bf16[128,2048]{1,0:T(8,128)(2,1)} reduce(bf16[128,4,2048]{2,1,0:T(4,128)(2,1)S(1)} %gather.14, bf16[]{:T(256)} %constant.42.clone.1), dimensions={1}, to_apply=%region_6.7 | reduce | flops 786432 | bytes 2621442 | tf_op jit(solution)/shard_map/reduce_sum | solution.py:119
  305.2 19.3 %reduce-scatter.6.cloned.1.call-done = bf16[512,768]{1,0:T(8,128)(2,1)} async-done(((bf16[2048,768]{1,0:T(8,128)(2,1)}), bf16[512,768]{1,0:T(8,128)(2,1)}) %reduce-scatter.6.cloned.1.call-update) | async-done | bytes 786448 | tf_op jit(solution)/shard_map/reduce_scatter | solution.py:110
  (37 shorter events, 0.2 us)
Async XLA Ops:
  7.2 7.2 %copy-start = (bf16[128,2048]{1,0:T(8,128)(2,1)S(1)}, bf16[128,2048]{1,0:T(8,128)(2,1)}, u32[]{:S(2)}) copy-start(bf16[128,2048]{1,0:T(8,128)(2,1)} %param.8) | copy-start | bytes 1572868
  7.2 2.3 copy-start.5
  7.2 2.9 copy-start.6
  7.2 168.5 %all-gather.8.cloned.1.call-start = ((), (), s32[]{:S(2)}) async-start(), calls=%async_computation.5 | async-start | bytes 3932160 | tf_op jit(solution)/shard_map/all_gather | solution.py:87
  7.9 172.4 %all-gather.6.cloned.1.call-start = ((), (), s32[]{:S(2)}) async-start(), calls=%async_computation.4 | async-start | bytes 3932160 | tf_op jit(solution)/shard_map/all_gather | solution.py:88
  8.7 181.8 %all-gather.4.cloned.1.call-start = ((), (), s32[]{:S(2)}) async-start(), calls=%async_computation.3 | async-start | bytes 3932160 | tf_op jit(solution)/shard_map/all_gather | solution.py:89
  9.4 295.7 %reduce-scatter.8.cloned.1.call-start = ((), (), s32[]{:S(2)}) async-start(), calls=%async_computation.8 | async-start | bytes 3932160 | tf_op jit(solution)/shard_map/reduce_scatter | solution.py:111
  14.4 4.0 %copy-start.2 = (bf16[128,2048]{1,0:T(8,128)(2,1)S(1)}, bf16[128,2048]{1,0:T(8,128)(2,1)}, u32[]{:S(2)}) copy-start(bf16[128,2048]{1,0:T(8,128)(2,1)} %param.7) | copy-start | bytes 1572868
  26.8 1.8 copy-start.3
  180.3 6.0 %copy-start.4 = (bf16[576,4096]{1,0:T(8,128)(2,1)S(1)}, bf16[576,4096]{1,0:T(8,128)(2,1)}, u32[]{:S(2)}) copy-start(bf16[576,4096]{1,0:T(8,128)(2,1)} %reshape.78) | copy-start | bytes 14155780
  185.1 1.2 copy-start.8
  190.5 114.7 %reduce-scatter.4.cloned.1.call-start = ((), (), s32[]{:S(2)}) async-start(), calls=%async_computation.6 | async-start | bytes 3932160 | tf_op jit(solution)/shard_map/reduce_scatter | solution.py:109
  203.2 1.2 copy-start.9
  203.2 121.3 %reduce-scatter.6.cloned.1.call-start = ((), (), s32[]{:S(2)}) async-start(), calls=%async_computation.7 | async-start | bytes 3932160 | tf_op jit(solution)/shard_map/reduce_scatter | solution.py:110
  210.4 4.1 %copy-start.7 = (bf16[1,2048,768]{2,1,0:T(8,128)(2,1)S(1)}, bf16[1,2048,768]{2,1,0:T(8,128)(2,1)}, u32[]{:S(2)}) copy-start(bf16[1,2048,768]{2,1,0:T(8,128)(2,1)} %all-gather.6.cloned.1.call-done) | copy-start | bytes 9437188
  210.4 4.1 %copy-start.10 = (bf16[576,768]{1,0:T(8,128)(2,1)S(1)}, bf16[576,768]{1,0:T(8,128)(2,1)}, u32[]{:S(2)}) copy-start(bf16[576,768]{1,0:T(8,128)(2,1)} %get-tuple-element.4) | copy-start | bytes 2654212
  298.5 26.0 %copy-start.1 = (bf16[128,2048]{1,0:T(8,128)(2,1)S(1)}, bf16[128,2048]{1,0:T(8,128)(2,1)}, u32[]{:S(2)}) copy-start(bf16[128,2048]{1,0:T(8,128)(2,1)} %param.8) | copy-start | bytes 1572868
Sparse Core Ops, SparseCore 0:
  9.8 45.9 all-gather.7
  57.6 42.3 all-gather.5
  101.8 42.3 all-gather.3
  190.6 46.7 reduce-scatter.7
  240.3 40.5 reduce-scatter.3
  283.9 40.5 reduce-scatter.5

commit v4 on v1

v4 whole, which is shorter than its diff:
```python
import jax
import jax.numpy as jnp
from jax import lax
from jax.sharding import PartitionSpec as P

LANES = 128


def silu_parts(pre_gate):
    sigma = jax.nn.sigmoid(pre_gate)
    return (pre_gate * sigma, sigma * (1.0 + pre_gate * (1.0 - sigma)))


def exchange(block):
    owners = block.shape[0]
    flat = block.reshape(owners, -1, LANES)
    got = lax.all_to_all(flat, "expert", split_axis=0, concat_axis=0, tiled=True)
    return got


def shards(tokens, cotangent, expert_ids, gate_probs, w_gate, w_up, w_down):
    tok_rows, top_count = expert_ids.shape
    width = tokens.shape[1]
    owners = lax.axis_size("expert")
    groups = lax.axis_size("dp")
    slot_cap = (tok_rows * top_count * 9 + 8 * owners - 1) // (8 * owners)
    flat_ids = expert_ids.reshape(-1)
    one_hot = (flat_ids[:, None] == jnp.arange(owners, dtype=jnp.int32)[None, :]).astype(jnp.int32)
    ranks = jnp.sum((jnp.cumsum(one_hot, axis=0) - 1) * one_hot, axis=1)
    slots = (flat_ids * slot_cap + ranks).reshape(tok_rows, top_count)
    picks = slots[None, :, :] == jnp.arange(owners * slot_cap, dtype=jnp.int32)[:, None, None]
    select = jnp.any(picks, axis=2).astype(jnp.bfloat16)
    slot_probs = jnp.sum(jnp.where(picks, gate_probs[None, :, :], 0.0), axis=(1, 2))
    send_rows = jnp.dot(select, tokens, preferred_element_type=jnp.float32).astype(jnp.bfloat16)
    send_cot = (
        slot_probs[:, None] * jnp.dot(select, cotangent, preferred_element_type=jnp.float32)
    ).astype(jnp.bfloat16)
    send_both = jnp.concatenate([send_rows, send_cot], axis=1).reshape(owners, slot_cap, 2 * width)
    full_gate, full_up, full_down = (
        lax.all_gather(w_gate, "dp", axis=1, tiled=True),
        lax.all_gather(w_up, "dp", axis=1, tiled=True),
        lax.all_gather(w_down, "dp", axis=1, tiled=True),
    )
    gate_full = full_gate[0]
    up_full = full_up[0]
    down_full = full_down[0]
    got_both = exchange(send_both).reshape(owners * slot_cap, 2 * width)
    rows = got_both[:, :width]
    scaled = got_both[:, width:]
    pre_gate = jnp.dot(rows, gate_full, preferred_element_type=jnp.float32)
    pre_up = jnp.dot(rows, up_full, preferred_element_type=jnp.float32)
    act_value, act_slope = silu_parts(pre_gate)
    activ = (act_value * pre_up).astype(jnp.bfloat16)
    grad_act = jnp.dot(scaled, down_full.T, preferred_element_type=jnp.float32)
    grad_pre_gate = (grad_act * pre_up * act_slope).astype(jnp.bfloat16)
    grad_pre_up = (grad_act * act_value).astype(jnp.bfloat16)
    part_gate = jnp.dot(rows.T, grad_pre_gate, preferred_element_type=jnp.float32)
    part_up = jnp.dot(rows.T, grad_pre_up, preferred_element_type=jnp.float32)
    part_down = jnp.dot(activ.T, scaled, preferred_element_type=jnp.float32)
    parts = (part_gate, part_up, part_down)
    packed = jnp.concatenate(
        [p.astype(jnp.bfloat16).reshape(groups, -1, LANES) for p in parts], axis=1
    )
    summed = lax.psum_scatter(packed, "dp", scatter_dimension=0, tiled=True)[0]
    sums = []
    start = 0
    for p in parts:
        length = p.size // groups // LANES
        sums.append(summed[start:start + length].reshape(1, -1, p.shape[1]))
        start += length
    sum_gate, sum_up, sum_down = sums
    slot_grad = jnp.dot(grad_pre_gate, gate_full.T, preferred_element_type=jnp.float32)
    slot_grad = (
        slot_grad + jnp.dot(grad_pre_up, up_full.T, preferred_element_type=jnp.float32)
    ).astype(jnp.bfloat16)
    returned = exchange(slot_grad.reshape(owners, slot_cap, width)).reshape(owners * slot_cap, width)
    grad_tokens = lax.dot_general(
        select, returned, (((0,), (0,)), ((), ())), preferred_element_type=jnp.float32
    ).astype(jnp.bfloat16)
    return (grad_tokens, sum_gate, sum_up, sum_down)


def solution(mesh):
    placed = (
        P(("expert", "dp"), None),
        P(("expert", "dp"), None),
        P(("expert", "dp"), None),
        P(("expert", "dp"), None),
        P("expert", "dp", None),
        P("expert", "dp", None),
        P("expert", "dp", None),
    )
    return jax.shard_map(
        shards,
        mesh=mesh,
        in_specs=placed,
        out_specs=(
            P(("expert", "dp"), None),
            P("expert", "dp", None),
            P("expert", "dp", None),
            P("expert", "dp", None),
        ),
        check_vma=False,
    )
```

time: 424 us -> 319 us (0.75)
  waiting for transfers between devices: 277 us -> 114 us
  blocking collectives: 0 us -> 65.5 us
  starting transfers between devices: 24.1 us -> 13.4 us
  local copies, waits for them, and re-layouts: 46 us -> 51.4 us
  other arithmetic: 22 us -> 17 us
    all_to_all x2 -> x1, waiting for transfers between devices: 275 us -> 104 us  [exchange(): lax.all_to_all(flat, 'expert', split_axis=0, concat_axis=0, tiled=True)]
    all_to_all x0 -> x1, blocking collectives: none -> 65.5 us  [exchange(): lax.all_to_all(flat, 'expert', split_axis=0, concat_axis=0, tiled=True)]
    reshape x4 -> x8, local copies, waits for them, and re-layouts: 14.8 us -> 34.8 us  [the longest x3 18.7 us: shards(): p.astype(jnp.bfloat16).reshape(groups, -1, LANES)]
    gather x5 -> x0, local copies, waits for them, and re-layouts: 15.7 us -> none  [the longest x2 6.23 us: shards(): tokens[source]]
    another operation x1 -> x3, local copies, waits for them, and re-layouts: 0.01 us -> 12.1 us  [the longest x2 12.1 us: exchange(): flat = block.reshape(owners, -1, LANES)]
    concatenate x0 -> x1, other arithmetic: none -> 11.1 us  [shards(): jnp.concatenate([p.astype(jnp.bfloat16).reshape(groups, -1, LANES) for p...]
    all_to_all x2 -> x1, starting transfers between devices: 23.4 us -> 13.2 us  [exchange(): lax.all_to_all(flat, 'expert', split_axis=0, concat_axis=0, tiled=True)]
    reduce_scatter x3 -> x1, waiting for transfers between devices: 0.01 us -> 8.21 us  [shards(): summed = lax.psum_scatter(packed, 'dp', scatter_dimension=0, tiled=True)[0]]
  transfers between devices with their start and end apart: 8 -> 5, of which waited for: 2 -> 2; matrix products, arithmetic and copies ran while one was open for 25% -> 19% of each run, Pallas kernels for 0% -> 0%
where the time goes in v4:
time: 319 us; the launch traced here: 318 us
  waiting for transfers between devices  114 us (36%)
  blocking collectives  65.5 us (21%)
  local copies, waits for them, and re-layouts  51.4 us (16%)
  matrix products  42.5 us (13%)
  other arithmetic  17 us (5%)
  between operations  13.9 us (4%)
  starting transfers between devices  13.4 us (4%)
    all_to_all x1, waiting for transfers between devices, exchange(): lax.all_to_all(flat, 'expert', split_axis=0, concat_axis=0, tiled=True)  104 us
    all_to_all x1, blocking collectives, exchange(): lax.all_to_all(flat, 'expert', split_axis=0, concat_axis=0, tiled=True)  65.5 us
    reshape x3, local copies, waits for them, and re-layouts, shards(): p.astype(jnp.bfloat16).reshape(groups, -1, LANES)  18.7 us
    all_to_all x1, starting transfers between devices, exchange(): lax.all_to_all(flat, 'expert', split_axis=0, concat_axis=0, tiled=True)  13.2 us
    another operation x2, local copies, waits for them, and re-layouts, exchange(): flat = block.reshape(owners, -1, LANES)  12.1 us
    concatenate x1, other arithmetic, shards(): jnp.concatenate([p.astype(jnp.bfloat16).reshape(groups, -1, LANES) for p...  11.1 us
    reduce_scatter x1, waiting for transfers between devices, shards(): summed = lax.psum_scatter(packed, 'dp', scatter_dimension=0, tiled=True)[0]  8.21 us
    reshape x1, local copies, waits for them, and re-layouts, shards(): got_both = exchange(send_both).reshape(owners * slot_cap, 2 * width)  8.16 us
  transfers between devices with their start and end apart: 5, of which 2 were waited for; matrix products, arithmetic and copies ran while one was open for 19% of the time, Pallas kernels for 0%

profile of v4, /device:TPU:1, one launch (start us, length us, event | category | flops | bytes accessed | tf_op | source)
XLA Modules:
  0.0 317.8 jit_solution(2095896184770892702)
XLA Ops:
  7.2 0.0 all-gather.8.cloned.1.call-start
  7.2 0.7 all-gather.8.cloned.1.call-update
  7.9 0.8 copy.25
  8.7 0.1 eq.42
  8.8 0.1 eq.38
  9.0 1.2 reduce-window.6
  10.2 0.2 slice_reduce_fusion
  10.4 0.1 fusion.22
  10.6 0.1 reduce_sum.21
  10.7 0.1 copy.28
  10.7 0.7 multiply_add_fusion
  11.4 0.1 fusion.19
  11.6 0.9 select_reduce_fusion
  12.5 0.8 convolution_convert_fusion.3
  13.3 0.8 multiply_convert_fusion
  14.0 2.8 pad_maximum_fusion.1
  16.8 8.3 %reshape_reshape.6 = bf16[64,288,128]{2,1,0:T(8,128)(2,1)} reshape(bf16[576,4096]{1,0:T(8,128)(2,1)} %pad_maximum_fusion.1) | data formatting | bytes 9437184 | tf_op jit(solution)/shard_map/reshape;reshape | solution.py:16
  25.1 13.2 %all-to-all-start = ((bf16[64,288,128]{2,1,0:T(8,128)(2,1)}), bf16[64,288,128]{2,1,0:T(8,128)(2,1)}, u32[]{:S(2)}, u32[]{:S(2)}) async-start(bf16[64,288,128]{2,1,0:T(8,128)(2,1)} %reshape_reshape.6), calls=%async_computation | async-start | bytes 9437184 | tf_op jit(solution)/shard_map/all_to_all | solution.py:17
  38.4 0.0 all-gather.6.cloned.1.call-start
  38.4 0.7 all-gather.6.cloned.1.call-update
  39.1 0.0 all-gather.4.cloned.1.call-start
  39.2 0.7 all-gather.4.cloned.1.call-update
  39.8 0.0 reduce-scatter.2.cloned.1.call-start
  39.9 103.7 %all-to-all-done = bf16[64,288,128]{2,1,0:T(8,128)(2,1)} async-done(((bf16[64,288,128]{2,1,0:T(8,128)(2,1)}), bf16[64,288,128]{2,1,0:T(8,128)(2,1)}, u32[]{:S(2)}, u32[]{:S(2)}) %all-to-all-start) | async-done | bytes 4718624 | tf_op jit(solution)/shard_map/all_to_all | solution.py:17
  143.6 8.2 %reshape.67 = bf16[576,4096]{1,0:T(8,128)(2,1)} reshape(bf16[64,288,128]{2,1,0:T(8,128)(2,1)} %all-to-all-done) | data formatting | bytes 9437184 | tf_op jit(solution)/shard_map/reshape | solution.py:47
  151.8 4.6 %fusion.2 = f32[576,768]{1,0:T(8,128)S(1)} fusion(bf16[1,2048,768]{2,1,0:T(8,128)(2,1)} %all-gather.8.cloned.1.call-done, bf16[576,4096]{1,0:T(8,128)(2,1)} %reshape.67), kind=kOutput, calls=%fused_computation.9 | convolution fusion | flops 1811939328 | bytes 7274496 | tf_op jit(solution)/shard_map/dot_general | solution.py:50
  156.4 0.0 all-gather.6.cloned.1.call-done
  156.4 5.2 %fusion.6 = f32[576,768]{1,0:T(8,128)S(1)} fusion(bf16[1,2048,768]{2,1,0:T(8,128)(2,1)} %all-gather.6.cloned.1.call-done, bf16[576,4096]{1,0:T(8,128)(2,1)} %reshape.67), kind=kOutput, calls=%fused_computation.13 | convolution fusion | flops 1811939328 | bytes 7274496 | tf_op jit(solution)/shard_map/dot_general | solution.py:51
  161.7 1.2 copy-done.6
  162.9 4.1 %convolution_convert_fusion = bf16[768,2048]{1,0:T(8,128)(2,1)} fusion(bf16[576,4096]{1,0:T(8,128)(2,1)S(1)} %copy-done.2, f32[576,768]{1,0:T(8,128)S(1)} %fusion.6, f32[576,768]{1,0:T(8,128)S(1)} %fusion.2), kind=kOutput, calls=%fused_computation.4 | convolution fusion | flops 1816166400 | bytes 9043968 | tf_op jit(solution)/shard_map/dot_general | solution.py:59
  167.0 5.9 %reshape.71 = bf16[4,3072,128]{2,1,0:T(8,128)(2,1)} reshape(bf16[768,2048]{1,0:T(8,128)(2,1)} %convolution_convert_fusion) | data formatting | bytes 6291456 | tf_op jit(solution)/shard_map/reshape | solution.py:62
  172.9 6.1 %multiply_convert_fusion.2 = (bf16[576,768]{1,0:T(8,128)(2,1)S(1)}, bf16[576,768]{1,0:T(8,128)(2,1)S(1)}) fusion(f32[576,768]{1,0:T(8,128)} %copy-done.5, f32[576,768]{1,0:T(8,128)} %copy-done.6, bf16[1,768,2048]{2,1,0:T(8,128)(2,1)} %all-gather.4.cloned.1.call-done, bf16[576,4096]{1,0:T(8,128)(2,1)} %reshape.67), kind=kOutput, calls=%fused_computation.22 | convolution fusion | flops 1817690112 | bytes 10813440 | tf_op jit(solution)/shard_map/dot_general | solution.py:54
  179.0 6.0 %convolution_convert_fusion.1 = bf16[2048,768]{1,0:T(8,128)(2,1)} fusion(bf16[576,768]{1,0:T(8,128)(2,1)S(1)} %get-tuple-element.4, bf16[576,4096]{1,0:T(8,128)(2,1)} %reshape.67), kind=kOutput, calls=%fused_computation.5 | convolution fusion | flops 1813512192 | bytes 6389760 | tf_op jit(solution)/shard_map/dot_general | solution.py:58
  185.0 6.0 %convolution_convert_fusion.2 = bf16[2048,768]{1,0:T(8,128)(2,1)} fusion(bf16[576,768]{1,0:T(8,128)(2,1)S(1)} %get-tuple-element.5, bf16[576,4096]{1,0:T(8,128)(2,1)} %reshape.67), kind=kOutput, calls=%fused_computation.6 | convolution fusion | flops 1813512192 | bytes 6389760 | tf_op jit(solution)/shard_map/dot_general | solution.py:57
  191.0 6.4 %reshape.69 = bf16[4,3072,128]{2,1,0:T(8,128)(2,1)} reshape(bf16[2048,768]{1,0:T(8,128)(2,1)} %convolution_convert_fusion.2) | data formatting | bytes 6291456 | tf_op jit(solution)/shard_map/reshape | solution.py:62
  197.4 6.4 %reshape.70 = bf16[4,3072,128]{2,1,0:T(8,128)(2,1)} reshape(bf16[2048,768]{1,0:T(8,128)(2,1)} %convolution_convert_fusion.1) | data formatting | bytes 6291456 | tf_op jit(solution)/shard_map/reshape | solution.py:62
  203.8 11.1 %pad_maximum_fusion = bf16[4,9216,128]{2,1,0:T(8,128)(2,1)} fusion(bf16[4,3072,128]{2,1,0:T(8,128)(2,1)} %reshape.71, bf16[4,3072,128]{2,1,0:T(8,128)(2,1)} %reshape.70, bf16[4,3072,128]{2,1,0:T(8,128)(2,1)} %reshape.69), kind=kLoop, calls=%fused_computation | loop fusion | flops 28311552 | bytes 18874368 | tf_op jit(solution)/shard_map/concatenate | solution.py:61
  214.9 4.1 %fusion = f32[576,2048]{1,0:T(8,128)S(1)} fusion(bf16[576,768]{1,0:T(8,128)(2,1)S(1)} %get-tuple-element.5, bf16[1,2048,768]{2,1,0:T(8,128)(2,1)} %all-gather.8.cloned.1.call-done), kind=kOutput, calls=%fused_computation.7 | convolution fusion | flops 1811939328 | bytes 8749056 | tf_op jit(solution)/shard_map/dot_general | solution.py:72
  219.0 3.5 %add_convert_fusion = bf16[576,2048]{1,0:T(8,128)(2,1)} fusion(f32[576,2048]{1,0:T(8,128)S(1)} %fusion, bf16[576,768]{1,0:T(8,128)(2,1)S(1)} %get-tuple-element.4, bf16[1,2048,768]{2,1,0:T(8,128)(2,1)S(1)} %copy-done.4), kind=kOutput, calls=%fused_computation.2 | convolution fusion | flops 1814298624 | bytes 11108352 | tf_op jit(solution)/shard_map/dot_general | solution.py:74
  222.5 3.8 %reshape_reshape.7 = bf16[64,144,128]{2,1,0:T(8,128)(2,1)S(1)} reshape(bf16[576,2048]{1,0:T(8,128)(2,1)} %add_convert_fusion) | data formatting | bytes 4718592 | tf_op jit(solution)/shard_map/reshape;reshape | solution.py:16
  226.3 65.5 %all_to_all.10 = bf16[64,144,128]{2,1,0:T(8,128)(2,1)} all-to-all(bf16[64,144,128]{2,1,0:T(8,128)(2,1)S(1)} %reshape_reshape.7), channel_id=1, replica_groups=mesh['expert'=64,'dp'=4] {'expert'}, dimensions={0} | all-to-all | bytes 4718592 | tf_op jit(solution)/shard_map/all_to_all | solution.py:17
  291.8 3.6 %reshape.68 = bf16[576,2048]{1,0:T(8,128)(2,1)S(1)} reshape(bf16[64,144,128]{2,1,0:T(8,128)(2,1)} %all_to_all.10) | data formatting | bytes 4718592 | tf_op jit(solution)/shard_map/reshape | solution.py:76
  295.5 1.4 convolution_convert_fusion.4
  296.9 8.2 %reduce-scatter.2.cloned.1.call-done = bf16[1,9216,128]{2,1,0:T(8,128)(2,1)} async-done(((bf16[4,9216,128]{2,1,0:T(8,128)(2,1)}), bf16[1,9216,128]{2,1,0:T(8,128)(2,1)}) %reduce-scatter.2.cloned.1.call-update) | async-done | bytes 2359312 | tf_op jit(solution)/shard_map/reduce_scatter | solution.py:64
  305.1 1.8 fusion.25
  306.9 1.2 reshape.74
  308.2 1.6 reshape.73
  309.7 1.6 reshape.72
  (19 shorter events, 0.1 us)
Async XLA Ops:
  7.2 5.3 %copy-start = (bf16[128,2048]{1,0:T(8,128)(2,1)S(1)}, bf16[128,2048]{1,0:T(8,128)(2,1)}, u32[]{:S(2)}) copy-start(bf16[128,2048]{1,0:T(8,128)(2,1)} %param.7) | copy-start | bytes 1572868
  7.2 6.1 %copy-start.3 = (bf16[128,2048]{1,0:T(8,128)(2,1)S(1)}, bf16[128,2048]{1,0:T(8,128)(2,1)}, u32[]{:S(2)}) copy-start(bf16[128,2048]{1,0:T(8,128)(2,1)} %param.8) | copy-start | bytes 1572868
  7.2 144.6 %all-gather.8.cloned.1.call-start = ((), (), s32[]{:S(2)}) async-start(), calls=%async_computation.5 | async-start | bytes 3932160 | tf_op jit(solution)/shard_map/all_gather | solution.py:40
  25.1 118.5 %all-to-all-start = ((bf16[64,288,128]{2,1,0:T(8,128)(2,1)}), bf16[64,288,128]{2,1,0:T(8,128)(2,1)}, u32[]{:S(2)}, u32[]{:S(2)}) async-start(bf16[64,288,128]{2,1,0:T(8,128)(2,1)} %reshape_reshape.6), calls=%async_computation | async-start | bytes 9437184 | tf_op jit(solution)/shard_map/all_to_all | solution.py:17
  38.4 118.0 %all-gather.6.cloned.1.call-start = ((), (), s32[]{:S(2)}) async-start(), calls=%async_computation.4 | async-start | bytes 3932160 | tf_op jit(solution)/shard_map/all_gather | solution.py:41
  39.1 133.8 %all-gather.4.cloned.1.call-start = ((), (), s32[]{:S(2)}) async-start(), calls=%async_computation.3 | async-start | bytes 3932160 | tf_op jit(solution)/shard_map/all_gather | solution.py:42
  39.8 265.3 %reduce-scatter.2.cloned.1.call-start = ((), (), s32[]{:S(2)}) async-start(), calls=%async_computation.6 | async-start | bytes 11796480 | tf_op jit(solution)/shard_map/reduce_scatter | solution.py:64
  156.4 5.3 %copy-start.5 = (f32[576,768]{1,0:T(8,128)}, f32[576,768]{1,0:T(8,128)S(1)}, u32[]{:S(2)}) copy-start(f32[576,768]{1,0:T(8,128)S(1)} %fusion.2) | copy-start | bytes 5308420
  156.4 6.5 %copy-start.2 = (bf16[576,4096]{1,0:T(8,128)(2,1)S(1)}, bf16[576,4096]{1,0:T(8,128)(2,1)}, u32[]{:S(2)}) copy-start(bf16[576,4096]{1,0:T(8,128)(2,1)} %reshape.67) | copy-start | bytes 14155780
  161.7 1.2 copy-start.6
  214.9 4.1 %copy-start.4 = (bf16[1,2048,768]{2,1,0:T(8,128)(2,1)S(1)}, bf16[1,2048,768]{2,1,0:T(8,128)(2,1)}, u32[]{:S(2)}) copy-start(bf16[1,2048,768]{2,1,0:T(8,128)(2,1)} %all-gather.6.cloned.1.call-done) | copy-start | bytes 9437188
  305.1 6.2 %copy-start.1 = (bf16[128,2048]{1,0:T(8,128)(2,1)S(1)}, bf16[128,2048]{1,0:T(8,128)(2,1)}, u32[]{:S(2)}) copy-start(bf16[128,2048]{1,0:T(8,128)(2,1)} %param.7) | copy-start | bytes 1572868
Sparse Core Ops, SparseCore 0:
  9.8 45.9 all-gather.7
  57.6 42.3 all-gather.5
  101.8 42.3 all-gather.3
  215.0 90.0 reduce-scatter.1

commit v5 on v4

--- a/solution.py
+++ b/solution.py
@@ -54,21 +54,15 @@
     grad_act = jnp.dot(scaled, down_full.T, preferred_element_type=jnp.float32)
     grad_pre_gate = (grad_act * pre_up * act_slope).astype(jnp.bfloat16)
     grad_pre_up = (grad_act * act_value).astype(jnp.bfloat16)
-    part_gate = jnp.dot(rows.T, grad_pre_gate, preferred_element_type=jnp.float32)
-    part_up = jnp.dot(rows.T, grad_pre_up, preferred_element_type=jnp.float32)
+    grad_pre_both = jnp.concatenate([grad_pre_gate, grad_pre_up], axis=1)
+    part_both = jnp.dot(rows.T, grad_pre_both, preferred_element_type=jnp.float32)
     part_down = jnp.dot(activ.T, scaled, preferred_element_type=jnp.float32)
-    parts = (part_gate, part_up, part_down)
-    packed = jnp.concatenate(
-        [p.astype(jnp.bfloat16).reshape(groups, -1, LANES) for p in parts], axis=1
-    )
-    summed = lax.psum_scatter(packed, "dp", scatter_dimension=0, tiled=True)[0]
-    sums = []
-    start = 0
-    for p in parts:
-        length = p.size // groups // LANES
-        sums.append(summed[start:start + length].reshape(1, -1, p.shape[1]))
-        start += length
-    sum_gate, sum_up, sum_down = sums
+    sum_down = lax.psum_scatter(part_down.astype(jnp.bfloat16), "dp", scatter_dimension=0, tiled=True)
+    sum_both = lax.psum_scatter(part_both.astype(jnp.bfloat16), "dp", scatter_dimension=0, tiled=True)
+    hidden = grad_pre_gate.shape[1]
+    sum_gate = sum_both[:, :hidden][None]
+    sum_up = sum_both[:, hidden:][None]
+    sum_down = sum_down[None]
     slot_grad = jnp.dot(grad_pre_gate, gate_full.T, preferred_element_type=jnp.float32)
     slot_grad = (
         slot_grad + jnp.dot(grad_pre_up, up_full.T, preferred_element_type=jnp.float32)

time: 319 us -> 295 us (0.925)
  local copies, waits for them, and re-layouts: 51.4 us -> 28 us
  other arithmetic: 17 us -> 5.82 us
  waiting for transfers between devices: 114 us -> 122 us
    reshape x6 -> x0, local copies, waits for them, and re-layouts: 23 us -> none  [the longest x3 18.7 us: shards(): p.astype(jnp.bfloat16).reshape(groups, -1, LANES)]
    concatenate x1 -> x0, other arithmetic: 11.1 us -> none  [shards(): jnp.concatenate([p.astype(jnp.bfloat16).reshape(groups, -1, LANES) for p...]
    reduce_scatter x1 -> x2, waiting for transfers between devices: 8.21 us -> 16 us  [the longest x1 16 us: shards(): lax.psum_scatter(part_down.astype(jnp.bfloat16), 'dp', scatter_dimension=...]
    dot_general x2 -> x1, matrix products: 11.9 us -> 8.88 us  [shards(): jnp.dot(rows.T, grad_pre_both, preferred_element_type=jnp.float32)]
  transfers between devices with their start and end apart: 5 -> 6, of which waited for: 2 -> 2; matrix products, arithmetic and copies ran while one was open for 19% -> 21% of each run, Pallas kernels for 0% -> 0%
where the time goes in v5:
time: 295 us; the launch traced here: 294 us
  waiting for transfers between devices  122 us (41%)
  blocking collectives  66.3 us (22%)
  matrix products  44.2 us (15%)
  local copies, waits for them, and re-layouts  28 us (9%)
  between operations  13.9 us (5%)
  starting transfers between devices  13.8 us (5%)
  other arithmetic  5.82 us (2%)
    all_to_all x1, waiting for transfers between devices, exchange(): lax.all_to_all(flat, 'expert', split_axis=0, concat_axis=0, tiled=True)  104 us
    all_to_all x1, blocking collectives, exchange(): lax.all_to_all(flat, 'expert', split_axis=0, concat_axis=0, tiled=True)  66.3 us
    reduce_scatter x1, waiting for transfers between devices, shards(): lax.psum_scatter(part_down.astype(jnp.bfloat16), 'dp', scatter_dimension=...  16 us
    all_to_all x1, starting transfers between devices, exchange(): lax.all_to_all(flat, 'expert', split_axis=0, concat_axis=0, tiled=True)  13.2 us
    another operation x2, local copies, waits for them, and re-layouts, exchange(): flat = block.reshape(owners, -1, LANES)  12.1 us
    dot_general x1, matrix products, shards(): jnp.dot(rows.T, grad_pre_both, preferred_element_type=jnp.float32)  8.88 us
    reshape x1, local copies, waits for them, and re-layouts, shards(): got_both = exchange(send_both).reshape(owners * slot_cap, 2 * width)  8.21 us
    dot_general x1, matrix products, shards(): part_down = jnp.dot(activ.T, scaled, preferred_element_type=jnp.float32)  7.07 us
  transfers between devices with their start and end apart: 6, of which 2 were waited for; matrix products, arithmetic and copies ran while one was open for 21% of the time, Pallas kernels for 0%

profile of v5, /device:TPU:1, one launch (start us, length us, event | category | flops | bytes accessed | tf_op | source)
XLA Modules:
  0.0 293.7 jit_solution(14761022164266578412)
XLA Ops:
  7.2 0.0 copy-start
  7.2 0.0 all-gather.8.cloned.1.call-start
  7.2 0.0 copy-start.2
  7.2 0.7 all-gather.8.cloned.1.call-update
  7.9 0.8 copy.25
  8.7 0.1 eq.42
  8.8 0.1 eq.38
  8.9 1.2 reduce-window.6
  10.2 0.2 slice_reduce_fusion
  10.4 0.1 fusion.24
  10.5 0.1 reduce_sum.21
  10.7 0.1 copy.28
  10.7 0.7 multiply_add_fusion
  11.4 0.1 fusion.21
  11.6 0.9 select_reduce_fusion
  12.5 0.0 copy-done
  12.5 0.8 convolution_convert_fusion.2
  13.2 0.0 copy-done.2
  13.3 0.8 multiply_convert_fusion
  14.0 2.7 pad_maximum_fusion
  16.7 8.4 %reshape_reshape.6 = bf16[64,288,128]{2,1,0:T(8,128)(2,1)} reshape(bf16[576,4096]{1,0:T(8,128)(2,1)} %pad_maximum_fusion) | data formatting | bytes 9437184 | tf_op jit(solution)/shard_map/reshape;reshape | solution.py:16
  25.1 13.2 %all-to-all-start = ((bf16[64,288,128]{2,1,0:T(8,128)(2,1)}), bf16[64,288,128]{2,1,0:T(8,128)(2,1)}, u32[]{:S(2)}, u32[]{:S(2)}) async-start(bf16[64,288,128]{2,1,0:T(8,128)(2,1)} %reshape_reshape.6), calls=%async_computation | async-start | bytes 9437184 | tf_op jit(solution)/shard_map/all_to_all | solution.py:17
  38.3 0.0 all-gather.6.cloned.1.call-start
  38.4 0.7 all-gather.6.cloned.1.call-update
  39.1 0.0 all-gather.4.cloned.1.call-start
  39.1 0.7 all-gather.4.cloned.1.call-update
  39.8 0.2 reduce-scatter.3.cloned.1.call-start
  40.0 103.5 %all-to-all-done = bf16[64,288,128]{2,1,0:T(8,128)(2,1)} async-done(((bf16[64,288,128]{2,1,0:T(8,128)(2,1)}), bf16[64,288,128]{2,1,0:T(8,128)(2,1)}, u32[]{:S(2)}, u32[]{:S(2)}) %all-to-all-start) | async-done | bytes 4718624 | tf_op jit(solution)/shard_map/all_to_all | solution.py:17
  143.6 8.2 %reshape.43 = bf16[576,4096]{1,0:T(8,128)(2,1)} reshape(bf16[64,288,128]{2,1,0:T(8,128)(2,1)} %all-to-all-done) | data formatting | bytes 9437184 | tf_op jit(solution)/shard_map/reshape | solution.py:47
  151.8 5.8 %fusion.2 = f32[576,768]{1,0:T(8,128)} fusion(bf16[1,2048,768]{2,1,0:T(8,128)(2,1)} %all-gather.8.cloned.1.call-done, bf16[576,4096]{1,0:T(8,128)(2,1)} %reshape.43), kind=kOutput, calls=%fused_computation.7 | convolution fusion | flops 1811939328 | bytes 7274496 | tf_op jit(solution)/shard_map/dot_general | solution.py:50
  157.6 5.8 %fusion.6 = f32[576,768]{1,0:T(8,128)} fusion(bf16[1,2048,768]{2,1,0:T(8,128)(2,1)} %all-gather.6.cloned.1.call-done, bf16[576,4096]{1,0:T(8,128)(2,1)} %reshape.43), kind=kOutput, calls=%fused_computation.11 | convolution fusion | flops 1811939328 | bytes 7274496 | tf_op jit(solution)/shard_map/dot_general | solution.py:51
  163.4 6.1 %multiply_convert_fusion.2 = (bf16[576,768]{1,0:T(8,128)(2,1)S(1)}, bf16[576,768]{1,0:T(8,128)(2,1)S(1)}) fusion(f32[576,768]{1,0:T(8,128)} %fusion.2, f32[576,768]{1,0:T(8,128)} %fusion.6, bf16[1,768,2048]{2,1,0:T(8,128)(2,1)} %all-gather.4.cloned.1.call-done, bf16[576,4096]{1,0:T(8,128)(2,1)} %reshape.43), kind=kOutput, calls=%fused_computation.26 | convolution fusion | flops 1817690112 | bytes 10813440 | tf_op jit(solution)/shard_map/dot_general | solution.py:54
  169.5 8.9 %convolution_convert_fusion = bf16[2048,1536]{1,0:T(8,128)(2,1)} fusion(bf16[576,4096]{1,0:T(8,128)(2,1)} %reshape.43, bf16[576,768]{1,0:T(8,128)(2,1)S(1)} %get-tuple-element.4, bf16[576,768]{1,0:T(8,128)(2,1)S(1)} %get-tuple-element.5), kind=kOutput, calls=%fused_computation | convolution fusion | flops 3630563328 | bytes 10420224 | tf_op jit(solution)/shard_map/dot_general | solution.py:58
  178.4 0.0 reduce-scatter.3.cloned.1.call-update
  178.4 0.3 reduce-scatter.5.cloned.1.call-start
  178.7 7.1 %convolution_convert_fusion.1 = bf16[768,2048]{1,0:T(8,128)(2,1)} fusion(bf16[576,4096]{1,0:T(8,128)(2,1)} %reshape.43, f32[576,768]{1,0:T(8,128)} %fusion.6, f32[576,768]{1,0:T(8,128)} %fusion.2), kind=kOutput, calls=%fused_computation.4 | convolution fusion | flops 1816166400 | bytes 9043968 | tf_op jit(solution)/shard_map/dot_general | solution.py:59
  185.8 0.0 reduce-scatter.5.cloned.1.call-update
  185.8 0.0 copy-start.3
  185.8 4.1 %fusion = f32[576,2048]{1,0:T(8,128)S(1)} fusion(bf16[576,768]{1,0:T(8,128)(2,1)S(1)} %get-tuple-element.5, bf16[1,2048,768]{2,1,0:T(8,128)(2,1)} %all-gather.8.cloned.1.call-done), kind=kOutput, calls=%fused_computation.5 | convolution fusion | flops 1811939328 | bytes 8749056 | tf_op jit(solution)/shard_map/dot_general | solution.py:66
  189.9 0.0 copy-done.3
  189.9 3.5 %add_convert_fusion = bf16[576,2048]{1,0:T(8,128)(2,1)} fusion(f32[576,2048]{1,0:T(8,128)S(1)} %fusion, bf16[576,768]{1,0:T(8,128)(2,1)S(1)} %get-tuple-element.4, bf16[1,2048,768]{2,1,0:T(8,128)(2,1)S(1)} %copy-done.3), kind=kOutput, calls=%fused_computation.2 | convolution fusion | flops 1814298624 | bytes 11108352 | tf_op jit(solution)/shard_map/dot_general | solution.py:68
  193.4 3.7 %reshape_reshape.7 = bf16[64,144,128]{2,1,0:T(8,128)(2,1)S(1)} reshape(bf16[576,2048]{1,0:T(8,128)(2,1)} %add_convert_fusion) | data formatting | bytes 4718592 | tf_op jit(solution)/shard_map/reshape;reshape | solution.py:16
  197.1 66.3 %all_to_all.10 = bf16[64,144,128]{2,1,0:T(8,128)(2,1)} all-to-all(bf16[64,144,128]{2,1,0:T(8,128)(2,1)S(1)} %reshape_reshape.7), channel_id=1, replica_groups=mesh['expert'=64,'dp'=4] {'expert'}, dimensions={0} | all-to-all | bytes 4718592 | tf_op jit(solution)/shard_map/all_to_all | solution.py:17
  263.4 3.7 %reshape.44 = bf16[576,2048]{1,0:T(8,128)(2,1)S(1)} reshape(bf16[64,144,128]{2,1,0:T(8,128)(2,1)} %all_to_all.10) | data formatting | bytes 4718592 | tf_op jit(solution)/shard_map/reshape | solution.py:70
  267.1 1.4 convolution_convert_fusion.3
  268.5 2.6 slice_bitcast_fusion
  271.1 16.0 %reduce-scatter.5.cloned.1.call-done = bf16[192,2048]{1,0:T(8,128)(2,1)} async-done(((bf16[768,2048]{1,0:T(8,128)(2,1)}), bf16[192,2048]{1,0:T(8,128)(2,1)}) %reduce-scatter.5.cloned.1.call-update) | async-done | bytes 786448 | tf_op jit(solution)/shard_map/reduce_scatter | solution.py:60
  287.2 0.0 copy-done.1
  (8 shorter events, 0.1 us)
Async XLA Ops:
  7.2 5.3 %copy-start = (bf16[128,2048]{1,0:T(8,128)(2,1)S(1)}, bf16[128,2048]{1,0:T(8,128)(2,1)}, u32[]{:S(2)}) copy-start(bf16[128,2048]{1,0:T(8,128)(2,1)} %param.7) | copy-start | bytes 1572868
  7.2 144.6 %all-gather.8.cloned.1.call-start = ((), (), s32[]{:S(2)}) async-start(), calls=%async_computation.6 | async-start | bytes 3932160 | tf_op jit(solution)/shard_map/all_gather | solution.py:40
  7.2 6.0 %copy-start.2 = (bf16[128,2048]{1,0:T(8,128)(2,1)S(1)}, bf16[128,2048]{1,0:T(8,128)(2,1)}, u32[]{:S(2)}) copy-start(bf16[128,2048]{1,0:T(8,128)(2,1)} %param.8) | copy-start | bytes 1572868
  25.1 118.5 %all-to-all-start = ((bf16[64,288,128]{2,1,0:T(8,128)(2,1)}), bf16[64,288,128]{2,1,0:T(8,128)(2,1)}, u32[]{:S(2)}, u32[]{:S(2)}) async-start(bf16[64,288,128]{2,1,0:T(8,128)(2,1)} %reshape_reshape.6), calls=%async_computation | async-start | bytes 9437184 | tf_op jit(solution)/shard_map/all_to_all | solution.py:17
  38.3 119.3 %all-gather.6.cloned.1.call-start = ((), (), s32[]{:S(2)}) async-start(), calls=%async_computation.5 | async-start | bytes 3932160 | tf_op jit(solution)/shard_map/all_gather | solution.py:41
  39.1 124.3 %all-gather.4.cloned.1.call-start = ((), (), s32[]{:S(2)}) async-start(), calls=%async_computation.4 | async-start | bytes 3932160 | tf_op jit(solution)/shard_map/all_gather | solution.py:42
  39.8 228.7 %reduce-scatter.3.cloned.1.call-start = ((), (), s32[]{:S(2)}) async-start(), calls=%async_computation.7 | async-start | bytes 7864320 | tf_op jit(solution)/shard_map/reduce_scatter | solution.py:61
  178.4 108.7 %reduce-scatter.5.cloned.1.call-start = ((), (), s32[]{:S(2)}) async-start(), calls=%async_computation.8 | async-start | bytes 3932160 | tf_op jit(solution)/shard_map/reduce_scatter | solution.py:60
  185.8 4.1 %copy-start.3 = (bf16[1,2048,768]{2,1,0:T(8,128)(2,1)S(1)}, bf16[1,2048,768]{2,1,0:T(8,128)(2,1)}, u32[]{:S(2)}) copy-start(bf16[1,2048,768]{2,1,0:T(8,128)(2,1)} %all-gather.6.cloned.1.call-done) | copy-start | bytes 9437188
  263.4 23.8 %copy-start.1 = (bf16[128,2048]{1,0:T(8,128)(2,1)S(1)}, bf16[128,2048]{1,0:T(8,128)(2,1)}, u32[]{:S(2)}) copy-start(bf16[128,2048]{1,0:T(8,128)(2,1)} %param.7) | copy-start | bytes 1572868
Sparse Core Ops, SparseCore 0:
  9.8 45.9 all-gather.7
  57.6 42.3 all-gather.5
  101.8 42.3 all-gather.3
  178.6 64.9 reduce-scatter.2
  246.6 40.5 reduce-scatter.4

commit v6 on v5

--- a/solution.py
+++ b/solution.py
@@ -51,13 +51,13 @@
     pre_up = jnp.dot(rows, up_full, preferred_element_type=jnp.float32)
     act_value, act_slope = silu_parts(pre_gate)
     activ = (act_value * pre_up).astype(jnp.bfloat16)
+    part_down = jnp.dot(activ.T, scaled, preferred_element_type=jnp.float32).astype(jnp.bfloat16)
+    sum_down = lax.psum_scatter(part_down, "dp", scatter_dimension=0, tiled=True)
     grad_act = jnp.dot(scaled, down_full.T, preferred_element_type=jnp.float32)
     grad_pre_gate = (grad_act * pre_up * act_slope).astype(jnp.bfloat16)
     grad_pre_up = (grad_act * act_value).astype(jnp.bfloat16)
     grad_pre_both = jnp.concatenate([grad_pre_gate, grad_pre_up], axis=1)
     part_both = jnp.dot(rows.T, grad_pre_both, preferred_element_type=jnp.float32)
-    part_down = jnp.dot(activ.T, scaled, preferred_element_type=jnp.float32)
-    sum_down = lax.psum_scatter(part_down.astype(jnp.bfloat16), "dp", scatter_dimension=0, tiled=True)
     sum_both = lax.psum_scatter(part_both.astype(jnp.bfloat16), "dp", scatter_dimension=0, tiled=True)
     hidden = grad_pre_gate.shape[1]
     sum_gate = sum_both[:, :hidden][None]
@@ -67,6 +67,7 @@
     slot_grad = (
         slot_grad + jnp.dot(grad_pre_up, up_full.T, preferred_element_type=jnp.float32)
     ).astype(jnp.bfloat16)
+    sum_down, slot_grad = lax.optimization_barrier((sum_down, slot_grad))
     returned = exchange(slot_grad.reshape(owners, slot_cap, width)).reshape(owners * slot_cap, width)
     grad_tokens = lax.dot_general(
         select, returned, (((0,), (0,)), ((), ())), preferred_element_type=jnp.float32

time: 295 us -> 302 us (1.024)
  waiting for transfers between devices: 122 us -> 128 us
    reduce_scatter x1, waiting for transfers between devices: 16 us -> 22.2 us  [shards(): lax.psum_scatter(part_down, 'dp', scatter_dimension=0, tiled=True)]
where the time goes in v6:
time: 302 us
  waiting for transfers between devices  128 us (42%)
  blocking collectives  68.6 us (23%)
  matrix products  43.7 us (14%)
  local copies, waits for them, and re-layouts  28 us (9%)
  between operations  13.9 us (5%)
  starting transfers between devices  13.6 us (5%)
  other arithmetic  5.82 us (2%)
    all_to_all x1, waiting for transfers between devices, exchange(): lax.all_to_all(flat, 'expert', split_axis=0, concat_axis=0, tiled=True)  104 us
    all_to_all x1, blocking collectives, exchange(): lax.all_to_all(flat, 'expert', split_axis=0, concat_axis=0, tiled=True)  68.6 us
    reduce_scatter x1, waiting for transfers between devices, shards(): lax.psum_scatter(part_down, 'dp', scatter_dimension=0, tiled=True)  22.2 us
    all_to_all x1, starting transfers between devices, exchange(): lax.all_to_all(flat, 'expert', split_axis=0, concat_axis=0, tiled=True)  13.2 us
    another operation x2, local copies, waits for them, and re-layouts, exchange(): flat = block.reshape(owners, -1, LANES)  12 us
    dot_general x1, matrix products, shards(): jnp.dot(rows.T, grad_pre_both, preferred_element_type=jnp.float32)  8.92 us
    reshape x1, local copies, waits for them, and re-layouts, shards(): got_both = exchange(send_both).reshape(owners * slot_cap, 2 * width)  8.21 us
    dot_general x1, matrix products, shards(): pre_gate = jnp.dot(rows, gate_full, preferred_element_type=jnp.float32)  6.25 us
  transfers between devices with their start and end apart: 6, of which 2 were waited for; matrix products, arithmetic and copies ran while one was open for 21% of the time, Pallas kernels for 0%

profile of v6, /device:TPU:1, one launch (start us, length us, event | category | flops | bytes accessed | tf_op | source)
XLA Modules:
  0.0 301.5 jit_solution(6699683814241984474)
XLA Ops:
  7.2 0.0 copy-start
  7.2 0.0 all-gather.6.cloned.1.call-start
  7.2 0.0 copy-start.2
  7.2 0.7 all-gather.6.cloned.1.call-update
  7.9 0.8 copy.25
  8.7 0.1 eq.38
  8.8 0.1 eq.42
  8.9 1.2 reduce-window.6
  10.2 0.2 slice_reduce_fusion
  10.4 0.1 fusion.24
  10.6 0.1 reduce_sum.21
  10.7 0.1 copy.28
  10.7 0.7 multiply_add_fusion
  11.4 0.1 fusion.21
  11.6 0.9 select_reduce_fusion
  12.5 0.0 copy-done
  12.5 0.8 convolution_convert_fusion.2
  13.2 0.0 copy-done.2
  13.3 0.8 multiply_convert_fusion
  14.0 2.7 pad_maximum_fusion
  16.7 8.4 %reshape_reshape.6 = bf16[64,288,128]{2,1,0:T(8,128)(2,1)} reshape(bf16[576,4096]{1,0:T(8,128)(2,1)} %pad_maximum_fusion) | data formatting | bytes 9437184 | tf_op jit(solution)/shard_map/reshape;reshape | solution.py:16
  25.1 13.2 %all-to-all-start = ((bf16[64,288,128]{2,1,0:T(8,128)(2,1)}), bf16[64,288,128]{2,1,0:T(8,128)(2,1)}, u32[]{:S(2)}, u32[]{:S(2)}) async-start(bf16[64,288,128]{2,1,0:T(8,128)(2,1)} %reshape_reshape.6), calls=%async_computation | async-start | bytes 9437184 | tf_op jit(solution)/shard_map/all_to_all | solution.py:17
  38.3 0.0 all-gather.8.cloned.1.call-start
  38.3 0.7 all-gather.8.cloned.1.call-update
  39.0 0.0 all-gather.4.cloned.1.call-start
  39.1 0.7 all-gather.4.cloned.1.call-update
  39.8 0.0 reduce-scatter.3.cloned.1.call-start
  39.8 103.7 %all-to-all-done = bf16[64,288,128]{2,1,0:T(8,128)(2,1)} async-done(((bf16[64,288,128]{2,1,0:T(8,128)(2,1)}), bf16[64,288,128]{2,1,0:T(8,128)(2,1)}, u32[]{:S(2)}, u32[]{:S(2)}) %all-to-all-start) | async-done | bytes 4718624 | tf_op jit(solution)/shard_map/all_to_all | solution.py:17
  143.5 8.2 %reshape.43 = bf16[576,4096]{1,0:T(8,128)(2,1)} reshape(bf16[64,288,128]{2,1,0:T(8,128)(2,1)} %all-to-all-done) | data formatting | bytes 9437184 | tf_op jit(solution)/shard_map/reshape | solution.py:47
  151.8 5.8 %fusion.4 = f32[576,768]{1,0:T(8,128)} fusion(bf16[1,2048,768]{2,1,0:T(8,128)(2,1)} %all-gather.6.cloned.1.call-done, bf16[576,4096]{1,0:T(8,128)(2,1)} %reshape.43), kind=kOutput, calls=%fused_computation.9 | convolution fusion | flops 1811939328 | bytes 7274496 | tf_op jit(solution)/shard_map/dot_general | solution.py:51
  157.6 5.8 %fusion = f32[576,768]{1,0:T(8,128)} fusion(bf16[1,768,2048]{2,1,0:T(8,128)(2,1)} %all-gather.8.cloned.1.call-done, bf16[576,4096]{1,0:T(8,128)(2,1)} %reshape.43), kind=kOutput, calls=%fused_computation.5 | convolution fusion | flops 1811939328 | bytes 7274496 | tf_op jit(solution)/shard_map/dot_general | solution.py:56
  163.4 6.3 %multiply_convert_fusion.2 = (bf16[576,768]{1,0:T(8,128)(2,1)S(1)}, bf16[576,768]{1,0:T(8,128)(2,1)S(1)}, f32[576,768]{1,0:T(8,128)S(1)}) fusion(f32[576,768]{1,0:T(8,128)} %fusion, f32[576,768]{1,0:T(8,128)} %fusion.4, bf16[1,2048,768]{2,1,0:T(8,128)(2,1)} %all-gather.4.cloned.1.call-done, bf16[576,4096]{1,0:T(8,128)(2,1)} %reshape.43), kind=kOutput, calls=%fused_computation.26 | convolution fusion | flops 1817690112 | bytes 12582912 | tf_op jit(solution)/shard_map/dot_general | solution.py:50
  169.7 0.0 copy-done.4
  169.7 5.8 %convolution_convert_fusion.1 = bf16[768,2048]{1,0:T(8,128)(2,1)} fusion(bf16[576,4096]{1,0:T(8,128)(2,1)} %reshape.43, f32[576,768]{1,0:T(8,128)S(1)} %copy-done.4, f32[576,768]{1,0:T(8,128)S(1)} %get-tuple-element.12), kind=kOutput, calls=%fused_computation.4 | convolution fusion | flops 1816166400 | bytes 9043968 | tf_op jit(solution)/shard_map/dot_general | solution.py:54
  175.5 0.0 reduce-scatter.3.cloned.1.call-update
  175.5 0.2 reduce-scatter.5.cloned.1.call-start
  175.8 8.9 %convolution_convert_fusion = bf16[2048,1536]{1,0:T(8,128)(2,1)} fusion(bf16[576,4096]{1,0:T(8,128)(2,1)} %reshape.43, bf16[576,768]{1,0:T(8,128)(2,1)S(1)} %get-tuple-element.9, bf16[576,768]{1,0:T(8,128)(2,1)S(1)} %get-tuple-element.8), kind=kOutput, calls=%fused_computation | convolution fusion | flops 3630563328 | bytes 10420224 | tf_op jit(solution)/shard_map/dot_general | solution.py:60
  184.7 0.0 reduce-scatter.5.cloned.1.call-update
  184.7 0.0 copy-start.3
  184.7 4.6 %fusion.2 = f32[576,2048]{1,0:T(8,128)S(1)} fusion(bf16[576,768]{1,0:T(8,128)(2,1)S(1)} %get-tuple-element.9, bf16[1,2048,768]{2,1,0:T(8,128)(2,1)} %all-gather.6.cloned.1.call-done), kind=kOutput, calls=%fused_computation.7 | convolution fusion | flops 1811939328 | bytes 8749056 | tf_op jit(solution)/shard_map/dot_general | solution.py:68
  189.3 0.0 copy-done.3
  189.3 3.5 %add_convert_fusion = bf16[576,2048]{1,0:T(8,128)(2,1)} fusion(f32[576,2048]{1,0:T(8,128)S(1)} %fusion.2, bf16[576,768]{1,0:T(8,128)(2,1)S(1)} %get-tuple-element.8, bf16[1,2048,768]{2,1,0:T(8,128)(2,1)S(1)} %copy-done.3), kind=kOutput, calls=%fused_computation.2 | convolution fusion | flops 1814298624 | bytes 11108352 | tf_op jit(solution)/shard_map/dot_general | solution.py:66
  192.8 22.2 %reduce-scatter.3.cloned.1.call-done = bf16[192,2048]{1,0:T(8,128)(2,1)} async-done(((bf16[768,2048]{1,0:T(8,128)(2,1)}), bf16[192,2048]{1,0:T(8,128)(2,1)}) %reduce-scatter.3.cloned.1.call-update) | async-done | bytes 786448 | tf_op jit(solution)/shard_map/reduce_scatter | solution.py:55
  215.0 3.7 %reshape_reshape.7 = bf16[64,144,128]{2,1,0:T(8,128)(2,1)S(1)} reshape(bf16[576,2048]{1,0:T(8,128)(2,1)} %add_convert_fusion) | data formatting | bytes 4718592 | tf_op jit(solution)/shard_map/reshape;reshape | solution.py:16
  218.7 68.6 %all_to_all.10 = bf16[64,144,128]{2,1,0:T(8,128)(2,1)} all-to-all(bf16[64,144,128]{2,1,0:T(8,128)(2,1)S(1)} %reshape_reshape.7), channel_id=1, replica_groups=mesh['expert'=64,'dp'=4] {'expert'}, dimensions={0} | all-to-all | bytes 4718592 | tf_op jit(solution)/shard_map/all_to_all | solution.py:17
  287.2 3.7 %reshape.44 = bf16[576,2048]{1,0:T(8,128)(2,1)S(1)} reshape(bf16[64,144,128]{2,1,0:T(8,128)(2,1)} %all_to_all.10) | data formatting | bytes 4718592 | tf_op jit(solution)/shard_map/reshape | solution.py:71
  291.0 1.4 convolution_convert_fusion.3
  292.4 2.6 slice_bitcast_fusion
  (10 shorter events, 0.1 us)
Async XLA Ops:
  7.2 5.3 %copy-start = (bf16[128,2048]{1,0:T(8,128)(2,1)S(1)}, bf16[128,2048]{1,0:T(8,128)(2,1)}, u32[]{:S(2)}) copy-start(bf16[128,2048]{1,0:T(8,128)(2,1)} %param.7) | copy-start | bytes 1572868
  7.2 144.6 %all-gather.6.cloned.1.call-start = ((), (), s32[]{:S(2)}) async-start(), calls=%async_computation.5 | async-start | bytes 3932160 | tf_op jit(solution)/shard_map/all_gather | solution.py:41
  7.2 6.0 %copy-start.2 = (bf16[128,2048]{1,0:T(8,128)(2,1)S(1)}, bf16[128,2048]{1,0:T(8,128)(2,1)}, u32[]{:S(2)}) copy-start(bf16[128,2048]{1,0:T(8,128)(2,1)} %param.8) | copy-start | bytes 1572868
  25.1 118.4 %all-to-all-start = ((bf16[64,288,128]{2,1,0:T(8,128)(2,1)}), bf16[64,288,128]{2,1,0:T(8,128)(2,1)}, u32[]{:S(2)}, u32[]{:S(2)}) async-start(bf16[64,288,128]{2,1,0:T(8,128)(2,1)} %reshape_reshape.6), calls=%async_computation | async-start | bytes 9437184 | tf_op jit(solution)/shard_map/all_to_all | solution.py:17
  38.3 119.3 %all-gather.8.cloned.1.call-start = ((), (), s32[]{:S(2)}) async-start(), calls=%async_computation.7 | async-start | bytes 3932160 | tf_op jit(solution)/shard_map/all_gather | solution.py:42
  39.0 124.4 %all-gather.4.cloned.1.call-start = ((), (), s32[]{:S(2)}) async-start(), calls=%async_computation.4 | async-start | bytes 3932160 | tf_op jit(solution)/shard_map/all_gather | solution.py:40
  39.8 175.2 %reduce-scatter.3.cloned.1.call-start = ((), (), s32[]{:S(2)}) async-start(), calls=%async_computation.6 | async-start | bytes 3932160 | tf_op jit(solution)/shard_map/reduce_scatter | solution.py:55
  163.4 6.3 %copy-start.4 = (f32[576,768]{1,0:T(8,128)S(1)}, f32[576,768]{1,0:T(8,128)}, u32[]{:S(2)}) copy-start(f32[576,768]{1,0:T(8,128)} %fusion.4) | copy-start | bytes 5308420
  175.5 116.9 %reduce-scatter.5.cloned.1.call-start = ((), (), s32[]{:S(2)}) async-start(), calls=%async_computation.8 | async-start | bytes 7864320 | tf_op jit(solution)/shard_map/reduce_scatter | solution.py:61
  184.7 4.6 %copy-start.3 = (bf16[1,2048,768]{2,1,0:T(8,128)(2,1)S(1)}, bf16[1,2048,768]{2,1,0:T(8,128)(2,1)}, u32[]{:S(2)}) copy-start(bf16[1,2048,768]{2,1,0:T(8,128)(2,1)} %all-gather.4.cloned.1.call-done) | copy-start | bytes 9437188
  287.2 7.7 %copy-start.1 = (bf16[128,2048]{1,0:T(8,128)(2,1)S(1)}, bf16[128,2048]{1,0:T(8,128)(2,1)}, u32[]{:S(2)}) copy-start(bf16[128,2048]{1,0:T(8,128)(2,1)} %param.7) | copy-start | bytes 1572868
Sparse Core Ops, SparseCore 0:
  9.8 45.9 all-gather.5
  57.6 42.3 all-gather.7
  101.8 42.3 all-gather.3
  175.7 39.2 reduce-scatter.2
  217.4 66.2 reduce-scatter.4

commit v7 on v5

--- a/solution.py
+++ b/solution.py
@@ -1,9 +1,77 @@
 import jax
 import jax.numpy as jnp
 from jax import lax
+from jax.experimental import pallas as pl
+from jax.experimental.pallas import tpu as pltpu
 from jax.sharding import PartitionSpec as P
 
 LANES = 128
+XS = 4
+
+
+def _exchange_kernel(send_ref, recv_ref, send_sems, recv_sems, local_sem):
+    n = send_ref.shape[0]
+    me = lax.axis_index("expert")
+    group = lax.axis_index("dp")
+    local = pltpu.make_async_copy(send_ref.at[me], recv_ref.at[me], local_sem.at[0])
+    local.start()
+
+    def remote(peer, slot):
+        return pltpu.make_async_remote_copy(
+            src_ref=send_ref.at[peer],
+            dst_ref=recv_ref.at[slot],
+            send_sem=send_sems.at[peer],
+            recv_sem=recv_sems.at[slot],
+            device_id=(peer, group),
+            device_id_type=pl.DeviceIdType.MESH,
+        )
+
+    zs = n // (XS * 2)
+
+    def offset(k):
+        j = k % zs
+        dz = jnp.where(j % 2 == 0, j // 2, zs - (j + 1) // 2)
+        rest = k // zs
+        return dz, rest // 2, rest % 2
+
+    def peer_at(k, sign):
+        dz, dx, dc = offset(k)
+        z, x, c = me // (XS * 2), (me // 2) % XS, me % 2
+        pz = (z + sign * dz + zs) % zs
+        px = (x + sign * dx + XS) % XS
+        pc = (c + sign * dc + 2) % 2
+        return (pz * XS + px) * 2 + pc
+
+    def start(k, carry):
+        remote(peer_at(k, 1), me).start()
+        return carry
+
+    lax.fori_loop(1, n, start, 0)
+
+    def wait(k, carry):
+        remote(peer_at(k, 1), me).wait_send()
+        src = peer_at(k, -1)
+        remote(src, src).wait_recv()
+        return carry
+
+    lax.fori_loop(1, n, wait, 0)
+    local.wait()
+
+
+def exchange_kernel(x):
+    n = x.shape[0]
+    return pl.pallas_call(
+        _exchange_kernel,
+        out_shape=jax.ShapeDtypeStruct(x.shape, x.dtype),
+        in_specs=[pl.BlockSpec(memory_space=pl.ANY)],
+        out_specs=pl.BlockSpec(memory_space=pl.ANY),
+        scratch_shapes=[
+            pltpu.SemaphoreType.DMA((n,)),
+            pltpu.SemaphoreType.DMA((n,)),
+            pltpu.SemaphoreType.DMA((1,)),
+        ],
+        compiler_params=pltpu.CompilerParams(has_side_effects=True),
+    )(x)
 
 
 def silu_parts(pre_gate):
@@ -44,7 +112,8 @@
     gate_full = full_gate[0]
     up_full = full_up[0]
     down_full = full_down[0]
-    got_both = exchange(send_both).reshape(owners * slot_cap, 2 * width)
+    flat = send_both.reshape(owners, -1, LANES)
+    got_both = exchange_kernel(flat).reshape(owners * slot_cap, 2 * width)
     rows = got_both[:, :width]
     scaled = got_both[:, width:]
     pre_gate = jnp.dot(rows, gate_full, preferred_element_type=jnp.float32)

time: 295 us -> 299 us (1.014)
  Pallas kernels: 0 us -> 124 us
  waiting for transfers between devices: 122 us -> 17.1 us
  starting transfers between devices: 13.8 us -> 0.41 us
    pallas_call x0 -> x1, Pallas kernels: none -> 124 us  [exchange_kernel(): pl.pallas_call(_exchange_kernel, out_shape=jax.ShapeDtypeStruct(x.shape,...]
    all_to_all x1 -> x0, waiting for transfers between devices: 104 us -> none  [exchange(): lax.all_to_all(flat, 'expert', split_axis=0, concat_axis=0, tiled=True)]
    all_to_all x1 -> x0, starting transfers between devices: 13.2 us -> none  [exchange(): lax.all_to_all(flat, 'expert', split_axis=0, concat_axis=0, tiled=True)]
    another operation x2 -> x1, local copies, waits for them, and re-layouts: 12.1 us -> 3.7 us  [exchange(): flat = block.reshape(owners, -1, LANES)]
    another operation x1 -> x2, local copies, waits for them, and re-layouts: 0.01 us -> 8.28 us  [the longest x1 8.28 us: shards(): flat = send_both.reshape(owners, -1, LANES)]
  transfers between devices with their start and end apart: 6 -> 5, of which waited for: 2 -> 1; matrix products, arithmetic and copies ran while one was open for 21% -> 21% of each run, Pallas kernels for 0% -> 42%
where the time goes in v7:
time: 299 us
  Pallas kernels  124 us (41%)
  blocking collectives  66.2 us (22%)
  matrix products  44.7 us (15%)
  local copies, waits for them, and re-layouts  27.3 us (9%)
  waiting for transfers between devices  17.1 us (6%)
  between operations  13.9 us (5%)
  other arithmetic  4.47 us (1%)
    pallas_call x1, Pallas kernels, exchange_kernel(): pl.pallas_call(_exchange_kernel, out_shape=jax.ShapeDtypeStruct(x.shape,...  124 us
    all_to_all x1, blocking collectives, exchange(): lax.all_to_all(flat, 'expert', split_axis=0, concat_axis=0, tiled=True)  66.2 us
    reduce_scatter x1, waiting for transfers between devices, shards(): lax.psum_scatter(part_down.astype(jnp.bfloat16), 'dp', scatter_dimension=...  15 us
    dot_general x1, matrix products, shards(): jnp.dot(rows.T, grad_pre_both, preferred_element_type=jnp.float32)  8.99 us
    another operation x1, local copies, waits for them, and re-layouts, shards(): flat = send_both.reshape(owners, -1, LANES)  8.28 us
    reshape x1, local copies, waits for them, and re-layouts, shards(): got_both = exchange_kernel(flat).reshape(owners * slot_cap, 2 * width)  8.2 us
    dot_general x1, matrix products, shards(): part_down = jnp.dot(activ.T, scaled, preferred_element_type=jnp.float32)  7.1 us
    dot_general x1, matrix products, shards(): grad_act = jnp.dot(scaled, down_full.T, preferred_element_type=jnp.float32)  6.12 us
  transfers between devices with their start and end apart: 5, of which 1 were waited for; matrix products, arithmetic and copies ran while one was open for 21% of the time, Pallas kernels for 42%

profile of v7, /device:TPU:1, one launch (start us, length us, event | category | flops | bytes accessed | tf_op | source)
XLA Modules:
  0.0 298.6 jit_solution(17525913966513554131)
XLA Ops:
  7.2 0.0 copy-start
  7.2 0.0 copy-start.3
  7.2 0.0 copy-start.4
  7.2 0.0 all-gather.8.cloned.1.call-start
  7.2 0.7 all-gather.8.cloned.1.call-update
  7.9 0.0 all-gather.6.cloned.1.call-start
  8.0 0.7 all-gather.6.cloned.1.call-update
  8.7 0.0 copy-start.2
  8.7 0.0 all-gather.4.cloned.1.call-start
  8.7 0.7 all-gather.4.cloned.1.call-update
  9.4 0.0 reduce-scatter.3.cloned.1.call-start
  9.5 0.0 copy-done.3
  9.5 0.1 copy.25
  9.6 0.1 eq.42
  9.7 0.1 eq.38
  9.8 1.2 reduce-window.6
  11.0 0.2 slice_reduce_fusion
  11.3 0.1 fusion.24
  11.4 0.1 reduce_sum.21
  11.6 0.1 copy.28
  11.6 0.2 fusion.21
  11.8 0.0 copy-done.4
  11.8 0.2 select_reduce_fusion
  12.0 0.0 copy-done
  12.0 0.8 convolution_convert_fusion.2
  12.8 0.0 copy-done.2
  12.8 0.8 multiply_convert_fusion
  13.6 2.7 pad_maximum_fusion
  16.3 8.3 %reshape_reshape.6.send_ref = bf16[64,288,128]{2,1,0:T(8,128)(2,1)} reshape(bf16[576,4096]{1,0:T(8,128)(2,1)} %pad_maximum_fusion) | data formatting | bytes 9437184 | tf_op jit(solution)/shard_map/reshape;reshape | solution.py:115
  24.6 124.5 %shard_map.102 = bf16[64,288,128]{2,1,0:T(8,128)(2,1)} custom-call(bf16[64,288,128]{2,1,0:T(8,128)(2,1)} %reshape_reshape.6.send_ref), custom_call_target="tpu_custom_call" | custom-call | tf_op jit(solution)/shard_map/pallas_call | solution.py:63
  149.1 8.2 %reshape.43 = bf16[576,4096]{1,0:T(8,128)(2,1)} reshape(bf16[64,288,128]{2,1,0:T(8,128)(2,1)} %shard_map.102) | data formatting | bytes 9437184 | tf_op jit(solution)/shard_map/reshape | solution.py:116
  157.3 5.9 %fusion.2 = f32[576,768]{1,0:T(8,128)} fusion(bf16[1,2048,768]{2,1,0:T(8,128)(2,1)} %all-gather.8.cloned.1.call-done, bf16[576,4096]{1,0:T(8,128)(2,1)} %reshape.43), kind=kOutput, calls=%fused_computation.7 | convolution fusion | flops 1811939328 | bytes 7274496 | tf_op jit(solution)/shard_map/dot_general | solution.py:119
  163.1 5.9 %fusion.6 = f32[576,768]{1,0:T(8,128)} fusion(bf16[1,2048,768]{2,1,0:T(8,128)(2,1)} %all-gather.6.cloned.1.call-done, bf16[576,4096]{1,0:T(8,128)(2,1)} %reshape.43), kind=kOutput, calls=%fused_computation.11 | convolution fusion | flops 1811939328 | bytes 7274496 | tf_op jit(solution)/shard_map/dot_general | solution.py:120
  169.0 6.1 %multiply_convert_fusion.2 = (bf16[576,768]{1,0:T(8,128)(2,1)S(1)}, bf16[576,768]{1,0:T(8,128)(2,1)S(1)}) fusion(f32[576,768]{1,0:T(8,128)} %fusion.2, f32[576,768]{1,0:T(8,128)} %fusion.6, bf16[1,768,2048]{2,1,0:T(8,128)(2,1)} %all-gather.4.cloned.1.call-done, bf16[576,4096]{1,0:T(8,128)(2,1)} %reshape.43), kind=kOutput, calls=%fused_computation.26 | convolution fusion | flops 1817690112 | bytes 10813440 | tf_op jit(solution)/shard_map/dot_general | solution.py:123
  175.1 9.0 %convolution_convert_fusion = bf16[2048,1536]{1,0:T(8,128)(2,1)} fusion(bf16[576,4096]{1,0:T(8,128)(2,1)} %reshape.43, bf16[576,768]{1,0:T(8,128)(2,1)S(1)} %get-tuple-element.4, bf16[576,768]{1,0:T(8,128)(2,1)S(1)} %get-tuple-element.5), kind=kOutput, calls=%fused_computation | convolution fusion | flops 3630563328 | bytes 10420224 | tf_op jit(solution)/shard_map/dot_general | solution.py:127
  184.1 0.0 reduce-scatter.3.cloned.1.call-update
  184.1 0.3 reduce-scatter.5.cloned.1.call-start
  184.4 7.1 %convolution_convert_fusion.1 = bf16[768,2048]{1,0:T(8,128)(2,1)} fusion(bf16[576,4096]{1,0:T(8,128)(2,1)} %reshape.43, f32[576,768]{1,0:T(8,128)} %fusion.6, f32[576,768]{1,0:T(8,128)} %fusion.2), kind=kOutput, calls=%fused_computation.4 | convolution fusion | flops 1816166400 | bytes 9043968 | tf_op jit(solution)/shard_map/dot_general | solution.py:128
  191.5 0.0 reduce-scatter.5.cloned.1.call-update
  191.6 4.3 %fusion = f32[576,2048]{1,0:T(8,128)S(1)} fusion(bf16[576,768]{1,0:T(8,128)(2,1)S(1)} %get-tuple-element.5, bf16[1,2048,768]{2,1,0:T(8,128)(2,1)} %all-gather.8.cloned.1.call-done), kind=kOutput, calls=%fused_computation.5 | convolution fusion | flops 1811939328 | bytes 8749056 | tf_op jit(solution)/shard_map/dot_general | solution.py:135
  195.9 0.0 copy-done.5
  195.9 3.5 %add_convert_fusion = bf16[576,2048]{1,0:T(8,128)(2,1)} fusion(f32[576,2048]{1,0:T(8,128)S(1)} %fusion, bf16[576,768]{1,0:T(8,128)(2,1)S(1)} %get-tuple-element.4, bf16[1,2048,768]{2,1,0:T(8,128)(2,1)S(1)} %copy-done.5), kind=kOutput, calls=%fused_computation.2 | convolution fusion | flops 1814298624 | bytes 11108352 | tf_op jit(solution)/shard_map/dot_general | solution.py:137
  199.4 3.7 %reshape_reshape.7 = bf16[64,144,128]{2,1,0:T(8,128)(2,1)S(1)} reshape(bf16[576,2048]{1,0:T(8,128)(2,1)} %add_convert_fusion) | data formatting | bytes 4718592 | tf_op jit(solution)/shard_map/reshape;reshape | solution.py:84
  203.1 66.2 %all_to_all.5 = bf16[64,144,128]{2,1,0:T(8,128)(2,1)} all-to-all(bf16[64,144,128]{2,1,0:T(8,128)(2,1)S(1)} %reshape_reshape.7), channel_id=1, replica_groups=mesh['expert'=64,'dp'=4] {'expert'}, dimensions={0} | all-to-all | bytes 4718592 | tf_op jit(solution)/shard_map/all_to_all | solution.py:85
  269.3 3.7 %reshape.44 = bf16[576,2048]{1,0:T(8,128)(2,1)S(1)} reshape(bf16[64,144,128]{2,1,0:T(8,128)(2,1)} %all_to_all.5) | data formatting | bytes 4718592 | tf_op jit(solution)/shard_map/reshape | solution.py:139
  273.0 1.4 convolution_convert_fusion.3
  274.4 2.7 slice_bitcast_fusion
  277.1 15.0 %reduce-scatter.5.cloned.1.call-done = bf16[192,2048]{1,0:T(8,128)(2,1)} async-done(((bf16[768,2048]{1,0:T(8,128)(2,1)}), bf16[192,2048]{1,0:T(8,128)(2,1)}) %reduce-scatter.5.cloned.1.call-update) | async-done | bytes 786448 | tf_op jit(solution)/shard_map/reduce_scatter | solution.py:129
  (11 shorter events, 0.1 us)
Async XLA Ops:
  7.2 4.9 %copy-start = (bf16[128,2048]{1,0:T(8,128)(2,1)S(1)}, bf16[128,2048]{1,0:T(8,128)(2,1)}, u32[]{:S(2)}) copy-start(bf16[128,2048]{1,0:T(8,128)(2,1)} %param.7) | copy-start | bytes 1572868
  7.2 2.3 copy-start.3
  7.2 4.6 %copy-start.4 = (f32[128,4]{0,1:T(4,128)S(1)}, f32[128,4]{0,1:T(4,128)}, u32[]{:S(2)}) copy-start(f32[128,4]{0,1:T(4,128)} %param.10) | copy-start | bytes 6148
  7.2 150.1 %all-gather.8.cloned.1.call-start = ((), (), s32[]{:S(2)}) async-start(), calls=%async_computation.5 | async-start | bytes 3932160 | tf_op jit(solution)/shard_map/all_gather | solution.py:108
  7.9 155.2 %all-gather.6.cloned.1.call-start = ((), (), s32[]{:S(2)}) async-start(), calls=%async_computation.4 | async-start | bytes 3932160 | tf_op jit(solution)/shard_map/all_gather | solution.py:109
  8.7 4.1 %copy-start.2 = (bf16[128,2048]{1,0:T(8,128)(2,1)S(1)}, bf16[128,2048]{1,0:T(8,128)(2,1)}, u32[]{:S(2)}) copy-start(bf16[128,2048]{1,0:T(8,128)(2,1)} %param.8) | copy-start | bytes 1572868
  8.7 160.3 %all-gather.4.cloned.1.call-start = ((), (), s32[]{:S(2)}) async-start(), calls=%async_computation.3 | async-start | bytes 3932160 | tf_op jit(solution)/shard_map/all_gather | solution.py:110
  9.4 265.0 %reduce-scatter.3.cloned.1.call-start = ((), (), s32[]{:S(2)}) async-start(), calls=%async_computation.6 | async-start | bytes 7864320 | tf_op jit(solution)/shard_map/reduce_scatter | solution.py:130
  184.1 107.9 %reduce-scatter.5.cloned.1.call-start = ((), (), s32[]{:S(2)}) async-start(), calls=%async_computation.7 | async-start | bytes 3932160 | tf_op jit(solution)/shard_map/reduce_scatter | solution.py:129
  191.5 4.3 %copy-start.5 = (bf16[1,2048,768]{2,1,0:T(8,128)(2,1)S(1)}, bf16[1,2048,768]{2,1,0:T(8,128)(2,1)}, u32[]{:S(2)}) copy-start(bf16[1,2048,768]{2,1,0:T(8,128)(2,1)} %all-gather.6.cloned.1.call-done) | copy-start | bytes 9437188
  269.3 22.8 %copy-start.1 = (bf16[128,2048]{1,0:T(8,128)(2,1)S(1)}, bf16[128,2048]{1,0:T(8,128)(2,1)}, u32[]{:S(2)}) copy-start(bf16[128,2048]{1,0:T(8,128)(2,1)} %param.7) | copy-start | bytes 1572868
Sparse Core Ops, SparseCore 0:
  9.8 45.9 all-gather.7
  57.6 42.3 all-gather.5
  101.8 42.3 all-gather.3
  184.3 64.1 reduce-scatter.2
  251.5 40.5 reduce-scatter.4

commit v8 on v5

--- a/solution.py
+++ b/solution.py
@@ -1,9 +1,94 @@
 import jax
 import jax.numpy as jnp
 from jax import lax
+from jax.experimental import pallas as pl
+from jax.experimental.pallas import tpu as pltpu
 from jax.sharding import PartitionSpec as P
 
 LANES = 128
+
+
+def _return_kernel(send_ref, down_ref, recv_ref, down_out, send_sems, recv_sems, y_send, y_recv, local_sems):
+    n = send_ref.shape[0]
+    groups = down_ref.shape[0]
+    me = lax.axis_index("expert")
+    group = lax.axis_index("dp")
+    local = pltpu.make_async_copy(send_ref.at[me], recv_ref.at[me], local_sems.at[0])
+    local.start()
+    local_down = pltpu.make_async_copy(down_ref.at[group], down_out.at[group], local_sems.at[1])
+    local_down.start()
+
+    def remote(peer, slot):
+        return pltpu.make_async_remote_copy(
+            src_ref=send_ref.at[peer],
+            dst_ref=recv_ref.at[slot],
+            send_sem=send_sems.at[peer],
+            recv_sem=recv_sems.at[slot],
+            device_id=(peer, group),
+            device_id_type=pl.DeviceIdType.MESH,
+        )
+
+    def across(target, slot):
+        return pltpu.make_async_remote_copy(
+            src_ref=down_ref.at[target],
+            dst_ref=down_out.at[slot],
+            send_sem=y_send.at[target],
+            recv_sem=y_recv.at[slot],
+            device_id=(me, target),
+            device_id_type=pl.DeviceIdType.MESH,
+        )
+
+    def start_y(k, carry):
+        across(lax.rem(group + k, groups), group).start()
+        return carry
+
+    lax.fori_loop(1, groups, start_y, 0)
+
+    def start(i, carry):
+        remote(lax.rem(me + i, n), me).start()
+        return carry
+
+    lax.fori_loop(1, n, start, 0)
+
+    def wait_y(k, carry):
+        across(lax.rem(group + k, groups), group).wait_send()
+        src = lax.rem(group - k + groups, groups)
+        across(src, src).wait_recv()
+        return carry
+
+    lax.fori_loop(1, groups, wait_y, 0)
+
+    def wait(i, carry):
+        remote(lax.rem(me + i, n), me).wait_send()
+        src = lax.rem(me - i + n, n)
+        remote(src, src).wait_recv()
+        return carry
+
+    lax.fori_loop(1, n, wait, 0)
+    local.wait()
+    local_down.wait()
+
+
+def return_and_reduce(blocks, down_parts):
+    n = blocks.shape[0]
+    groups = down_parts.shape[0]
+    return pl.pallas_call(
+        _return_kernel,
+        out_shape=(
+            jax.ShapeDtypeStruct(blocks.shape, blocks.dtype),
+            jax.ShapeDtypeStruct(down_parts.shape, down_parts.dtype),
+        ),
+        in_specs=[pl.BlockSpec(memory_space=pl.ANY)] * 2,
+        out_specs=(pl.BlockSpec(memory_space=pl.ANY), pl.BlockSpec(memory_space=pl.ANY)),
+        scratch_shapes=[
+            pltpu.SemaphoreType.DMA((n,)),
+            pltpu.SemaphoreType.DMA((n,)),
+            pltpu.SemaphoreType.DMA((groups,)),
+            pltpu.SemaphoreType.DMA((groups,)),
+            pltpu.SemaphoreType.DMA((2,)),
+        ],
+        compiler_params=pltpu.CompilerParams(has_side_effects=True),
+    )(blocks, down_parts)
 
 
 def silu_parts(pre_gate):
@@ -56,18 +141,20 @@
     grad_pre_up = (grad_act * act_value).astype(jnp.bfloat16)
     grad_pre_both = jnp.concatenate([grad_pre_gate, grad_pre_up], axis=1)
     part_both = jnp.dot(rows.T, grad_pre_both, preferred_element_type=jnp.float32)
-    part_down = jnp.dot(activ.T, scaled, preferred_element_type=jnp.float32)
-    sum_down = lax.psum_scatter(part_down.astype(jnp.bfloat16), "dp", scatter_dimension=0, tiled=True)
+    part_down = jnp.dot(activ.T, scaled, preferred_element_type=jnp.float32).astype(jnp.bfloat16)
     sum_both = lax.psum_scatter(part_both.astype(jnp.bfloat16), "dp", scatter_dimension=0, tiled=True)
     hidden = grad_pre_gate.shape[1]
     sum_gate = sum_both[:, :hidden][None]
     sum_up = sum_both[:, hidden:][None]
-    sum_down = sum_down[None]
     slot_grad = jnp.dot(grad_pre_gate, gate_full.T, preferred_element_type=jnp.float32)
     slot_grad = (
         slot_grad + jnp.dot(grad_pre_up, up_full.T, preferred_element_type=jnp.float32)
     ).astype(jnp.bfloat16)
-    returned = exchange(slot_grad.reshape(owners, slot_cap, width)).reshape(owners * slot_cap, width)
+    returned, down_parts = return_and_reduce(
+        slot_grad.reshape(owners, -1, LANES), part_down.reshape(groups, -1, part_down.shape[1])
+    )
+    returned = returned.reshape(owners * slot_cap, width)
+    sum_down = jnp.sum(down_parts.astype(jnp.float32), axis=0).astype(jnp.bfloat16)[None]
     grad_tokens = lax.dot_general(
         select, returned, (((0,), (0,)), ((), ())), preferred_element_type=jnp.float32
     ).astype(jnp.bfloat16)

time: 295 us -> 296 us (level)
  Pallas kernels: 0 us -> 81.9 us
  blocking collectives: 66.3 us -> 0 us
  waiting for transfers between devices: 122 us -> 106 us
  other arithmetic: 5.82 us -> 9.46 us
    pallas_call x0 -> x1, Pallas kernels: none -> 81.9 us  [return_and_reduce(): pl.pallas_call(_return_kernel, out_shape=(jax.ShapeDtypeStruct(blocks.sha...]
    all_to_all x1 -> x0, blocking collectives: 66.3 us -> none  [exchange(): lax.all_to_all(flat, 'expert', split_axis=0, concat_axis=0, tiled=True)]
    reduce_scatter x1 -> x0, waiting for transfers between devices: 16 us -> none  [shards(): lax.psum_scatter(part_down.astype(jnp.bfloat16), 'dp', scatter_dimension=...]
    another operation x2 -> x1, local copies, waits for them, and re-layouts: 12.1 us -> 8.28 us  [exchange(): flat = block.reshape(owners, -1, LANES)]
    reduce_sum x0 -> x1, other arithmetic: none -> 3.64 us  [shards(): jnp.sum(down_parts.astype(jnp.float32), axis=0).astype(jnp.bfloat16)[None]]
    reshape x1 -> x2, local copies, waits for them, and re-layouts: 3.72 us -> 6.15 us  [the longest x1 3.65 us: shards(): returned = returned.reshape(owners * slot_cap, width)]
  transfers between devices with their start and end apart: 6 -> 5, of which waited for: 2 -> 1; matrix products, arithmetic and copies ran while one was open for 21% -> 21% of each run, Pallas kernels for 0% -> 28%
where the time goes in v8:
time: 296 us; the launch traced here: 295 us
  waiting for transfers between devices  106 us (36%)
  Pallas kernels  81.9 us (28%)
  matrix products  44.3 us (15%)
  local copies, waits for them, and re-layouts  26.7 us (9%)
  between operations  13.9 us (5%)
  starting transfers between devices  13.5 us (5%)
  other arithmetic  9.46 us (3%)
    all_to_all x1, waiting for transfers between devices, exchange(): lax.all_to_all(flat, 'expert', split_axis=0, concat_axis=0, tiled=True)  104 us
    pallas_call x1, Pallas kernels, return_and_reduce(): pl.pallas_call(_return_kernel, out_shape=(jax.ShapeDtypeStruct(blocks.sha...  81.9 us
    all_to_all x1, starting transfers between devices, exchange(): lax.all_to_all(flat, 'expert', split_axis=0, concat_axis=0, tiled=True)  13.2 us
    dot_general x1, matrix products, shards(): jnp.dot(rows.T, grad_pre_both, preferred_element_type=jnp.float32)  9.2 us
    another operation x1, local copies, waits for them, and re-layouts, exchange(): flat = block.reshape(owners, -1, LANES)  8.28 us
    dot_general x1, matrix products, shards(): jnp.dot(activ.T, scaled, preferred_element_type=jnp.float32)  8.27 us
    reshape x1, local copies, waits for them, and re-layouts, shards(): got_both = exchange(send_both).reshape(owners * slot_cap, 2 * width)  8.19 us
    dot_general x1, matrix products, shards(): grad_act = jnp.dot(scaled, down_full.T, preferred_element_type=jnp.float32)  6.12 us
  transfers between devices with their start and end apart: 5, of which 1 were waited for; matrix products, arithmetic and copies ran while one was open for 21% of the time, Pallas kernels for 28%

profile of v8, /device:TPU:1, one launch (start us, length us, event | category | flops | bytes accessed | tf_op | source)
XLA Modules:
  0.0 295.4 jit_solution(544517684976696557)
XLA Ops:
  7.2 0.0 copy-start
  7.2 0.0 all-gather.8.cloned.1.call-start
  7.2 0.0 copy-start.2
  7.2 0.7 all-gather.8.cloned.1.call-update
  7.9 0.8 copy.25
  8.7 0.1 eq.38
  8.8 0.1 eq.42
  8.9 1.2 reduce-window.6
  10.2 0.2 slice_reduce_fusion
  10.4 0.1 fusion.24
  10.6 0.1 reduce_sum.33
  10.7 0.1 copy.28
  10.7 0.7 multiply_add_fusion
  11.4 0.1 fusion.21
  11.6 0.9 select_reduce_fusion
  12.5 0.0 copy-done
  12.5 0.8 convolution_convert_fusion.2
  13.2 0.0 copy-done.2
  13.3 0.8 multiply_convert_fusion
  14.0 2.7 pad_maximum_fusion
  16.7 8.3 %reshape_reshape.3 = bf16[64,288,128]{2,1,0:T(8,128)(2,1)} reshape(bf16[576,4096]{1,0:T(8,128)(2,1)} %pad_maximum_fusion) | data formatting | bytes 9437184 | tf_op jit(solution)/shard_map/reshape;reshape | solution.py:101
  25.0 13.2 %all-to-all-start = ((bf16[64,288,128]{2,1,0:T(8,128)(2,1)}), bf16[64,288,128]{2,1,0:T(8,128)(2,1)}, u32[]{:S(2)}, u32[]{:S(2)}) async-start(bf16[64,288,128]{2,1,0:T(8,128)(2,1)} %reshape_reshape.3), calls=%async_computation | async-start | bytes 9437184 | tf_op jit(solution)/shard_map/all_to_all | solution.py:102
  38.2 0.0 all-gather.6.cloned.1.call-start
  38.3 0.7 all-gather.6.cloned.1.call-update
  39.0 0.0 all-gather.4.cloned.1.call-start
  39.0 0.7 all-gather.4.cloned.1.call-update
  39.7 0.2 reduce-scatter.2.cloned.1.call-start
  39.9 103.5 %all-to-all-done = bf16[64,288,128]{2,1,0:T(8,128)(2,1)} async-done(((bf16[64,288,128]{2,1,0:T(8,128)(2,1)}), bf16[64,288,128]{2,1,0:T(8,128)(2,1)}, u32[]{:S(2)}, u32[]{:S(2)}) %all-to-all-start) | async-done | bytes 4718624 | tf_op jit(solution)/shard_map/all_to_all | solution.py:102
  143.5 8.2 %reshape.49 = bf16[576,4096]{1,0:T(8,128)(2,1)} reshape(bf16[64,288,128]{2,1,0:T(8,128)(2,1)} %all-to-all-done) | data formatting | bytes 9437184 | tf_op jit(solution)/shard_map/reshape | solution.py:132
  151.7 5.8 %fusion.2 = f32[576,768]{1,0:T(8,128)} fusion(bf16[1,2048,768]{2,1,0:T(8,128)(2,1)} %all-gather.8.cloned.1.call-done, bf16[576,4096]{1,0:T(8,128)(2,1)} %reshape.49), kind=kOutput, calls=%fused_computation.7 | convolution fusion | flops 1811939328 | bytes 7274496 | tf_op jit(solution)/shard_map/dot_general | solution.py:135
  157.5 5.8 %fusion.6 = f32[576,768]{1,0:T(8,128)} fusion(bf16[1,2048,768]{2,1,0:T(8,128)(2,1)} %all-gather.6.cloned.1.call-done, bf16[576,4096]{1,0:T(8,128)(2,1)} %reshape.49), kind=kOutput, calls=%fused_computation.11 | convolution fusion | flops 1811939328 | bytes 7274496 | tf_op jit(solution)/shard_map/dot_general | solution.py:136
  163.3 6.1 %multiply_convert_fusion.2 = (bf16[576,768]{1,0:T(8,128)(2,1)S(1)}, bf16[576,768]{1,0:T(8,128)(2,1)S(1)}) fusion(f32[576,768]{1,0:T(8,128)} %fusion.2, f32[576,768]{1,0:T(8,128)} %fusion.6, bf16[1,768,2048]{2,1,0:T(8,128)(2,1)} %all-gather.4.cloned.1.call-done, bf16[576,4096]{1,0:T(8,128)(2,1)} %reshape.49), kind=kOutput, calls=%fused_computation.26 | convolution fusion | flops 1817690112 | bytes 10813440 | tf_op jit(solution)/shard_map/dot_general | solution.py:139
  169.4 0.0 copy-start.4
  169.5 9.2 %convolution_convert_fusion = bf16[2048,1536]{1,0:T(8,128)(2,1)} fusion(bf16[576,4096]{1,0:T(8,128)(2,1)} %reshape.49, bf16[576,768]{1,0:T(8,128)(2,1)S(1)} %get-tuple-element.8, bf16[576,768]{1,0:T(8,128)(2,1)S(1)} %get-tuple-element.9), kind=kOutput, calls=%fused_computation | convolution fusion | flops 3630563328 | bytes 10420224 | tf_op jit(solution)/shard_map/dot_general | solution.py:143
  178.7 0.0 copy-done.4
  178.7 0.0 reduce-scatter.2.cloned.1.call-update
  178.7 4.1 %fusion = f32[576,2048]{1,0:T(8,128)S(1)} fusion(bf16[576,768]{1,0:T(8,128)(2,1)S(1)} %get-tuple-element.9, bf16[1,2048,768]{2,1,0:T(8,128)(2,1)} %all-gather.8.cloned.1.call-done), kind=kOutput, calls=%fused_computation.5 | convolution fusion | flops 1811939328 | bytes 8749056 | tf_op jit(solution)/shard_map/dot_general | solution.py:149
  182.8 0.0 copy-done.3
  182.8 0.0 copy-done.5
  182.8 2.0 add_convert_fusion
  184.8 2.5 reshape.50.send_ref
  187.3 8.3 %convolution_convert_fusion.1 = bf16[768,2048]{1,0:T(8,128)(2,1)} fusion(bf16[576,4096]{1,0:T(8,128)(2,1)} %reshape.49, f32[576,768]{1,0:T(8,128)} %fusion.6, f32[576,768]{1,0:T(8,128)} %fusion.2), kind=kOutput, calls=%fused_computation.4 | convolution fusion | flops 1816166400 | bytes 9043968 | tf_op jit(solution)/shard_map/dot_general | solution.py:144
  195.6 81.9 %shard_map.102 = (bf16[64,144,128]{2,1,0:T(8,128)(2,1)}, bf16[4,192,2048]{2,1,0:T(8,128)(2,1)}) custom-call(bf16[64,144,128]{2,1,0:T(8,128)(2,1)} %reshape.50.send_ref, bf16[4,192,2048]{2,1,0:T(8,128)(2,1)} %bitcast.46), custom_call_target="tpu_custom_call" | custom-call | tf_op jit(solution)/shard_map/pallas_call | solution.py:75
  277.5 3.7 %reshape.52 = bf16[576,2048]{1,0:T(8,128)(2,1)S(1)} reshape(bf16[64,144,128]{2,1,0:T(8,128)(2,1)} %get-tuple-element.6) | data formatting | bytes 4718592 | tf_op jit(solution)/shard_map/reshape | solution.py:156
  281.2 0.0 copy-start.1
  281.2 3.6 %reduce_sum.35 = bf16[192,2048]{1,0:T(8,128)(2,1)} reduce(bf16[4,192,2048]{2,1,0:T(8,128)(2,1)} %get-tuple-element.7, bf16[]{:T(256)} %constant.18.clone.1), dimensions={0}, to_apply=%region_6.7 | reduce | flops 1179648 | bytes 3932162 | tf_op jit(solution)/shard_map/reduce_sum | solution.py:157
  284.8 1.4 convolution_convert_fusion.3
  286.3 2.6 slice_bitcast_fusion
  (10 shorter events, 0.1 us)
Async XLA Ops:
  7.2 5.3 %copy-start = (bf16[128,2048]{1,0:T(8,128)(2,1)S(1)}, bf16[128,2048]{1,0:T(8,128)(2,1)}, u32[]{:S(2)}) copy-start(bf16[128,2048]{1,0:T(8,128)(2,1)} %param.7) | copy-start | bytes 1572868
  7.2 144.5 %all-gather.8.cloned.1.call-start = ((), (), s32[]{:S(2)}) async-start(), calls=%async_computation.4 | async-start | bytes 3932160 | tf_op jit(solution)/shard_map/all_gather | solution.py:125
  7.2 6.0 %copy-start.2 = (bf16[128,2048]{1,0:T(8,128)(2,1)S(1)}, bf16[128,2048]{1,0:T(8,128)(2,1)}, u32[]{:S(2)}) copy-start(bf16[128,2048]{1,0:T(8,128)(2,1)} %param.8) | copy-start | bytes 1572868
  25.0 118.4 %all-to-all-start = ((bf16[64,288,128]{2,1,0:T(8,128)(2,1)}), bf16[64,288,128]{2,1,0:T(8,128)(2,1)}, u32[]{:S(2)}, u32[]{:S(2)}) async-start(bf16[64,288,128]{2,1,0:T(8,128)(2,1)} %reshape_reshape.3), calls=%async_computation | async-start | bytes 9437184 | tf_op jit(solution)/shard_map/all_to_all | solution.py:102
  38.2 119.3 %all-gather.6.cloned.1.call-start = ((), (), s32[]{:S(2)}) async-start(), calls=%async_computation.3 | async-start | bytes 3932160 | tf_op jit(solution)/shard_map/all_gather | solution.py:126
  39.0 124.3 %all-gather.4.cloned.1.call-start = ((), (), s32[]{:S(2)}) async-start(), calls=%async_computation.2 | async-start | bytes 3932160 | tf_op jit(solution)/shard_map/all_gather | solution.py:127
  39.7 246.6 %reduce-scatter.2.cloned.1.call-start = ((), (), s32[]{:S(2)}) async-start(), calls=%async_computation.5 | async-start | bytes 7864320 | tf_op jit(solution)/shard_map/reduce_scatter | solution.py:145
  169.4 9.2 %copy-start.4 = (bf16[576,768]{1,0:T(8,128)(2,1)}, bf16[576,768]{1,0:T(8,128)(2,1)S(1)}, u32[]{:S(2)}) copy-start(bf16[576,768]{1,0:T(8,128)(2,1)S(1)} %get-tuple-element.8) | copy-start | bytes 2654212
  178.7 4.1 %copy-start.3 = (bf16[1,2048,768]{2,1,0:T(8,128)(2,1)S(1)}, bf16[1,2048,768]{2,1,0:T(8,128)(2,1)}, u32[]{:S(2)}) copy-start(bf16[1,2048,768]{2,1,0:T(8,128)(2,1)} %all-gather.6.cloned.1.call-done) | copy-start | bytes 9437188
  178.7 4.1 %copy-start.5 = (bf16[576,768]{1,0:T(8,128)(2,1)S(1)}, bf16[576,768]{1,0:T(8,128)(2,1)}, u32[]{:S(2)}) copy-start(bf16[576,768]{1,0:T(8,128)(2,1)} %copy-done.4) | copy-start | bytes 2654212
  281.2 7.7 %copy-start.1 = (bf16[128,2048]{1,0:T(8,128)(2,1)S(1)}, bf16[128,2048]{1,0:T(8,128)(2,1)}, u32[]{:S(2)}) copy-start(bf16[128,2048]{1,0:T(8,128)(2,1)} %param.7) | copy-start | bytes 1572868
Sparse Core Ops, SparseCore 0:
  9.8 45.9 all-gather.7
  57.6 42.3 all-gather.5
  101.8 42.3 all-gather.3
  178.8 98.6 reduce-scatter.1

commit v9 on v5

--- a/solution.py
+++ b/solution.py
@@ -56,13 +56,19 @@
     grad_pre_up = (grad_act * act_value).astype(jnp.bfloat16)
     grad_pre_both = jnp.concatenate([grad_pre_gate, grad_pre_up], axis=1)
     part_both = jnp.dot(rows.T, grad_pre_both, preferred_element_type=jnp.float32)
-    part_down = jnp.dot(activ.T, scaled, preferred_element_type=jnp.float32)
-    sum_down = lax.psum_scatter(part_down.astype(jnp.bfloat16), "dp", scatter_dimension=0, tiled=True)
+    part_down = jnp.dot(activ.T, scaled, preferred_element_type=jnp.float32).astype(jnp.bfloat16)
+    quarters = part_down.reshape(groups, -1, part_down.shape[1])
+    mine = lax.axis_index("dp")
+    sum_down = lax.dynamic_index_in_dim(quarters, mine, keepdims=False).astype(jnp.float32)
+    for shift in range(1, groups):
+        block = lax.dynamic_index_in_dim(quarters, (mine + shift) % groups, keepdims=False)
+        ring = [(i, (i + shift) % groups) for i in range(groups)]
+        sum_down = sum_down + lax.ppermute(block, "dp", ring).astype(jnp.float32)
     sum_both = lax.psum_scatter(part_both.astype(jnp.bfloat16), "dp", scatter_dimension=0, tiled=True)
     hidden = grad_pre_gate.shape[1]
     sum_gate = sum_both[:, :hidden][None]
     sum_up = sum_both[:, hidden:][None]
-    sum_down = sum_down[None]
+    sum_down = sum_down.astype(jnp.bfloat16)[None]
     slot_grad = jnp.dot(grad_pre_gate, gate_full.T, preferred_element_type=jnp.float32)
     slot_grad = (
         slot_grad + jnp.dot(grad_pre_up, up_full.T, preferred_element_type=jnp.float32)

time: 295 us -> 294 us (level)
  blocking collectives: 66.3 us -> 0 us
  waiting for transfers between devices: 122 us -> 173 us
  starting transfers between devices: 13.8 us -> 26.1 us
  other arithmetic: 5.82 us -> 9.15 us
    ppermute x0 -> x3, waiting for transfers between devices: none -> 67.5 us  [shards(): sum_down = sum_down + lax.ppermute(block, 'dp', ring).astype(jnp.float32)]
    all_to_all x1 -> x0, blocking collectives: 66.3 us -> none  [exchange(): lax.all_to_all(flat, 'expert', split_axis=0, concat_axis=0, tiled=True)]
    reduce_scatter x1 -> x0, waiting for transfers between devices: 16 us -> none  [shards(): lax.psum_scatter(part_down.astype(jnp.bfloat16), 'dp', scatter_dimension=...]
    all_to_all x1 -> x2, starting transfers between devices: 13.2 us -> 20.8 us  [exchange(): lax.all_to_all(flat, 'expert', split_axis=0, concat_axis=0, tiled=True)]
    ppermute x0 -> x3, starting transfers between devices: none -> 5.01 us  [shards(): sum_down = sum_down + lax.ppermute(block, 'dp', ring).astype(jnp.float32)]
    broadcast_in_dim x0 -> x1, other arithmetic: none -> 3.32 us  [shards(): sum_down = sum_down.astype(jnp.bfloat16)[None]]
    all_to_all x1 -> x2, waiting for transfers between devices: 104 us -> 104 us  [exchange(): lax.all_to_all(flat, 'expert', split_axis=0, concat_axis=0, tiled=True)]
  transfers between devices with their start and end apart: 6 -> 9, of which waited for: 2 -> 3; matrix products, arithmetic and copies ran while one was open for 21% -> 21% of each run, Pallas kernels for 0% -> 0%
where the time goes in v9:
time: 294 us; the launch traced here: 293 us
  waiting for transfers between devices  173 us (59%)
  matrix products  43.1 us (15%)
  local copies, waits for them, and re-layouts  28 us (10%)
  starting transfers between devices  26.1 us (9%)
  between operations  14 us (5%)
  other arithmetic  9.15 us (3%)
    all_to_all x2, waiting for transfers between devices, exchange(): lax.all_to_all(flat, 'expert', split_axis=0, concat_axis=0, tiled=True)  104 us
    ppermute x3, waiting for transfers between devices, shards(): sum_down = sum_down + lax.ppermute(block, 'dp', ring).astype(jnp.float32)  67.5 us
    all_to_all x2, starting transfers between devices, exchange(): lax.all_to_all(flat, 'expert', split_axis=0, concat_axis=0, tiled=True)  20.8 us
    another operation x2, local copies, waits for them, and re-layouts, exchange(): flat = block.reshape(owners, -1, LANES)  10.8 us
    dot_general x1, matrix products, shards(): jnp.dot(rows.T, grad_pre_both, preferred_element_type=jnp.float32)  9.19 us
    reshape x1, local copies, waits for them, and re-layouts, shards(): got_both = exchange(send_both).reshape(owners * slot_cap, 2 * width)  8.18 us
    dot_general x1, matrix products, shards(): grad_act = jnp.dot(scaled, down_full.T, preferred_element_type=jnp.float32)  6.12 us
  transfers between devices with their start and end apart: 9, of which 3 were waited for; matrix products, arithmetic and copies ran while one was open for 21% of the time, Pallas kernels for 0%

profile of v9, /device:TPU:1, one launch (start us, length us, event | category | flops | bytes accessed | tf_op | source)
XLA Modules:
  0.0 293.5 jit_solution(9418358548655144059)
XLA Ops:
  7.2 0.0 copy-start
  7.2 0.0 all-gather.6.cloned.1.call-start
  7.2 0.7 all-gather.6.cloned.1.call-update
  7.9 0.8 copy.25
  8.7 0.1 eq.46
  8.8 0.1 eq.42
  8.9 1.2 reduce-window.6
  10.1 0.2 slice_reduce_fusion
  10.4 0.1 fusion.28
  10.5 0.1 reduce_sum.21
  10.7 0.1 copy.28
  10.7 0.7 multiply_add_fusion
  11.4 0.1 fusion.24
  11.6 0.9 select_reduce_fusion
  12.5 0.8 convolution_convert_fusion.2
  13.3 0.8 multiply_convert_fusion
  14.0 2.7 pad_maximum_fusion
  16.7 8.3 %reshape_reshape.6 = bf16[64,288,128]{2,1,0:T(8,128)(2,1)} reshape(bf16[576,4096]{1,0:T(8,128)(2,1)} %pad_maximum_fusion) | data formatting | bytes 9437184 | tf_op jit(solution)/shard_map/reshape;reshape | solution.py:16
  25.0 13.2 %all-to-all-start = ((bf16[64,288,128]{2,1,0:T(8,128)(2,1)}), bf16[64,288,128]{2,1,0:T(8,128)(2,1)}, u32[]{:S(2)}, u32[]{:S(2)}) async-start(bf16[64,288,128]{2,1,0:T(8,128)(2,1)} %reshape_reshape.6), calls=%async_computation | async-start | bytes 9437184 | tf_op jit(solution)/shard_map/all_to_all | solution.py:17
  38.2 0.0 all-gather.8.cloned.1.call-start
  38.3 0.7 all-gather.8.cloned.1.call-update
  39.0 0.0 all-gather.4.cloned.1.call-start
  39.0 0.7 all-gather.4.cloned.1.call-update
  39.7 0.2 reduce-scatter.2.cloned.1.call-start
  40.0 103.5 %all-to-all-done = bf16[64,288,128]{2,1,0:T(8,128)(2,1)} async-done(((bf16[64,288,128]{2,1,0:T(8,128)(2,1)}), bf16[64,288,128]{2,1,0:T(8,128)(2,1)}, u32[]{:S(2)}, u32[]{:S(2)}) %all-to-all-start) | async-done | bytes 4718624 | tf_op jit(solution)/shard_map/all_to_all | solution.py:17
  143.5 8.2 %reshape.48 = bf16[576,4096]{1,0:T(8,128)(2,1)} reshape(bf16[64,288,128]{2,1,0:T(8,128)(2,1)} %all-to-all-done) | data formatting | bytes 9437184 | tf_op jit(solution)/shard_map/reshape | solution.py:47
  151.7 5.8 %fusion.6 = f32[576,768]{1,0:T(8,128)} fusion(bf16[1,2048,768]{2,1,0:T(8,128)(2,1)} %all-gather.6.cloned.1.call-done, bf16[576,4096]{1,0:T(8,128)(2,1)} %reshape.48), kind=kOutput, calls=%fused_computation.11 | convolution fusion | flops 1811939328 | bytes 7274496 | tf_op jit(solution)/shard_map/dot_general | solution.py:51
  157.5 5.8 %fusion.2 = f32[576,768]{1,0:T(8,128)} fusion(bf16[1,2048,768]{2,1,0:T(8,128)(2,1)} %all-gather.8.cloned.1.call-done, bf16[576,4096]{1,0:T(8,128)(2,1)} %reshape.48), kind=kOutput, calls=%fused_computation.7 | convolution fusion | flops 1811939328 | bytes 7274496 | tf_op jit(solution)/shard_map/dot_general | solution.py:50
  163.3 6.1 %multiply_convert_fusion.2 = (bf16[576,768]{1,0:T(8,128)(2,1)S(1)}, bf16[576,768]{1,0:T(8,128)(2,1)S(1)}) fusion(f32[576,768]{1,0:T(8,128)} %fusion.2, f32[576,768]{1,0:T(8,128)} %fusion.6, bf16[1,768,2048]{2,1,0:T(8,128)(2,1)} %all-gather.4.cloned.1.call-done, bf16[576,4096]{1,0:T(8,128)(2,1)} %reshape.48), kind=kOutput, calls=%fused_computation.26 | convolution fusion | flops 1817690112 | bytes 10813440 | tf_op jit(solution)/shard_map/dot_general | solution.py:54
  169.4 9.2 %convolution_convert_fusion = bf16[2048,1536]{1,0:T(8,128)(2,1)} fusion(bf16[576,4096]{1,0:T(8,128)(2,1)} %reshape.48, bf16[576,768]{1,0:T(8,128)(2,1)S(1)} %get-tuple-element.4, bf16[576,768]{1,0:T(8,128)(2,1)S(1)} %get-tuple-element.5), kind=kOutput, calls=%fused_computation | convolution fusion | flops 3630563328 | bytes 10420224 | tf_op jit(solution)/shard_map/dot_general | solution.py:58
  178.6 0.0 reduce-scatter.2.cloned.1.call-update
  178.7 4.1 %fusion = f32[576,2048]{1,0:T(8,128)S(1)} fusion(bf16[576,768]{1,0:T(8,128)(2,1)S(1)} %get-tuple-element.5, bf16[1,2048,768]{2,1,0:T(8,128)(2,1)} %all-gather.8.cloned.1.call-done), kind=kOutput, calls=%fused_computation.5 | convolution fusion | flops 1811939328 | bytes 8749056 | tf_op jit(solution)/shard_map/dot_general | solution.py:72
  182.8 2.0 add_convert_fusion
  184.8 2.5 reshape_reshape.7
  187.3 7.6 %all-to-all-start.1 = ((bf16[64,144,128]{2,1,0:T(8,128)(2,1)}), bf16[64,144,128]{2,1,0:T(8,128)(2,1)S(1)}, u32[]{:S(2)}, u32[]{:S(2)}) async-start(bf16[64,144,128]{2,1,0:T(8,128)(2,1)} %reshape_reshape.7), calls=%async_computation.1 | async-start | bytes 4718592 | tf_op jit(solution)/shard_map/all_to_all | solution.py:17
  195.0 5.5 %convolution_convert_fusion.1 = bf16[768,2048]{1,0:T(8,128)(2,1)S(1)} fusion(bf16[576,4096]{1,0:T(8,128)(2,1)} %reshape.48, f32[576,768]{1,0:T(8,128)} %fusion.6, f32[576,768]{1,0:T(8,128)} %fusion.2), kind=kOutput, calls=%fused_computation.4 | convolution fusion | flops 1816166400 | bytes 9043968 | tf_op jit(solution)/shard_map/dot_general | solution.py:59
  200.4 1.6 dynamic-slice_bitcast_fusion.2
  202.0 0.9 copy-done.2
  202.9 1.4 collective-permute-start
  204.3 2.5 collective-permute-start.1
  206.8 1.1 collective-permute-start.2
  207.9 32.7 %collective-permute-done = bf16[192,2048]{1,0:T(8,128)(2,1)} collective-permute-done((bf16[192,2048]{1,0:T(8,128)(2,1)}, bf16[192,2048]{1,0:T(8,128)(2,1)}, u32[]{:S(2)}, u32[]{:S(2)}) %collective-permute-start) | collective-permute-done | bytes 786464 | tf_op jit(solution)/shard_map/ppermute | solution.py:66
  240.6 34.8 %collective-permute-done.1 = bf16[192,2048]{1,0:T(8,128)(2,1)} collective-permute-done((bf16[192,2048]{1,0:T(8,128)(2,1)}, bf16[192,2048]{1,0:T(8,128)(2,1)}, u32[]{:S(2)}, u32[]{:S(2)}) %collective-permute-start.1) | collective-permute-done | bytes 786464 | tf_op jit(solution)/shard_map/ppermute | solution.py:66
  275.4 3.3 %fusion.25 = bf16[1,192,2048]{2,1,0:T(8,128)(2,1)} fusion(bf16[192,2048]{1,0:T(8,128)(2,1)} %collective-permute-done.2, bf16[192,2048]{1,0:T(8,128)(2,1)} %collective-permute-done.1, bf16[192,2048]{1,0:T(8,128)(2,1)} %collective-permute-done, bf16[4,192,2048]{2,1,0:T(8,128)(2,1)} %bitcast.57, s32[]{:T(128)S(6)} %select_n.33), kind=kLoop, calls=%fused_computation.37 | loop fusion | flops 3145728 | bytes 3932164 | tf_op jit(solution)/shard_map/broadcast_in_dim | solution.py:71
  278.8 0.0 all-to-all-done.1
  278.8 2.5 reshape.49
  281.2 3.1 %convolution_convert_fusion.3 = bf16[128,2048]{1,0:T(8,128)(2,1)} fusion(pred[576,128]{1,0:T(8,128)(4,1)S(1)} %fusion.24, bf16[576,2048]{1,0:T(8,128)(2,1)} %reshape.49), kind=kOutput, calls=%fused_computation.16 | convolution fusion | flops 302252032 | bytes 2957312 | tf_op jit(solution)/shard_map/dot_general | solution.py:77
  284.3 2.6 slice_bitcast_fusion
  (20 shorter events, 0.1 us)
Async XLA Ops:
  7.2 5.3 %copy-start = (bf16[128,2048]{1,0:T(8,128)(2,1)S(1)}, bf16[128,2048]{1,0:T(8,128)(2,1)}, u32[]{:S(2)}) copy-start(bf16[128,2048]{1,0:T(8,128)(2,1)} %param.7) | copy-start | bytes 1572868
  7.2 144.5 %all-gather.6.cloned.1.call-start = ((), (), s32[]{:S(2)}) async-start(), calls=%async_computation.4 | async-start | bytes 3932160 | tf_op jit(solution)/shard_map/all_gather | solution.py:41
  7.2 6.0 %copy-start.3 = (bf16[128,2048]{1,0:T(8,128)(2,1)S(1)}, bf16[128,2048]{1,0:T(8,128)(2,1)}, u32[]{:S(2)}) copy-start(bf16[128,2048]{1,0:T(8,128)(2,1)} %param.8) | copy-start | bytes 1572868
  25.0 118.5 %all-to-all-start = ((bf16[64,288,128]{2,1,0:T(8,128)(2,1)}), bf16[64,288,128]{2,1,0:T(8,128)(2,1)}, u32[]{:S(2)}, u32[]{:S(2)}) async-start(bf16[64,288,128]{2,1,0:T(8,128)(2,1)} %reshape_reshape.6), calls=%async_computation | async-start | bytes 9437184 | tf_op jit(solution)/shard_map/all_to_all | solution.py:17
  38.2 119.3 %all-gather.8.cloned.1.call-start = ((), (), s32[]{:S(2)}) async-start(), calls=%async_computation.5 | async-start | bytes 3932160 | tf_op jit(solution)/shard_map/all_gather | solution.py:40
  39.0 124.3 %all-gather.4.cloned.1.call-start = ((), (), s32[]{:S(2)}) async-start(), calls=%async_computation.3 | async-start | bytes 3932160 | tf_op jit(solution)/shard_map/all_gather | solution.py:42
  39.7 244.6 %reduce-scatter.2.cloned.1.call-start = ((), (), s32[]{:S(2)}) async-start(), calls=%async_computation.6 | async-start | bytes 7864320 | tf_op jit(solution)/shard_map/reduce_scatter | solution.py:67
  169.4 9.2 %copy-start.5 = (bf16[576,768]{1,0:T(8,128)(2,1)}, bf16[576,768]{1,0:T(8,128)(2,1)S(1)}, u32[]{:S(2)}) copy-start(bf16[576,768]{1,0:T(8,128)(2,1)S(1)} %get-tuple-element.4) | copy-start | bytes 2654212
  178.7 4.1 %copy-start.4 = (bf16[1,2048,768]{2,1,0:T(8,128)(2,1)S(1)}, bf16[1,2048,768]{2,1,0:T(8,128)(2,1)}, u32[]{:S(2)}) copy-start(bf16[1,2048,768]{2,1,0:T(8,128)(2,1)} %all-gather.6.cloned.1.call-done) | copy-start | bytes 9437188
  178.7 4.1 %copy-start.6 = (bf16[576,768]{1,0:T(8,128)(2,1)S(1)}, bf16[576,768]{1,0:T(8,128)(2,1)}, u32[]{:S(2)}) copy-start(bf16[576,768]{1,0:T(8,128)(2,1)} %copy-done.5) | copy-start | bytes 2654212
  187.3 91.4 %all-to-all-start.1 = ((bf16[64,144,128]{2,1,0:T(8,128)(2,1)}), bf16[64,144,128]{2,1,0:T(8,128)(2,1)S(1)}, u32[]{:S(2)}, u32[]{:S(2)}) async-start(bf16[64,144,128]{2,1,0:T(8,128)(2,1)} %reshape_reshape.7), calls=%async_computation.1 | async-start | bytes 4718592 | tf_op jit(solution)/shard_map/all_to_all | solution.py:17
  200.4 2.5 copy-start.2
  202.9 37.7 %collective-permute-start = (bf16[192,2048]{1,0:T(8,128)(2,1)}, bf16[192,2048]{1,0:T(8,128)(2,1)}, u32[]{:S(2)}, u32[]{:S(2)}) collective-permute-start(bf16[192,2048]{1,0:T(8,128)(2,1)} %get-tuple-element.6), channel_id=1, source_target_pairs={{0,1},{1,2},{2,3},{3,0},{4,5},{5,6},{6,7},{7,4},{8,9},{9,10},{10,1... | collective-permute-start | bytes 2359304 | tf_op jit(solution)/shard_map/ppermute | solution.py:66
  204.3 71.1 %collective-permute-start.1 = (bf16[192,2048]{1,0:T(8,128)(2,1)}, bf16[192,2048]{1,0:T(8,128)(2,1)}, u32[]{:S(2)}, u32[]{:S(2)}) collective-permute-start(bf16[192,2048]{1,0:T(8,128)(2,1)} %get-tuple-element.8), channel_id=1, source_target_pairs={{0,2},{1,3},{2,0},{3,1},{4,6},{5,7},{6,4},{7,5},{8,10},{9,11},{10,... | collective-permute-start | bytes 2359304 | tf_op jit(solution)/shard_map/ppermute | solution.py:66
  206.8 68.6 %collective-permute-start.2 = (bf16[192,2048]{1,0:T(8,128)(2,1)}, bf16[192,2048]{1,0:T(8,128)(2,1)}, u32[]{:S(2)}, u32[]{:S(2)}) collective-permute-start(bf16[192,2048]{1,0:T(8,128)(2,1)} %get-tuple-element.7), channel_id=1, source_target_pairs={{0,3},{1,0},{2,1},{3,2},{4,7},{5,4},{6,5},{7,6},{8,11},{9,8},{10,9... | collective-permute-start | bytes 2359304 | tf_op jit(solution)/shard_map/ppermute | solution.py:66
  278.8 8.2 %copy-start.1 = (bf16[128,2048]{1,0:T(8,128)(2,1)S(1)}, bf16[128,2048]{1,0:T(8,128)(2,1)}, u32[]{:S(2)}) copy-start(bf16[128,2048]{1,0:T(8,128)(2,1)} %param.7) | copy-start | bytes 1572868
Sparse Core Ops, SparseCore 0:
  9.8 45.9 all-gather.5
  57.6 42.3 all-gather.7
  101.8 42.3 all-gather.3
  178.8 98.4 reduce-scatter.1

commit v10 on v5

--- a/solution.py
+++ b/solution.py
@@ -36,19 +36,16 @@
         slot_probs[:, None] * jnp.dot(select, cotangent, preferred_element_type=jnp.float32)
     ).astype(jnp.bfloat16)
     send_both = jnp.concatenate([send_rows, send_cot], axis=1).reshape(owners, slot_cap, 2 * width)
-    full_gate, full_up, full_down = (
-        lax.all_gather(w_gate, "dp", axis=1, tiled=True),
-        lax.all_gather(w_up, "dp", axis=1, tiled=True),
-        lax.all_gather(w_down, "dp", axis=1, tiled=True),
-    )
-    gate_full = full_gate[0]
-    up_full = full_up[0]
-    down_full = full_down[0]
+    hidden = w_gate.shape[2]
+    gate_up = jnp.concatenate([w_gate[0], w_up[0]], axis=1)
+    gu_full = lax.all_gather(gate_up, "dp", axis=0, tiled=True)
+    down_full = lax.all_gather(w_down, "dp", axis=1, tiled=True)[0]
     got_both = exchange(send_both).reshape(owners * slot_cap, 2 * width)
     rows = got_both[:, :width]
     scaled = got_both[:, width:]
-    pre_gate = jnp.dot(rows, gate_full, preferred_element_type=jnp.float32)
-    pre_up = jnp.dot(rows, up_full, preferred_element_type=jnp.float32)
+    pre_both = jnp.dot(rows, gu_full, preferred_element_type=jnp.float32)
+    pre_gate = pre_both[:, :hidden]
+    pre_up = pre_both[:, hidden:]
     act_value, act_slope = silu_parts(pre_gate)
     activ = (act_value * pre_up).astype(jnp.bfloat16)
     grad_act = jnp.dot(scaled, down_full.T, preferred_element_type=jnp.float32)
@@ -59,14 +56,10 @@
     part_down = jnp.dot(activ.T, scaled, preferred_element_type=jnp.float32)
     sum_down = lax.psum_scatter(part_down.astype(jnp.bfloat16), "dp", scatter_dimension=0, tiled=True)
     sum_both = lax.psum_scatter(part_both.astype(jnp.bfloat16), "dp", scatter_dimension=0, tiled=True)
-    hidden = grad_pre_gate.shape[1]
     sum_gate = sum_both[:, :hidden][None]
     sum_up = sum_both[:, hidden:][None]
     sum_down = sum_down[None]
-    slot_grad = jnp.dot(grad_pre_gate, gate_full.T, preferred_element_type=jnp.float32)
-    slot_grad = (
-        slot_grad + jnp.dot(grad_pre_up, up_full.T, preferred_element_type=jnp.float32)
-    ).astype(jnp.bfloat16)
+    slot_grad = jnp.dot(grad_pre_both, gu_full.T, preferred_element_type=jnp.float32).astype(jnp.bfloat16)
     returned = exchange(slot_grad.reshape(owners, slot_cap, width)).reshape(owners * slot_cap, width)
     grad_tokens = lax.dot_general(
         select, returned, (((0,), (0,)), ((), ())), preferred_element_type=jnp.float32

time: 295 us -> 290 us (0.983)
  matrix products: 44.2 us -> 40.4 us
    dot_general x4 -> x2, matrix products: 19.2 us -> 17.1 us  [the longest x1 9.07 us: shards(): pre_both = jnp.dot(rows, gu_full, preferred_element_type=jnp.float32)]
  transfers between devices with their start and end apart: 6 -> 5, of which waited for: 2 -> 2; matrix products, arithmetic and copies ran while one was open for 21% -> 20% of each run, Pallas kernels for 0% -> 0%
where the time goes in v10:
time: 290 us; the launch traced here: 289 us
  waiting for transfers between devices  121 us (42%)
  blocking collectives  66.2 us (23%)
  matrix products  40.4 us (14%)
  local copies, waits for them, and re-layouts  27.3 us (9%)
  between operations  13.9 us (5%)
  starting transfers between devices  13.5 us (5%)
  other arithmetic  7.27 us (3%)
    all_to_all x1, waiting for transfers between devices, exchange(): lax.all_to_all(flat, 'expert', split_axis=0, concat_axis=0, tiled=True)  104 us
    all_to_all x1, blocking collectives, exchange(): lax.all_to_all(flat, 'expert', split_axis=0, concat_axis=0, tiled=True)  66.2 us
    reduce_scatter x1, waiting for transfers between devices, shards(): lax.psum_scatter(part_down.astype(jnp.bfloat16), 'dp', scatter_dimension=...  15.6 us
    all_to_all x1, starting transfers between devices, exchange(): lax.all_to_all(flat, 'expert', split_axis=0, concat_axis=0, tiled=True)  13.2 us
    another operation x2, local copies, waits for them, and re-layouts, exchange(): flat = block.reshape(owners, -1, LANES)  12 us
    dot_general x1, matrix products, shards(): pre_both = jnp.dot(rows, gu_full, preferred_element_type=jnp.float32)  9.07 us
    reshape x1, local copies, waits for them, and re-layouts, shards(): got_both = exchange(send_both).reshape(owners * slot_cap, 2 * width)  8.17 us
    dot_general x1, matrix products, shards(): jnp.dot(grad_pre_both, gu_full.T, preferred_element_type=jnp.float32)  8.02 us
  transfers between devices with their start and end apart: 5, of which 2 were waited for; matrix products, arithmetic and copies ran while one was open for 20% of the time, Pallas kernels for 0%

profile of v10, /device:TPU:1, one launch (start us, length us, event | category | flops | bytes accessed | tf_op | source)
XLA Modules:
  0.0 289.4 jit_solution(11225194425697606818)
XLA Ops:
  7.2 0.0 copy-start
  7.2 0.0 all-gather.5.cloned.1.call-start
  7.2 0.0 copy-start.4
  7.2 0.0 copy-start.5
  7.2 2.7 pad_maximum_fusion.2
  10.0 0.0 all-gather.5.cloned.1.call-update
  10.0 0.0 copy-done.4
  10.0 0.0 copy-start.3
  10.0 0.1 copy.25
  10.1 0.1 eq.42
  10.2 0.1 eq.38
  10.4 1.2 reduce-window.6
  11.6 0.2 slice_reduce_fusion
  11.8 0.1 fusion.11
  12.0 0.1 reduce_sum.21
  12.1 0.1 copy.28
  12.2 0.2 fusion.8
  12.3 0.0 copy-done.5
  12.3 0.2 select_reduce_fusion
  12.5 0.0 copy-done
  12.5 0.8 convolution_convert_fusion.3
  13.3 0.0 copy-done.3
  13.3 0.8 multiply_convert_fusion
  14.1 2.8 pad_maximum_fusion
  16.9 8.3 %reshape_reshape.6 = bf16[64,288,128]{2,1,0:T(8,128)(2,1)} reshape(bf16[576,4096]{1,0:T(8,128)(2,1)} %pad_maximum_fusion) | data formatting | bytes 9437184 | tf_op jit(solution)/shard_map/reshape;reshape | solution.py:16
  25.2 13.2 %all-to-all-start = ((bf16[64,288,128]{2,1,0:T(8,128)(2,1)}), bf16[64,288,128]{2,1,0:T(8,128)(2,1)}, u32[]{:S(2)}, u32[]{:S(2)}) async-start(bf16[64,288,128]{2,1,0:T(8,128)(2,1)} %reshape_reshape.6), calls=%async_computation | async-start | bytes 9437184 | tf_op jit(solution)/shard_map/all_to_all | solution.py:17
  38.4 0.0 all-gather.3.cloned.1.call-start
  38.5 0.7 all-gather.3.cloned.1.call-update
  39.2 0.0 reduce-scatter.3.cloned.1.call-start
  39.2 104.4 %all-to-all-done = bf16[64,288,128]{2,1,0:T(8,128)(2,1)} async-done(((bf16[64,288,128]{2,1,0:T(8,128)(2,1)}), bf16[64,288,128]{2,1,0:T(8,128)(2,1)}, u32[]{:S(2)}, u32[]{:S(2)}) %all-to-all-start) | async-done | bytes 4718624 | tf_op jit(solution)/shard_map/all_to_all | solution.py:17
  143.7 8.2 %reshape.43 = bf16[576,4096]{1,0:T(8,128)(2,1)} reshape(bf16[64,288,128]{2,1,0:T(8,128)(2,1)} %all-to-all-done) | data formatting | bytes 9437184 | tf_op jit(solution)/shard_map/reshape | solution.py:43
  151.8 0.0 all-gather.5.cloned.1.call-done
  151.8 9.1 %fusion.3 = f32[576,1536]{1,0:T(8,128)} fusion(bf16[2048,1536]{1,0:T(8,128)(2,1)} %all-gather.5.cloned.1.call-done, bf16[576,4096]{1,0:T(8,128)(2,1)} %reshape.43), kind=kOutput, calls=%fused_computation.10 | convolution fusion | flops 3623878656 | bytes 12189696 | tf_op jit(solution)/shard_map/dot_general | solution.py:46
  160.9 6.3 %multiply_convert_fusion.3 = (bf16[576,768]{1,0:T(8,128)(2,1)S(1)}, bf16[576,768]{1,0:T(8,128)(2,1)S(1)}) fusion(f32[576,1536]{1,0:T(8,128)} %fusion.3, bf16[1,768,2048]{2,1,0:T(8,128)(2,1)} %all-gather.3.cloned.1.call-done, bf16[576,4096]{1,0:T(8,128)(2,1)} %reshape.43), kind=kOutput, calls=%fused_computation.17 | convolution fusion | flops 1817690112 | bytes 10813440 | tf_op jit(solution)/shard_map/dot_general | solution.py:51
  167.2 0.0 copy-done.2
  167.2 7.0 %convolution_convert_fusion = bf16[2048,1536]{1,0:T(8,128)(2,1)} fusion(bf16[576,4096]{1,0:T(8,128)(2,1)S(1)} %copy-done.2, bf16[576,768]{1,0:T(8,128)(2,1)S(1)} %get-tuple-element.5, bf16[576,768]{1,0:T(8,128)(2,1)S(1)} %get-tuple-element.4), kind=kOutput, calls=%fused_computation | convolution fusion | flops 3630563328 | bytes 10420224 | tf_op jit(solution)/shard_map/dot_general | solution.py:55
  174.2 0.0 reduce-scatter.3.cloned.1.call-update
  174.2 0.2 reduce-scatter.5.cloned.1.call-start
  174.4 7.1 %convolution_convert_fusion.1 = bf16[768,2048]{1,0:T(8,128)(2,1)} fusion(bf16[576,4096]{1,0:T(8,128)(2,1)} %reshape.43, f32[576,1536]{1,0:T(8,128)} %fusion.3), kind=kOutput, calls=%fused_computation.3 | convolution fusion | flops 1816166400 | bytes 9043968 | tf_op jit(solution)/shard_map/dot_general | solution.py:56
  181.5 0.0 reduce-scatter.5.cloned.1.call-update
  181.6 8.0 %convolution_convert_fusion.2 = bf16[576,2048]{1,0:T(8,128)(2,1)} fusion(bf16[2048,1536]{1,0:T(8,128)(2,1)} %all-gather.5.cloned.1.call-done, bf16[576,768]{1,0:T(8,128)(2,1)S(1)} %get-tuple-element.5, bf16[576,768]{1,0:T(8,128)(2,1)S(1)} %get-tuple-element.4), kind=kOutput, calls=%fused_computation.6 | convolution fusion | flops 3628597248 | bytes 10420224 | tf_op jit(solution)/shard_map/dot_general | solution.py:62
  189.6 3.7 %reshape_reshape.7 = bf16[64,144,128]{2,1,0:T(8,128)(2,1)S(1)} reshape(bf16[576,2048]{1,0:T(8,128)(2,1)} %convolution_convert_fusion.2) | data formatting | bytes 4718592 | tf_op jit(solution)/shard_map/reshape;reshape | solution.py:16
  193.3 66.2 %all_to_all.10 = bf16[64,144,128]{2,1,0:T(8,128)(2,1)} all-to-all(bf16[64,144,128]{2,1,0:T(8,128)(2,1)S(1)} %reshape_reshape.7), channel_id=1, replica_groups=mesh['expert'=64,'dp'=4] {'expert'}, dimensions={0} | all-to-all | bytes 4718592 | tf_op jit(solution)/shard_map/all_to_all | solution.py:17
  259.6 3.7 %reshape.44 = bf16[576,2048]{1,0:T(8,128)(2,1)S(1)} reshape(bf16[64,144,128]{2,1,0:T(8,128)(2,1)} %all_to_all.10) | data formatting | bytes 4718592 | tf_op jit(solution)/shard_map/reshape | solution.py:63
  263.3 1.4 convolution_convert_fusion.4
  264.7 2.6 slice_bitcast_fusion
  267.3 15.6 %reduce-scatter.5.cloned.1.call-done = bf16[192,2048]{1,0:T(8,128)(2,1)} async-done(((bf16[768,2048]{1,0:T(8,128)(2,1)}), bf16[192,2048]{1,0:T(8,128)(2,1)}) %reduce-scatter.5.cloned.1.call-update) | async-done | bytes 786448 | tf_op jit(solution)/shard_map/reduce_scatter | solution.py:57
  282.9 0.0 copy-done.1
  (8 shorter events, 0.1 us)
Async XLA Ops:
  7.2 5.4 %copy-start = (bf16[128,2048]{1,0:T(8,128)(2,1)S(1)}, bf16[128,2048]{1,0:T(8,128)(2,1)}, u32[]{:S(2)}) copy-start(bf16[128,2048]{1,0:T(8,128)(2,1)} %param.7) | copy-start | bytes 1572868
  7.2 144.6 %all-gather.5.cloned.1.call-start = ((), (), s32[]{:S(2)}) async-start(), calls=%async_computation.5 | async-start | bytes 7864320 | tf_op jit(solution)/shard_map/all_gather | solution.py:41
  7.2 2.8 copy-start.4
  7.2 5.1 %copy-start.5 = (f32[128,4]{0,1:T(4,128)S(1)}, f32[128,4]{0,1:T(4,128)}, u32[]{:S(2)}) copy-start(f32[128,4]{0,1:T(4,128)} %param.10) | copy-start | bytes 6148
  10.0 3.3 %copy-start.3 = (bf16[128,2048]{1,0:T(8,128)(2,1)S(1)}, bf16[128,2048]{1,0:T(8,128)(2,1)}, u32[]{:S(2)}) copy-start(bf16[128,2048]{1,0:T(8,128)(2,1)} %param.8) | copy-start | bytes 1572868
  25.2 118.4 %all-to-all-start = ((bf16[64,288,128]{2,1,0:T(8,128)(2,1)}), bf16[64,288,128]{2,1,0:T(8,128)(2,1)}, u32[]{:S(2)}, u32[]{:S(2)}) async-start(bf16[64,288,128]{2,1,0:T(8,128)(2,1)} %reshape_reshape.6), calls=%async_computation | async-start | bytes 9437184 | tf_op jit(solution)/shard_map/all_to_all | solution.py:17
  38.4 122.5 %all-gather.3.cloned.1.call-start = ((), (), s32[]{:S(2)}) async-start(), calls=%async_computation.4 | async-start | bytes 3932160 | tf_op jit(solution)/shard_map/all_gather | solution.py:42
  39.2 225.5 %reduce-scatter.3.cloned.1.call-start = ((), (), s32[]{:S(2)}) async-start(), calls=%async_computation.6 | async-start | bytes 7864320 | tf_op jit(solution)/shard_map/reduce_scatter | solution.py:58
  160.9 6.3 %copy-start.2 = (bf16[576,4096]{1,0:T(8,128)(2,1)S(1)}, bf16[576,4096]{1,0:T(8,128)(2,1)}, u32[]{:S(2)}) copy-start(bf16[576,4096]{1,0:T(8,128)(2,1)} %reshape.43) | copy-start | bytes 14155780
  174.2 108.7 %reduce-scatter.5.cloned.1.call-start = ((), (), s32[]{:S(2)}) async-start(), calls=%async_computation.7 | async-start | bytes 3932160 | tf_op jit(solution)/shard_map/reduce_scatter | solution.py:57
  259.5 23.4 %copy-start.1 = (bf16[128,2048]{1,0:T(8,128)(2,1)S(1)}, bf16[128,2048]{1,0:T(8,128)(2,1)}, u32[]{:S(2)}) copy-start(bf16[128,2048]{1,0:T(8,128)(2,1)} %param.7) | copy-start | bytes 1572868
Sparse Core Ops, SparseCore 0:
  10.1 72.0 all-gather.4
  84.0 42.8 all-gather.2
  174.3 64.9 reduce-scatter.2
  242.3 40.5 reduce-scatter.4

commit v11 on v10

--- a/solution.py
+++ b/solution.py
@@ -31,11 +31,11 @@
     picks = slots[None, :, :] == jnp.arange(owners * slot_cap, dtype=jnp.int32)[:, None, None]
     select = jnp.any(picks, axis=2).astype(jnp.bfloat16)
     slot_probs = jnp.sum(jnp.where(picks, gate_probs[None, :, :], 0.0), axis=(1, 2))
-    send_rows = jnp.dot(select, tokens, preferred_element_type=jnp.float32).astype(jnp.bfloat16)
-    send_cot = (
-        slot_probs[:, None] * jnp.dot(select, cotangent, preferred_element_type=jnp.float32)
-    ).astype(jnp.bfloat16)
-    send_both = jnp.concatenate([send_rows, send_cot], axis=1).reshape(owners, slot_cap, 2 * width)
+    both = jnp.dot(
+        select, jnp.concatenate([tokens, cotangent], axis=1), preferred_element_type=jnp.float32
+    )
+    scale = jnp.where(jnp.arange(2 * width) < width, 1.0, slot_probs[:, None])
+    send_both = (both * scale).astype(jnp.bfloat16).reshape(owners, slot_cap, 2 * width)
     hidden = w_gate.shape[2]
     gate_up = jnp.concatenate([w_gate[0], w_up[0]], axis=1)
     gu_full = lax.all_gather(gate_up, "dp", axis=0, tiled=True)

time: 290 us -> 290 us (level)
  no operation moved by 1% of the time
where the time goes in v11:
time: 290 us; the launch traced here: 289 us
  waiting for transfers between devices  121 us (42%)
  blocking collectives  66.3 us (23%)
  matrix products  42.5 us (15%)
  local copies, waits for them, and re-layouts  27.2 us (9%)
  between operations  13.9 us (5%)
  starting transfers between devices  13.5 us (5%)
  other arithmetic  4.51 us (2%)
    all_to_all x1, waiting for transfers between devices, exchange(): lax.all_to_all(flat, 'expert', split_axis=0, concat_axis=0, tiled=True)  104 us
    all_to_all x1, blocking collectives, exchange(): lax.all_to_all(flat, 'expert', split_axis=0, concat_axis=0, tiled=True)  66.3 us
    reduce_scatter x1, waiting for transfers between devices, shards(): lax.psum_scatter(part_down.astype(jnp.bfloat16), 'dp', scatter_dimension=...  15.7 us
    all_to_all x1, starting transfers between devices, exchange(): lax.all_to_all(flat, 'expert', split_axis=0, concat_axis=0, tiled=True)  13.2 us
    another operation x2, local copies, waits for them, and re-layouts, exchange(): flat = block.reshape(owners, -1, LANES)  12 us
    dot_general x1, matrix products, shards(): pre_both = jnp.dot(rows, gu_full, preferred_element_type=jnp.float32)  9.07 us
    reshape x1, local copies, waits for them, and re-layouts, shards(): got_both = exchange(send_both).reshape(owners * slot_cap, 2 * width)  8.17 us
    dot_general x1, matrix products, shards(): jnp.dot(grad_pre_both, gu_full.T, preferred_element_type=jnp.float32)  8.02 us
  transfers between devices with their start and end apart: 5, of which 2 were waited for; matrix products, arithmetic and copies ran while one was open for 20% of the time, Pallas kernels for 0%

profile of v11, /device:TPU:1, one launch (start us, length us, event | category | flops | bytes accessed | tf_op | source)
XLA Modules:
  0.0 288.7 jit_solution(8645809713938740740)
XLA Ops:
  7.2 0.0 all-gather.5.cloned.1.call-start
  7.2 0.0 copy-start.1
  7.2 0.0 copy-start.2
  7.2 0.0 copy-start.3
  7.2 0.0 copy-start.4
  7.3 2.8 pad_maximum_fusion.1
  10.0 0.0 all-gather.5.cloned.1.call-update
  10.0 0.0 copy-done.1
  10.0 0.1 copy.25
  10.2 0.1 eq.42
  10.3 0.1 eq.38
  10.4 1.2 reduce-window.6
  11.6 0.2 slice_reduce_fusion
  11.9 0.1 fusion.14
  12.0 0.1 reduce_sum.21
  12.1 0.1 copy.28
  12.2 0.1 fusion.8
  12.4 0.0 copy-done.2
  12.4 0.2 select_reduce_fusion
  12.6 0.0 copy-done.3
  12.6 0.0 copy-done.4
  12.6 3.6 %multiply_convert_fusion = bf16[576,4096]{1,0:T(8,128)(2,1)} fusion(pred[576,128]{1,0:T(8,128)(4,1)S(1)} %fusion.8, f32[576]{0:T(1024)S(1)} %select_reduce_fusion, pred[4096]{0:T(1024)(128)(4,1)S(1)} %iota_compare_fusion.3, bf16[128,2048]{1,0:T(8,128)(2,1)S(1)} %copy-done.3, bf16[128,2048]{1,0:T(8,128)(2,1)S(1)} %copy-done.4), kind=kOutput, calls=%fused_computation | convolution fusion | flops 613154816 | bytes 5847296 | tf_op jit(solution)/shard_map/dot_general | solution.py:34
  16.2 8.3 %reshape_reshape.6 = bf16[64,288,128]{2,1,0:T(8,128)(2,1)} reshape(bf16[576,4096]{1,0:T(8,128)(2,1)} %multiply_convert_fusion) | data formatting | bytes 9437184 | tf_op jit(solution)/shard_map/reshape;reshape | solution.py:16
  24.5 13.2 %all-to-all-start = ((bf16[64,288,128]{2,1,0:T(8,128)(2,1)}), bf16[64,288,128]{2,1,0:T(8,128)(2,1)}, u32[]{:S(2)}, u32[]{:S(2)}) async-start(bf16[64,288,128]{2,1,0:T(8,128)(2,1)} %reshape_reshape.6), calls=%async_computation | async-start | bytes 9437184 | tf_op jit(solution)/shard_map/all_to_all | solution.py:17
  37.7 0.0 all-gather.3.cloned.1.call-start
  37.7 0.7 all-gather.3.cloned.1.call-update
  38.4 0.0 reduce-scatter.3.cloned.1.call-start
  38.5 104.4 %all-to-all-done = bf16[64,288,128]{2,1,0:T(8,128)(2,1)} async-done(((bf16[64,288,128]{2,1,0:T(8,128)(2,1)}), bf16[64,288,128]{2,1,0:T(8,128)(2,1)}, u32[]{:S(2)}, u32[]{:S(2)}) %all-to-all-start) | async-done | bytes 4718624 | tf_op jit(solution)/shard_map/all_to_all | solution.py:17
  142.9 8.2 %reshape.43 = bf16[576,4096]{1,0:T(8,128)(2,1)} reshape(bf16[64,288,128]{2,1,0:T(8,128)(2,1)} %all-to-all-done) | data formatting | bytes 9437184 | tf_op jit(solution)/shard_map/reshape | solution.py:43
  151.1 0.0 all-gather.5.cloned.1.call-done
  151.1 9.1 %fusion.3 = f32[576,1536]{1,0:T(8,128)} fusion(bf16[2048,1536]{1,0:T(8,128)(2,1)} %all-gather.5.cloned.1.call-done, bf16[576,4096]{1,0:T(8,128)(2,1)} %reshape.43), kind=kOutput, calls=%fused_computation.8 | convolution fusion | flops 3623878656 | bytes 12189696 | tf_op jit(solution)/shard_map/dot_general | solution.py:46
  160.2 0.0 all-gather.3.cloned.1.call-done
  160.2 0.0 copy-start
  160.2 6.3 %multiply_convert_fusion.3 = (bf16[576,768]{1,0:T(8,128)(2,1)S(1)}, bf16[576,768]{1,0:T(8,128)(2,1)S(1)}) fusion(f32[576,1536]{1,0:T(8,128)} %fusion.3, bf16[1,768,2048]{2,1,0:T(8,128)(2,1)} %all-gather.3.cloned.1.call-done, bf16[576,4096]{1,0:T(8,128)(2,1)} %reshape.43), kind=kOutput, calls=%fused_computation.15 | convolution fusion | flops 1817690112 | bytes 10813440 | tf_op jit(solution)/shard_map/dot_general | solution.py:51
  166.5 0.0 copy-done
  166.5 7.0 %convolution_convert_fusion = bf16[2048,1536]{1,0:T(8,128)(2,1)} fusion(bf16[576,4096]{1,0:T(8,128)(2,1)S(1)} %copy-done, bf16[576,768]{1,0:T(8,128)(2,1)S(1)} %get-tuple-element.5, bf16[576,768]{1,0:T(8,128)(2,1)S(1)} %get-tuple-element.4), kind=kOutput, calls=%fused_computation.1 | convolution fusion | flops 3630563328 | bytes 10420224 | tf_op jit(solution)/shard_map/dot_general | solution.py:55
  173.5 0.0 reduce-scatter.3.cloned.1.call-update
  173.5 0.2 reduce-scatter.5.cloned.1.call-start
  173.7 7.1 %convolution_convert_fusion.1 = bf16[768,2048]{1,0:T(8,128)(2,1)} fusion(bf16[576,4096]{1,0:T(8,128)(2,1)} %reshape.43, f32[576,1536]{1,0:T(8,128)} %fusion.3), kind=kOutput, calls=%fused_computation.2 | convolution fusion | flops 1816166400 | bytes 9043968 | tf_op jit(solution)/shard_map/dot_general | solution.py:56
  180.8 0.0 reduce-scatter.5.cloned.1.call-update
  180.8 8.0 %convolution_convert_fusion.2 = bf16[576,2048]{1,0:T(8,128)(2,1)} fusion(bf16[2048,1536]{1,0:T(8,128)(2,1)} %all-gather.5.cloned.1.call-done, bf16[576,768]{1,0:T(8,128)(2,1)S(1)} %get-tuple-element.5, bf16[576,768]{1,0:T(8,128)(2,1)S(1)} %get-tuple-element.4), kind=kOutput, calls=%fused_computation.5 | convolution fusion | flops 3628597248 | bytes 10420224 | tf_op jit(solution)/shard_map/dot_general | solution.py:62
  188.9 3.7 %reshape_reshape.7 = bf16[64,144,128]{2,1,0:T(8,128)(2,1)S(1)} reshape(bf16[576,2048]{1,0:T(8,128)(2,1)} %convolution_convert_fusion.2) | data formatting | bytes 4718592 | tf_op jit(solution)/shard_map/reshape;reshape | solution.py:16
  192.6 66.3 %all_to_all.10 = bf16[64,144,128]{2,1,0:T(8,128)(2,1)} all-to-all(bf16[64,144,128]{2,1,0:T(8,128)(2,1)S(1)} %reshape_reshape.7), channel_id=1, replica_groups=mesh['expert'=64,'dp'=4] {'expert'}, dimensions={0} | all-to-all | bytes 4718592 | tf_op jit(solution)/shard_map/all_to_all | solution.py:17
  258.8 3.7 %reshape.44 = bf16[576,2048]{1,0:T(8,128)(2,1)S(1)} reshape(bf16[64,144,128]{2,1,0:T(8,128)(2,1)} %all_to_all.10) | data formatting | bytes 4718592 | tf_op jit(solution)/shard_map/reshape | solution.py:63
  262.5 1.4 convolution_convert_fusion.3
  263.9 0.0 reduce-scatter.3.cloned.1.call-done
  263.9 2.6 slice_bitcast_fusion
  266.5 15.7 %reduce-scatter.5.cloned.1.call-done = bf16[192,2048]{1,0:T(8,128)(2,1)} async-done(((bf16[768,2048]{1,0:T(8,128)(2,1)}), bf16[192,2048]{1,0:T(8,128)(2,1)}) %reduce-scatter.5.cloned.1.call-update) | async-done | bytes 786448 | tf_op jit(solution)/shard_map/reduce_scatter | solution.py:57
  (5 shorter events, 0.1 us)
Async XLA Ops:
  7.2 143.9 %all-gather.5.cloned.1.call-start = ((), (), s32[]{:S(2)}) async-start(), calls=%async_computation.5 | async-start | bytes 7864320 | tf_op jit(solution)/shard_map/all_gather | solution.py:41
  7.2 2.8 copy-start.1
  7.2 5.1 %copy-start.2 = (f32[128,4]{0,1:T(4,128)S(1)}, f32[128,4]{0,1:T(4,128)}, u32[]{:S(2)}) copy-start(f32[128,4]{0,1:T(4,128)} %param.10) | copy-start | bytes 6148
  7.2 5.3 %copy-start.3 = (bf16[128,2048]{1,0:T(8,128)(2,1)S(1)}, bf16[128,2048]{1,0:T(8,128)(2,1)}, u32[]{:S(2)}) copy-start(bf16[128,2048]{1,0:T(8,128)(2,1)} %param.8) | copy-start | bytes 1572868
  7.2 5.3 %copy-start.4 = (bf16[128,2048]{1,0:T(8,128)(2,1)S(1)}, bf16[128,2048]{1,0:T(8,128)(2,1)}, u32[]{:S(2)}) copy-start(bf16[128,2048]{1,0:T(8,128)(2,1)} %param.7) | copy-start | bytes 1572868
  24.5 118.4 %all-to-all-start = ((bf16[64,288,128]{2,1,0:T(8,128)(2,1)}), bf16[64,288,128]{2,1,0:T(8,128)(2,1)}, u32[]{:S(2)}, u32[]{:S(2)}) async-start(bf16[64,288,128]{2,1,0:T(8,128)(2,1)} %reshape_reshape.6), calls=%async_computation | async-start | bytes 9437184 | tf_op jit(solution)/shard_map/all_to_all | solution.py:17
  37.7 122.5 %all-gather.3.cloned.1.call-start = ((), (), s32[]{:S(2)}) async-start(), calls=%async_computation.4 | async-start | bytes 3932160 | tf_op jit(solution)/shard_map/all_gather | solution.py:42
  38.4 225.5 %reduce-scatter.3.cloned.1.call-start = ((), (), s32[]{:S(2)}) async-start(), calls=%async_computation.6 | async-start | bytes 7864320 | tf_op jit(solution)/shard_map/reduce_scatter | solution.py:58
  160.2 6.3 %copy-start = (bf16[576,4096]{1,0:T(8,128)(2,1)S(1)}, bf16[576,4096]{1,0:T(8,128)(2,1)}, u32[]{:S(2)}) copy-start(bf16[576,4096]{1,0:T(8,128)(2,1)} %reshape.43) | copy-start | bytes 14155780
  173.5 108.7 %reduce-scatter.5.cloned.1.call-start = ((), (), s32[]{:S(2)}) async-start(), calls=%async_computation.7 | async-start | bytes 3932160 | tf_op jit(solution)/shard_map/reduce_scatter | solution.py:57
Sparse Core Ops, SparseCore 0:
  10.2 72.0 all-gather.4
  84.0 42.8 all-gather.2
  173.6 64.9 reduce-scatter.2
  241.6 40.5 reduce-scatter.4

commit v12 on v10

--- a/solution.py
+++ b/solution.py
@@ -61,6 +61,7 @@
     sum_down = sum_down[None]
     slot_grad = jnp.dot(grad_pre_both, gu_full.T, preferred_element_type=jnp.float32).astype(jnp.bfloat16)
     returned = exchange(slot_grad.reshape(owners, slot_cap, width)).reshape(owners * slot_cap, width)
+    sum_down, returned = lax.optimization_barrier((sum_down, returned))
     grad_tokens = lax.dot_general(
         select, returned, (((0,), (0,)), ((), ())), preferred_element_type=jnp.float32
     ).astype(jnp.bfloat16)

time: 290 us -> 283 us (0.976)
  waiting for transfers between devices: 121 us -> 116 us
  matrix products: 40.4 us -> 36.9 us
    reduce_scatter x1, waiting for transfers between devices: 15.6 us -> 0.02 us  [shards(): lax.psum_scatter(part_down.astype(jnp.bfloat16), 'dp', scatter_dimension=...]
    reduce_scatter x1, waiting for transfers between devices: 0.01 us -> 10.4 us  [shards(): lax.psum_scatter(part_both.astype(jnp.bfloat16), 'dp', scatter_dimension=...]
    dot_general x1, matrix products: 7.11 us -> 4.15 us  [shards(): part_down = jnp.dot(activ.T, scaled, preferred_element_type=jnp.float32)]
  transfers between devices with their start and end apart: 5 -> 5, of which waited for: 2 -> 2; matrix products, arithmetic and copies ran while one was open for 20% -> 23% of each run, Pallas kernels for 0% -> 0%
where the time goes in v12:
time: 283 us; the launch traced here: 282 us
  waiting for transfers between devices  116 us (41%)
  blocking collectives  65.6 us (23%)
  matrix products  36.9 us (13%)
  local copies, waits for them, and re-layouts  29 us (10%)
  between operations  13.9 us (5%)
  starting transfers between devices  13.5 us (5%)
  other arithmetic  7.27 us (3%)
    all_to_all x1, waiting for transfers between devices, exchange(): lax.all_to_all(flat, 'expert', split_axis=0, concat_axis=0, tiled=True)  104 us
    all_to_all x1, blocking collectives, exchange(): lax.all_to_all(flat, 'expert', split_axis=0, concat_axis=0, tiled=True)  65.6 us
    all_to_all x1, starting transfers between devices, exchange(): lax.all_to_all(flat, 'expert', split_axis=0, concat_axis=0, tiled=True)  13.2 us
    another operation x2, local copies, waits for them, and re-layouts, exchange(): flat = block.reshape(owners, -1, LANES)  12 us
    reduce_scatter x1, waiting for transfers between devices, shards(): lax.psum_scatter(part_both.astype(jnp.bfloat16), 'dp', scatter_dimension=...  10.4 us
    dot_general x1, matrix products, shards(): jnp.dot(rows.T, grad_pre_both, preferred_element_type=jnp.float32)  8.97 us
    reshape x1, local copies, waits for them, and re-layouts, shards(): got_both = exchange(send_both).reshape(owners * slot_cap, 2 * width)  8.17 us
    dot_general x1, matrix products, shards(): jnp.dot(grad_pre_both, gu_full.T, preferred_element_type=jnp.float32)  7.95 us
  transfers between devices with their start and end apart: 5, of which 2 were waited for; matrix products, arithmetic and copies ran while one was open for 23% of the time, Pallas kernels for 0%

profile of v12, /device:TPU:1, one launch (start us, length us, event | category | flops | bytes accessed | tf_op | source)
XLA Modules:
  0.0 281.9 jit_solution(17588629339993834899)
XLA Ops:
  7.2 0.0 copy-start
  7.2 0.0 all-gather.3.cloned.1.call-start
  7.2 0.0 copy-start.4
  7.2 0.0 copy-start.5
  7.2 2.7 pad_maximum_fusion.2
  10.0 0.0 all-gather.3.cloned.1.call-update
  10.0 0.0 copy-done.4
  10.0 0.0 copy-start.3
  10.0 0.1 copy.25
  10.1 0.1 eq.42
  10.2 0.1 eq.38
  10.4 1.2 reduce-window.6
  11.6 0.2 slice_reduce_fusion
  11.8 0.1 fusion.11
  12.0 0.1 reduce_sum.21
  12.1 0.1 copy.28
  12.2 0.2 fusion.8
  12.3 0.0 copy-done.5
  12.3 0.2 select_reduce_fusion
  12.5 0.0 copy-done
  12.5 0.8 convolution_convert_fusion.3
  13.3 0.8 multiply_convert_fusion
  14.1 2.8 pad_maximum_fusion
  16.9 8.3 %reshape_reshape.6 = bf16[64,288,128]{2,1,0:T(8,128)(2,1)} reshape(bf16[576,4096]{1,0:T(8,128)(2,1)} %pad_maximum_fusion) | data formatting | bytes 9437184 | tf_op jit(solution)/shard_map/reshape;reshape | solution.py:16
  25.2 13.2 %all-to-all-start = ((bf16[64,288,128]{2,1,0:T(8,128)(2,1)}), bf16[64,288,128]{2,1,0:T(8,128)(2,1)}, u32[]{:S(2)}, u32[]{:S(2)}) async-start(bf16[64,288,128]{2,1,0:T(8,128)(2,1)} %reshape_reshape.6), calls=%async_computation | async-start | bytes 9437184 | tf_op jit(solution)/shard_map/all_to_all | solution.py:17
  38.4 0.0 all-gather.5.cloned.1.call-start
  38.5 0.7 all-gather.5.cloned.1.call-update
  39.2 0.0 reduce-scatter.3.cloned.1.call-start
  39.2 104.4 %all-to-all-done = bf16[64,288,128]{2,1,0:T(8,128)(2,1)} async-done(((bf16[64,288,128]{2,1,0:T(8,128)(2,1)}), bf16[64,288,128]{2,1,0:T(8,128)(2,1)}, u32[]{:S(2)}, u32[]{:S(2)}) %all-to-all-start) | async-done | bytes 4718624 | tf_op jit(solution)/shard_map/all_to_all | solution.py:17
  143.7 8.2 %reshape.43 = bf16[576,4096]{1,0:T(8,128)(2,1)} reshape(bf16[64,288,128]{2,1,0:T(8,128)(2,1)} %all-to-all-done) | data formatting | bytes 9437184 | tf_op jit(solution)/shard_map/reshape | solution.py:43
  151.8 6.8 %fusion.5 = f32[576,1536]{1,0:T(8,128)S(1)} fusion(bf16[2048,1536]{1,0:T(8,128)(2,1)} %all-gather.3.cloned.1.call-done, bf16[576,4096]{1,0:T(8,128)(2,1)} %reshape.43), kind=kOutput, calls=%fused_computation.12 | convolution fusion | flops 3623878656 | bytes 12189696 | tf_op jit(solution)/shard_map/dot_general | solution.py:46
  158.6 1.8 copy-done.6
  160.4 4.2 %convolution_convert_fusion.1 = bf16[768,2048]{1,0:T(8,128)(2,1)} fusion(bf16[576,4096]{1,0:T(8,128)(2,1)S(1)} %copy-done.2, f32[576,1536]{1,0:T(8,128)S(1)} %fusion.5), kind=kOutput, calls=%fused_computation.3 | convolution fusion | flops 1816166400 | bytes 9043968 | tf_op jit(solution)/shard_map/dot_general | solution.py:56
  164.6 0.0 reduce-scatter.3.cloned.1.call-update
  164.6 0.2 reduce-scatter.5.cloned.1.call-start
  164.9 0.0 all-gather.5.cloned.1.call-done
  164.9 6.1 %multiply_convert_fusion.2 = (bf16[576,768]{1,0:T(8,128)(2,1)S(1)}, bf16[576,768]{1,0:T(8,128)(2,1)S(1)}) fusion(f32[576,1536]{1,0:T(8,128)} %copy-done.6, bf16[1,768,2048]{2,1,0:T(8,128)(2,1)} %all-gather.5.cloned.1.call-done, bf16[576,4096]{1,0:T(8,128)(2,1)} %reshape.43), kind=kOutput, calls=%fused_computation.16 | convolution fusion | flops 1817690112 | bytes 10813440 | tf_op jit(solution)/shard_map/dot_general | solution.py:51
  171.0 9.0 %convolution_convert_fusion = bf16[2048,1536]{1,0:T(8,128)(2,1)} fusion(bf16[576,4096]{1,0:T(8,128)(2,1)} %reshape.43, bf16[576,768]{1,0:T(8,128)(2,1)S(1)} %get-tuple-element.9, bf16[576,768]{1,0:T(8,128)(2,1)S(1)} %get-tuple-element.8), kind=kOutput, calls=%fused_computation | convolution fusion | flops 3630563328 | bytes 10420224 | tf_op jit(solution)/shard_map/dot_general | solution.py:55
  180.0 0.0 reduce-scatter.5.cloned.1.call-update
  180.0 7.9 %convolution_convert_fusion.2 = bf16[576,2048]{1,0:T(8,128)(2,1)} fusion(bf16[2048,1536]{1,0:T(8,128)(2,1)} %all-gather.3.cloned.1.call-done, bf16[576,768]{1,0:T(8,128)(2,1)S(1)} %get-tuple-element.9, bf16[576,768]{1,0:T(8,128)(2,1)S(1)} %get-tuple-element.8), kind=kOutput, calls=%fused_computation.6 | convolution fusion | flops 3628597248 | bytes 10420224 | tf_op jit(solution)/shard_map/dot_general | solution.py:62
  188.0 3.7 %reshape_reshape.7 = bf16[64,144,128]{2,1,0:T(8,128)(2,1)S(1)} reshape(bf16[576,2048]{1,0:T(8,128)(2,1)} %convolution_convert_fusion.2) | data formatting | bytes 4718592 | tf_op jit(solution)/shard_map/reshape;reshape | solution.py:16
  191.7 65.6 %all_to_all.10 = bf16[64,144,128]{2,1,0:T(8,128)(2,1)} all-to-all(bf16[64,144,128]{2,1,0:T(8,128)(2,1)S(1)} %reshape_reshape.7), channel_id=1, replica_groups=mesh['expert'=64,'dp'=4] {'expert'}, dimensions={0} | all-to-all | bytes 4718592 | tf_op jit(solution)/shard_map/all_to_all | solution.py:17
  257.3 3.7 %reshape.44 = bf16[576,2048]{1,0:T(8,128)(2,1)S(1)} reshape(bf16[64,144,128]{2,1,0:T(8,128)(2,1)} %all_to_all.10) | data formatting | bytes 4718592 | tf_op jit(solution)/shard_map/reshape | solution.py:63
  260.9 0.0 reduce-scatter.3.cloned.1.call-done
  261.0 0.0 copy-start.1
  261.0 1.4 convolution_convert_fusion.4
  262.4 10.4 %reduce-scatter.5.cloned.1.call-done = bf16[512,1536]{1,0:T(8,128)(2,1)} async-done(((bf16[2048,1536]{1,0:T(8,128)(2,1)}), bf16[512,1536]{1,0:T(8,128)(2,1)}) %reduce-scatter.5.cloned.1.call-update) | async-done | bytes 1572880 | tf_op jit(solution)/shard_map/reduce_scatter | solution.py:58
  272.8 2.6 slice_bitcast_fusion
  (10 shorter events, 0.1 us)
Async XLA Ops:
  7.2 5.4 %copy-start = (bf16[128,2048]{1,0:T(8,128)(2,1)S(1)}, bf16[128,2048]{1,0:T(8,128)(2,1)}, u32[]{:S(2)}) copy-start(bf16[128,2048]{1,0:T(8,128)(2,1)} %param.7) | copy-start | bytes 1572868
  7.2 144.6 %all-gather.3.cloned.1.call-start = ((), (), s32[]{:S(2)}) async-start(), calls=%async_computation.4 | async-start | bytes 7864320 | tf_op jit(solution)/shard_map/all_gather | solution.py:41
  7.2 2.8 copy-start.4
  7.2 5.1 %copy-start.5 = (f32[128,4]{0,1:T(4,128)S(1)}, f32[128,4]{0,1:T(4,128)}, u32[]{:S(2)}) copy-start(f32[128,4]{0,1:T(4,128)} %param.10) | copy-start | bytes 6148
  10.0 3.3 %copy-start.3 = (bf16[128,2048]{1,0:T(8,128)(2,1)S(1)}, bf16[128,2048]{1,0:T(8,128)(2,1)}, u32[]{:S(2)}) copy-start(bf16[128,2048]{1,0:T(8,128)(2,1)} %param.8) | copy-start | bytes 1572868
  25.2 118.4 %all-to-all-start = ((bf16[64,288,128]{2,1,0:T(8,128)(2,1)}), bf16[64,288,128]{2,1,0:T(8,128)(2,1)}, u32[]{:S(2)}, u32[]{:S(2)}) async-start(bf16[64,288,128]{2,1,0:T(8,128)(2,1)} %reshape_reshape.6), calls=%async_computation | async-start | bytes 9437184 | tf_op jit(solution)/shard_map/all_to_all | solution.py:17
  38.4 126.5 %all-gather.5.cloned.1.call-start = ((), (), s32[]{:S(2)}) async-start(), calls=%async_computation.6 | async-start | bytes 3932160 | tf_op jit(solution)/shard_map/all_gather | solution.py:42
  39.2 221.8 %reduce-scatter.3.cloned.1.call-start = ((), (), s32[]{:S(2)}) async-start(), calls=%async_computation.5 | async-start | bytes 3932160 | tf_op jit(solution)/shard_map/reduce_scatter | solution.py:57
  151.8 8.6 %copy-start.2 = (bf16[576,4096]{1,0:T(8,128)(2,1)S(1)}, bf16[576,4096]{1,0:T(8,128)(2,1)}, u32[]{:S(2)}) copy-start(bf16[576,4096]{1,0:T(8,128)(2,1)} %reshape.43) | copy-start | bytes 14155780
  158.6 1.8 copy-start.6
  164.6 108.2 %reduce-scatter.5.cloned.1.call-start = ((), (), s32[]{:S(2)}) async-start(), calls=%async_computation.7 | async-start | bytes 7864320 | tf_op jit(solution)/shard_map/reduce_scatter | solution.py:58
  261.0 14.4 %copy-start.1 = (bf16[128,2048]{1,0:T(8,128)(2,1)S(1)}, bf16[128,2048]{1,0:T(8,128)(2,1)}, u32[]{:S(2)}) copy-start(bf16[128,2048]{1,0:T(8,128)(2,1)} %param.7) | copy-start | bytes 1572868
Sparse Core Ops, SparseCore 0:
  10.1 72.0 all-gather.2
  84.0 42.8 all-gather.4
  164.7 39.2 reduce-scatter.2
  206.5 66.2 reduce-scatter.4
